TPU v7x, 128 devices: a whole 4x4x4 slice. The times are simulated.
128 devices in a mesh: gz: 16 (over x, y), gy: 8 (over z, core).
Axes of the slice: x: 4, y: 4, z: 4, core: 2. Of those that a mesh axis runs over, the one named last changes fastest.
Arguments:
- applied_load: float32 [3, 128, 64, 512], P(None, 'gz', 'gy'), may hold values from -12 to 12
- start_field: float32 [3, 128, 64, 512], P(None, 'gz', 'gy'), may hold values from -2 to 2
- bone_mask: int32 [128, 64, 512], P('gz', 'gy'), may hold values 0 or 1
- element_stiffness: bfloat16 [24, 24], replicated, may hold values from -1.5 to 2, as said below
Outputs:
- corrected: float32 [3, 128, 64, 512], P(None, 'gz', 'gy')
Inputs may be any that keep to these rules, and one draw needn't show every extreme that they name: element_stiffness is symmetric and positive definite, and each of its diagonal entries is at least 0.125.
All inputs are finite; a program needn't handle non-finite values. No bound on the sum of `bone_mask` on one device may be relied on, other than what follows from the above.
Results may differ from a plain program's by a relative error of at most 0.0059.
Values may be sent and summed in bfloat16 or wider, within the bound.
No kernel may reach another device: no remote copies, remote signals or barrier semaphores. Data moves between devices by JAX's collectives and lax.ppermute only.
A program may use at most 64 MiB of HBM per device.

v0:
```python
import jax
import jax.numpy as jnp
from jax import lax
from jax.sharding import PartitionSpec as P
from jax.experimental import pallas as pl
from jax.experimental.pallas import tpu as pltpu

F32 = jnp.float32
BF16 = jnp.bfloat16
CHEB = 3
LOW = 0.1
MID = 0.5 * (1.0 + LOW)
HALF = 0.5 * (1.0 - LOW)
RATIO = (1.0 + LOW) / (1.0 - LOW)
ROWS = 16
BAND = 3 * ROWS
DEEP = 4


def iota(shape, dim):
    return lax.broadcasted_iota(jnp.int32, shape, dim)


def build_matrices(stiff):
    m = 4 * BAND
    row_m = iota((m, 24), 0)
    base_row = 12 * (row_m // (2 * BAND)) + 3 * ((row_m // BAND) % 2) + (row_m // ROWS) % 3
    col_e = iota((m, 24), 1)
    row_k = iota((24, m), 0)
    col_k = iota((24, m), 1)
    base_col = 6 * (col_k // (2 * BAND)) + 3 * ((col_k // BAND) % 2) + (col_k // ROWS) % 3
    mm = iota((m, m), 0)
    kk = iota((m, m), 1)
    gap = (mm % ROWS) - (kk % ROWS) + kk // (2 * BAND)
    blocks = []
    left = []
    for cy in range(2):
        pick = (col_e == base_row + 6 * cy).astype(BF16)
        left.append(jnp.dot(pick, stiff, preferred_element_type=F32).astype(BF16))
    for p in range(2):
        pick = (row_k == base_col + 12 * p).astype(BF16)
        block = jnp.zeros((m, m), F32)
        for cy in range(2):
            full = jnp.dot(left[cy], pick, preferred_element_type=F32)
            block = jnp.where(gap == cy, full, block)
        blocks.append(block.astype(BF16))
    md = iota((m, 2 * ROWS), 0)
    kd = iota((m, 2 * ROWS), 1)
    diag = jnp.zeros((m, 2 * ROWS), F32)
    for cy in range(2):
        own = jnp.sum(
            jnp.where(col_e == base_row + 6 * cy, left[cy].astype(F32), 0.0), axis=1, keepdims=True
        )
        diag = jnp.where((kd // ROWS == cy) & (kd % ROWS == md % ROWS), own, diag)
    return jnp.concatenate(blocks, axis=1), diag.astype(BF16)


def spectral_bound(stiff):
    wide = stiff.astype(F32)
    eye = iota((24, 24), 0) == iota((24, 24), 1)
    own = jnp.sum(jnp.where(eye, wide, 0.0), axis=1, keepdims=True)
    total = jnp.sum(jnp.abs(wide), axis=1, keepdims=True)
    return jnp.max(total / own, axis=0, keepdims=True)


def shift_up(values, width):
    rolled = pltpu.roll(values, width - 1, 1)
    return jnp.where(iota(values.shape, 1) == width - 1, 0.0, rolled)


def shift_down(values):
    rolled = pltpu.roll(values, 1, 1)
    return jnp.where(iota(values.shape, 1) == 0, 0.0, rolled)


def put_nodes(v_ref, z, values, width):
    v_ref[z, 0:BAND] = values.astype(BF16)
    v_ref[z, BAND : 2 * BAND] = shift_up(values, width).astype(BF16)


def put_scale(s_ref, layer, scale):
    s_ref[layer, 0:ROWS] = scale.astype(BF16)
    down = pltpu.roll(scale, 1, 0)
    down = jnp.where(iota(scale.shape, 0) == 0, 0.0, down)
    s_ref[layer, ROWS : 2 * ROWS] = down.astype(BF16)


def masked_nodes(v_ref, s_ref, layer, p, width):
    nodes = v_ref[layer + p].reshape(6, ROWS, width)
    parts = [
        (nodes * s_ref[layer, cy * ROWS : (cy + 1) * ROWS][None]).reshape(2 * BAND, width)
        for cy in range(2)
    ]
    return jnp.concatenate(parts, axis=0)


def layer_product(w_ref, v_ref, s_ref, layer, width):
    operand = jnp.concatenate(
        [masked_nodes(v_ref, s_ref, layer, p, width) for p in range(2)], axis=0
    )
    return jnp.dot(w_ref[...], operand, preferred_element_type=F32)


def gather_plane(first, carry_ref, width):
    both = first[0 : 2 * BAND] + carry_ref[...]
    return both[0:BAND] + shift_down(both[BAND : 2 * BAND])


def plane_loop(lo, hi, product, carry_ref, width, use):
    carry_ref[...] = product(lo - 1)[2 * BAND : 4 * BAND]

    def step(z, token):
        both = product(z)
        plane = gather_plane(both, carry_ref, width)
        carry_ref[...] = both[2 * BAND : 4 * BAND]
        use(z, plane)
        return token

    lax.fori_loop(lo, hi + 1, step, 0)


def invert_diagonal(
    lo, hi, wd_ref, s_ref, carry_ref, inv_ref, idle_ref, bound, width, past_z, past_y, first_z, first_y
):
    def product(layer):
        return jnp.dot(wd_ref[...], s_ref[layer], preferred_element_type=F32)

    rows = iota((BAND, width), 0) % ROWS
    keep_y = jnp.where((rows >= first_y) & (past_y == 1), 0.0, 1.0)

    def use(z, diag):
        idle = (diag == 0.0).astype(F32)
        keep_z = jnp.where((z >= first_z) & (past_z == 1), 0.0, 1.0)
        inv_ref[z] = keep_y * keep_z / ((diag + idle) * bound)
        idle_ref[z] = idle[0:ROWS]

    plane_loop(lo, hi, product, carry_ref, width, use)


def tile3(values):
    return jnp.concatenate([values, values, values], axis=0)


def sweep(lo, hi, refs, width, previous, current):
    w_ref, v_ref, s_ref, carry_ref, b_ref, x_ref, u_ref, inv_ref, idle_ref = refs

    def product(layer):
        return layer_product(w_ref, v_ref, s_ref, layer, width)

    def use(z, plane):
        x = x_ref[z]
        r = b_ref[z] - plane - tile3(idle_ref[z]) * x
        update = current * (inv_ref[z] * r)
        if previous is not None:
            update = previous * u_ref[z] + update
        x = x + update
        u_ref[z] = update
        x_ref[z] = x
        put_nodes(v_ref, z, x, width)

    plane_loop(lo, hi, product, carry_ref, width, use)


def chebyshev_factors():
    factors = []
    rho = 1.0 / RATIO
    for _ in range(CHEB - 1):
        nxt = 1.0 / (2.0 * RATIO - rho)
        factors.append((nxt * rho, 2.0 * nxt / HALF))
        rho = nxt
    return factors


def pack_z_kernel(place, x_ref, b_ref, m_ref, q0_ref, q1_ref):
    even = 1 - place[0]
    for out, up in ((q0_ref, even), (q1_ref, 1 - even)):
        for d in range(3):
            out[4 * d : 4 * d + 4] = x_ref[d, pl.ds(4 * up, 4)].astype(BF16)
            out[12 + 3 * d : 15 + 3 * d] = b_ref[d, pl.ds(5 * up, 3)].astype(BF16)
        out[21:25] = m_ref[pl.ds(4 * up, 4)].astype(F32).astype(BF16)


def z_planes(place, x_ref, b_ref, m_ref, r0_ref, r1_ref):
    odd = place[0] == 1

    def low(i):
        return jnp.where(odd, r0_ref[i].astype(F32), r1_ref[i].astype(F32))

    def high(i):
        return jnp.where(odd, r1_ref[i].astype(F32), r0_ref[i].astype(F32))

    def x_at(d, w):
        if w < 4:
            return low(4 * d + w)
        if w >= 12:
            return high(4 * d + w - 12)
        return x_ref[d, w - 4]

    def b_at(d, w):
        if w < 4:
            return low(12 + 3 * d + w - 1)
        if w >= 12:
            return high(12 + 3 * d + w - 12)
        return b_ref[d, w - 4]

    def m_at(w):
        if w < 4:
            return low(21 + w)
        if w >= 12:
            return high(21 + w - 12)
        return m_ref[w - 4].astype(F32)

    return x_at, b_at, m_at


def flip(values):
    return pltpu.roll(values, 4, 0)


def y_fields(x_at, b_at, m_at):
    fields = []
    for d in range(3):
        fields += [(x_at, (d,), w) for w in range(0, 16, 2)]
    for d in range(3):
        fields += [(b_at, (d,), w) for w in range(1, 15, 2)]
    fields += [(m_at, (), w) for w in range(0, 16, 2)]
    return fields


def pack_y_kernel(place, x_ref, b_ref, m_ref, r0_ref, r1_ref, q0_ref, q1_ref):
    even = place[1] == 0
    x_at, b_at, m_at = z_planes(place, x_ref, b_ref, m_ref, r0_ref, r1_ref)
    for index, (at, lead, w) in enumerate(y_fields(x_at, b_at, m_at)):
        a, b = at(*lead, w), at(*lead, w + 1)
        head = iota(a.shape, 0) < 4
        up = jnp.where(head, flip(a), b)
        down = jnp.where(head, a, flip(b))
        q0_ref[index] = jnp.where(even, up, down).astype(BF16)
        q1_ref[index] = jnp.where(even, down, up).astype(BF16)


def restrict_rows():
    out = iota((BAND, BAND), 0)
    src = iota((BAND, BAND), 1)
    gap = jnp.abs((src % ROWS) - 4 - 2 * ((out % ROWS) - 3))
    own = ((src % ROWS) >= 4) & ((src % ROWS) < 12) & (out // ROWS == src // ROWS)
    weight = jnp.where(gap == 0, 1.0, jnp.where(gap == 1, 0.5, 0.0))
    return jnp.where(own, weight, 0.0).astype(BF16)


def halve_rows():
    out = iota((ROWS, ROWS), 0)
    src = iota((ROWS, ROWS), 1)
    own = (src >= 4) & (src < 12) & ((src - 4) // 2 == out - 3)
    return own.astype(F32).astype(BF16)


def split(values):
    high = values.astype(BF16)
    return high, (values - high.astype(F32)).astype(BF16)


def fine_kernel(
    place, e_ref, x_in, b_in, m_in, r0_ref, r1_ref, y0_ref, y1_ref,
    out_ref, rhs_ref, sc_ref, q0_ref, q1_ref,
    w_ref, wd_ref, v_ref, s_ref, carry_ref, b_ref, x_ref, u_ref, inv_ref, idle_ref,
):
    width = x_in.shape[-1]
    stiff = e_ref[...]
    w_ref[...], wd_ref[...] = build_matrices(stiff)
    bound = spectral_bound(stiff)
    odd = place[1] == 1
    x_at, b_at, m_at = z_planes(place, x_in, b_in, m_in, r0_ref, r1_ref)
    head = iota((8, width), 0) < 4

    def windows(at, lead, w, index):
        low = jnp.where(odd, y0_ref[index].astype(F32), y1_ref[index].astype(F32))
        high = jnp.where(odd, y1_ref[index].astype(F32), y0_ref[index].astype(F32))
        both = []
        for k in range(2):
            own = flip(at(*lead, w + k))
            below = low if k == 0 else flip(low)
            above = flip(high) if k == 0 else high
            both.append(
                jnp.concatenate([jnp.where(head, below, own), jnp.where(head, own, above)], axis=0)
            )
        return both

    for index, (at, lead, w) in enumerate(y_fields(x_at, b_at, m_at)):
        for k, block in enumerate(windows(at, lead, w, index)):
            if at is m_at:
                put_scale(s_ref, w + k, block)
            elif at is b_at:
                b_ref[w + k, ROWS * lead[0] : ROWS * (lead[0] + 1)] = block
            else:
                x_ref[w + k, ROWS * lead[0] : ROWS * (lead[0] + 1)] = block

    def spread(z, token):
        put_nodes(v_ref, z, x_ref[z], width)
        return token

    lax.fori_loop(0, 16, spread, 0)
    invert_diagonal(
        1, 14, wd_ref, s_ref, carry_ref, inv_ref, idle_ref, bound, width, place[2], place[3], 12, 12
    )
    refs = (w_ref, v_ref, s_ref, carry_ref, b_ref, x_ref, u_ref, inv_ref, idle_ref)
    (p1, c1), (p2, c2) = chebyshev_factors()
    sweep(1, 14, refs, width, None, 1.0 / MID)
    sweep(2, 13, refs, width, p1, c1)
    sweep(3, 12, refs, width, p2, c2)

    def use(z, plane):
        u_ref[z] = b_ref[z] - plane - tile3(idle_ref[z]) * x_ref[z]

    plane_loop(
        4, 11, lambda layer: layer_product(w_ref, v_ref, s_ref, layer, width), carry_ref, width, use
    )
    for z in range(8):
        for d in range(3):
            a = x_ref[4 + z, ROWS * d : ROWS * d + 8]
            b = x_ref[4 + z, ROWS * d + 8 : ROWS * d + 16]
            out_ref[d, z] = flip(jnp.where(head, b, a))

    half = width // 2
    fine_x = iota((width, half), 0)
    coarse_x = iota((width, half), 1)
    gap = jnp.abs(fine_x - 2 * coarse_x)
    rx = jnp.where(gap == 0, 1.0, jnp.where(gap == 1, 0.5, 0.0)).astype(BF16)
    pair = (fine_x // 2 == coarse_x).astype(F32).astype(BF16)
    ry = restrict_rows()
    sums = []
    for k in range(5):
        total = 0.0
        if k > 0:
            total = 0.5 * u_ref[4 + 2 * k - 1]
        if k < 4:
            total = total + u_ref[4 + 2 * k] + 0.5 * u_ref[4 + 2 * k + 1]
        high, low = split(total)
        rows = jnp.dot(ry, high, preferred_element_type=F32) + jnp.dot(
            ry, low, preferred_element_type=F32
        )
        sums += [rows[ROWS * d : ROWS * d + 8] for d in range(3)]
    high, low = split(jnp.concatenate(sums, axis=0))
    rhs_ref[...] = (
        jnp.dot(high, rx, preferred_element_type=F32) + jnp.dot(low, rx, preferred_element_type=F32)
    ).reshape(15, 8, half)
    hy = halve_rows()
    counts = []
    for k in range(4):
        both = s_ref[4 + 2 * k, 0:ROWS] + s_ref[5 + 2 * k, 0:ROWS]
        counts.append(jnp.dot(hy, both, preferred_element_type=F32)[0:8])
    counts = jnp.concatenate(counts, axis=0).astype(BF16)
    sc_ref[...] = (0.25 * jnp.dot(counts, pair, preferred_element_type=F32)).reshape(4, 8, half)
    even = 1 - place[0]
    for out, up in ((q0_ref, even), (q1_ref, 1 - even)):
        out[0:9] = rhs_ref[pl.ds(6 * up, 9)].astype(BF16)
        out[9:12] = sc_ref[pl.ds(up, 3)].astype(BF16)


def pack_coarse_kernel(place, rhs_ref, sc_ref, r0_ref, r1_ref, full_ref, q_ref):
    odd = place[0] == 1

    def low(i):
        return jnp.where(odd, r0_ref[i].astype(F32), r1_ref[i].astype(F32))

    def high(i):
        return jnp.where(odd, r1_ref[i].astype(F32), r0_ref[i].astype(F32))

    for z in range(10):
        c = z - 3
        for d in range(4):
            value = jnp.zeros(rhs_ref.shape[1:], F32)
            if d < 3:
                if -2 <= c <= 0:
                    value = value + low(3 * (c + 2) + d)
                if 4 <= c <= 6:
                    value = value + high(3 * (c - 4) + d)
                if 0 <= c <= 4:
                    value = value + rhs_ref[3 * c + d]
            else:
                if c <= -1:
                    value = low(9 + c + 3)
                elif c >= 4:
                    value = high(9 + c - 4)
                else:
                    value = sc_ref[c]
            full_ref[4 * z + d] = value
            q_ref[4 * z + d] = value.astype(BF16)


def coarse_kernel(
    place, e_ref, full_ref, y0_ref, y1_ref, smooth_ref, out_ref,
    w_ref, wd_ref, v_ref, s_ref, carry_ref, b_ref, x_ref, u_ref, inv_ref, idle_ref,
):
    half = full_ref.shape[-1]
    width = 2 * half
    stiff = e_ref[...]
    w_ref[...], wd_ref[...] = build_matrices(stiff)
    bound = spectral_bound(stiff)
    odd = place[1] == 1
    rows8 = iota((8, half), 0)
    for z in range(10):
        for d in range(4):
            i = 4 * z + d
            low = jnp.where(odd, y0_ref[i].astype(F32), y1_ref[i].astype(F32))
            high = jnp.where(odd, y1_ref[i].astype(F32), y0_ref[i].astype(F32))
            low, high = flip(low), flip(high)
            first = (
                full_ref[i] + jnp.where(rows8 < 4, low, 0.0) + jnp.where(rows8 == 7, high, 0.0)
            )
            block = jnp.concatenate([first, jnp.where(rows8 < 4, high, 0.0)], axis=0)
            if d < 3:
                b_ref[z, ROWS * d : ROWS * (d + 1)] = block
            else:
                put_scale(s_ref, z, block)
    invert_diagonal(
        1, 9, wd_ref, s_ref, carry_ref, inv_ref, idle_ref, bound, half, place[2], place[3], 7, 7
    )

    def first_step(z, token):
        update = (1.0 / MID) * (inv_ref[z] * b_ref[z])
        u_ref[z] = update
        x_ref[z] = update
        put_nodes(v_ref, z, update, half)
        return token

    lax.fori_loop(1, 10, first_step, 0)
    refs = (w_ref, v_ref, s_ref, carry_ref, b_ref, x_ref, u_ref, inv_ref, idle_ref)
    (p1, c1), (p2, c2) = chebyshev_factors()
    sweep(2, 8, refs, half, p1, c1)
    sweep(3, 7, refs, half, p2, c2)

    coarse_x = iota((half, width), 0)
    fine_x = iota((half, width), 1)
    gap = jnp.abs(fine_x - 2 * coarse_x)
    px = jnp.where(gap == 0, 1.0, jnp.where(gap == 1, 0.5, 0.0)).astype(BF16)
    out_r = iota((24, BAND), 0)
    src_r = iota((24, BAND), 1)
    gap_y = jnp.abs((out_r % 8) - 2 * ((src_r % ROWS) - 3))
    py = jnp.where(gap_y == 0, 1.0, jnp.where(gap_y == 1, 0.5, 0.0))
    py = jnp.where(out_r // 8 == src_r // ROWS, py, 0.0).astype(BF16)
    for k in range(5):
        u_wide = jnp.dot(v_ref[3 + k, 0:BAND], px, preferred_element_type=F32)
        if k > 0:
            pieces = ((2 * k - 2, before), (2 * k - 1, 0.5 * (before + u_wide)))
            for z, plane in pieces:
                high, low = split(plane)
                fine = jnp.dot(py, high, preferred_element_type=F32) + jnp.dot(
                    py, low, preferred_element_type=F32
                )
                for d in range(3):
                    out_ref[d, z] = smooth_ref[d, z] + fine[8 * d : 8 * d + 8]
        before = u_wide


def swap(array, axis, offset):
    length = lax.axis_size(axis)
    pairs = []
    for i in range(offset, length - 1, 2):
        pairs += [(i, i + 1), (i + 1, i)]
    return lax.ppermute(array, axis, pairs)


def level_scratch(planes, width):
    return [
        pltpu.VMEM((4 * BAND, 8 * BAND), BF16),
        pltpu.VMEM((4 * BAND, 2 * ROWS), BF16),
        pltpu.VMEM((planes, 2 * BAND, width), BF16),
        pltpu.VMEM((planes, 2 * ROWS, width), BF16),
        pltpu.VMEM((2 * BAND, width), F32),
        pltpu.VMEM((planes, BAND, width), F32),
        pltpu.VMEM((planes, BAND, width), F32),
        pltpu.VMEM((planes, BAND, width), F32),
        pltpu.VMEM((planes, BAND, width), F32),
        pltpu.VMEM((planes, ROWS, width), F32),
    ]


def call(body, out_shape, n_in, scratch=(), name=None):
    vmem = pl.BlockSpec(memory_space=pltpu.VMEM)
    single = not isinstance(out_shape, (tuple, list))
    return pl.pallas_call(
        body,
        out_shape=out_shape,
        in_specs=[pl.BlockSpec(memory_space=pltpu.SMEM)] + [vmem] * n_in,
        out_specs=vmem if single else [vmem] * len(out_shape),
        scratch_shapes=list(scratch),
        compiler_params=pltpu.CompilerParams(vmem_limit_bytes=48 << 20),
        name=name,
    )


def body(applied_load, start_field, bone_mask, element_stiffness):
    width = applied_load.shape[-1]
    half = width // 2
    gz, gy = lax.axis_index("gz"), lax.axis_index("gy")
    place = jnp.stack(
        [
            gz % 2,
            gy % 2,
            (gz == lax.axis_size("gz") - 1).astype(jnp.int32),
            (gy == lax.axis_size("gy") - 1).astype(jnp.int32),
        ]
    ).astype(jnp.int32)
    shape = jax.ShapeDtypeStruct
    packet = shape((25, 8, width), BF16)
    q0, q1 = call(pack_z_kernel, [packet, packet], 3, name="pack_z")(
        place, start_field, applied_load, bone_mask
    )
    r1 = swap(q1, "gz", 1)
    r0 = swap(q0, "gz", 0)
    packet = shape((53, 8, width), BF16)
    q0, q1 = call(pack_y_kernel, [packet, packet], 5, name="pack_y")(
        place, start_field, applied_load, bone_mask, r0, r1
    )
    y1 = swap(q1, "gy", 1)
    y0 = swap(q0, "gy", 0)
    packet = shape((12, 8, half), BF16)
    smoothed, rhs, scale, q0, q1 = call(
        fine_kernel,
        [
            shape(start_field.shape, F32),
            shape((15, 8, half), F32),
            shape((4, 8, half), F32),
            packet,
            packet,
        ],
        8,
        level_scratch(16, width),
        name="fine",
    )(place, element_stiffness, start_field, applied_load, bone_mask, r0, r1, y0, y1)
    r1 = swap(q1, "gz", 1)
    r0 = swap(q0, "gz", 0)
    full, q = call(
        pack_coarse_kernel,
        [shape((40, 8, half), F32), shape((40, 8, half), BF16)],
        4,
        name="pack_coarse",
    )(place, rhs, scale, r0, r1)
    y1 = swap(q, "gy", 1)
    y0 = swap(q, "gy", 0)
    return call(
        coarse_kernel, shape(start_field.shape, F32), 5, level_scratch(11, half), name="coarse"
    )(place, element_stiffness, full, y0, y1, smoothed)


def solution(mesh):
    in_specs = (P(None, "gz", "gy", None), P(None, "gz", "gy", None), P("gz", "gy", None), P())
    out_specs = P(None, "gz", "gy", None)
    return jax.shard_map(body, mesh=mesh, in_specs=in_specs, out_specs=out_specs, check_vma=False)
```

profile of v0, /device:TPU:7, one launch (start us, length us, event | category | flops | bytes accessed | tf_op | source)
XLA Modules:
  0.0 78.1 jit_solution(14496070810875022033)
XLA Ops:
  0.0 0.1 pad_add_fusion.place
  0.1 0.0 copy-start
  0.1 1.0 %copy-done = f32[3,8,8,512]{3,2,1,0:T(8,128)S(1)} copy-done((f32[3,8,8,512]{3,2,1,0:T(8,128)S(1)}, f32[3,8,8,512]{3,2,1,0:T(8,128)}, u32[]{:S(2)}) %copy-start) | copy-done | bytes 393240
  1.1 0.0 copy-start.1
  1.1 1.0 %copy-done.1 = f32[3,8,8,512]{3,2,1,0:T(8,128)S(1)} copy-done((f32[3,8,8,512]{3,2,1,0:T(8,128)S(1)}, f32[3,8,8,512]{3,2,1,0:T(8,128)}, u32[]{:S(2)}) %copy-start.1) | copy-done | bytes 393240
  2.1 0.0 copy-start.2
  2.1 0.9 %copy-done.2 = s32[8,8,512]{2,1,0:T(8,128)S(1)} copy-done((s32[8,8,512]{2,1,0:T(8,128)S(1)}, s32[8,8,512]{2,1,0:T(8,128)}, u32[]{:S(2)}) %copy-start.2) | copy-done | bytes 131096
  3.0 0.6 pack_z.1
  3.6 1.4 %collective-permute-start = (bf16[25,8,512]{2,1,0:T(8,128)(2,1)S(1)}, bf16[25,8,512]{2,1,0:T(8,128)(2,1)S(1)}, u32[]{:S(2)}, u32[]{:S(2)}) collective-permute-start(bf16[25,8,512]{2,1,0:T(8,128)(2,1)S(1)} %get-tuple-element.16), channel_id=1, source_target_pairs={{0,8},{8,0},{16,24},{24,16},{32,40},{40,32},{48,56},{56,48},{64,72... | collective-permute-start | bytes 614408 | tf_op jit(solution)/shard_map/ppermute | solution.py:461
  4.9 4.1 %collective-permute-start.1 = (bf16[25,8,512]{2,1,0:T(8,128)(2,1)S(1)}, bf16[25,8,512]{2,1,0:T(8,128)(2,1)S(1)}, u32[]{:S(2)}, u32[]{:S(2)}) collective-permute-start(bf16[25,8,512]{2,1,0:T(8,128)(2,1)S(1)} %get-tuple-element.17), channel_id=1, source_target_pairs={{8,16},{16,8},{24,32},{32,24},{40,48},{48,40},{56,64},{64,56},{72,... | collective-permute-start | bytes 614408 | tf_op jit(solution)/shard_map/ppermute | solution.py:461
  9.0 0.6 collective-permute-done.r0_ref
  9.6 5.0 %collective-permute-done.1.r1_ref = bf16[25,8,512]{2,1,0:T(8,128)(2,1)S(1)} collective-permute-done((bf16[25,8,512]{2,1,0:T(8,128)(2,1)S(1)}, bf16[25,8,512]{2,1,0:T(8,128)(2,1)S(1)}, u32[]{:S(2)}, u32[]{:S(2)}) %collective-permute-start.1) | collective-permute-done | bytes 204832 | tf_op jit(solution)/shard_map/ppermute | solution.py:461
  14.6 0.0 copy-start.3
  14.6 0.8 %pack_y.1 = (bf16[53,8,512]{2,1,0:T(8,128)(2,1)S(1)}, bf16[53,8,512]{2,1,0:T(8,128)(2,1)S(1)}) custom-call(s32[4]{0:T(128)S(1)} %pad_add_fusion.place, f32[3,8,8,512]{3,2,1,0:T(8,128)S(1)} %copy-done, f32[3,8,8,512]{3,2,1,0:T(8,128)S(1)} %copy-done.1, s32[8,8,512]{2,1,0:T(8,128)S(1)} %copy-done.2, bf16[25,8,512]{2,1,0:T(8,128)(2,1)S(1)} %collective-permute-done.r0_ref, ...), custom_call_target="tpu_custom_call" | custom-call | tf_op jit(solution)/shard_map/pack_y/pallas_call | solution.py:513
  15.4 1.9 %collective-permute-start.2 = (bf16[53,8,512]{2,1,0:T(8,128)(2,1)S(1)}, bf16[53,8,512]{2,1,0:T(8,128)(2,1)S(1)}, u32[]{:S(2)}, u32[]{:S(2)}) collective-permute-start(bf16[53,8,512]{2,1,0:T(8,128)(2,1)S(1)} %get-tuple-element.18), channel_id=1, source_target_pairs={{0,1},{1,0},{2,3},{3,2},{4,5},{5,4},{6,7},{7,6},{8,9},{9,8},{10,11... | collective-permute-start | bytes 1302536 | tf_op jit(solution)/shard_map/ppermute | solution.py:461
  17.3 3.4 %collective-permute-start.3 = (bf16[53,8,512]{2,1,0:T(8,128)(2,1)S(1)}, bf16[53,8,512]{2,1,0:T(8,128)(2,1)S(1)}, u32[]{:S(2)}, u32[]{:S(2)}) collective-permute-start(bf16[53,8,512]{2,1,0:T(8,128)(2,1)S(1)} %get-tuple-element.19), channel_id=1, source_target_pairs={{1,2},{2,1},{3,4},{4,3},{5,6},{6,5},{9,10},{10,9},{11,12},{12,11},... | collective-permute-start | bytes 1302536 | tf_op jit(solution)/shard_map/ppermute | solution.py:461
  20.8 0.0 collective-permute-done.2.y0_ref
  20.8 6.1 %collective-permute-done.3.y1_ref = bf16[53,8,512]{2,1,0:T(8,128)(2,1)S(1)} collective-permute-done((bf16[53,8,512]{2,1,0:T(8,128)(2,1)S(1)}, bf16[53,8,512]{2,1,0:T(8,128)(2,1)S(1)}, u32[]{:S(2)}, u32[]{:S(2)}) %collective-permute-start.3) | collective-permute-done | bytes 434208 | tf_op jit(solution)/shard_map/ppermute | solution.py:461
  26.8 0.0 copy-done.3
  26.8 25.7 %fine.1 = (f32[3,8,8,512]{3,2,1,0:T(8,128)S(1)}, f32[15,8,256]{2,1,0:T(8,128)S(1)}, f32[4,8,256]{2,1,0:T(8,128)S(1)}, bf16[12,8,256]{2,1,0:T(8,128)(2,1)S(1)}, bf16[12,8,256]{2,1,0:T(8,128)(2,1)S(1)}) custom-call(s32[4]{0:T(128)S(1)} %pad_add_fusion.place, bf16[24,24]{1,0:T(8,128)(2,1)S(1)} %copy-done.3, f32[3,8,8,512]{3,2,1,0:T(8,128)S(1)} %copy-done, ...), custom_call_target="tpu_custom_call" | custom-call | tf_op jit(solution)/shard_map/fine/pallas_call | solution.py:519
  52.6 0.1 collective-permute-start.4
  52.7 4.1 %collective-permute-start.5 = (bf16[12,8,256]{2,1,0:T(8,128)(2,1)S(1)}, bf16[12,8,256]{2,1,0:T(8,128)(2,1)S(1)}, u32[]{:S(2)}, u32[]{:S(2)}) collective-permute-start(bf16[12,8,256]{2,1,0:T(8,128)(2,1)S(1)} %get-tuple-element.23), channel_id=1, source_target_pairs={{8,16},{16,8},{24,32},{32,24},{40,48},{48,40},{56,64},{64,56},{72,... | collective-permute-start | bytes 147464 | tf_op jit(solution)/shard_map/ppermute | solution.py:461
  56.8 0.0 collective-permute-done.4.r0_ref
  56.8 2.8 %collective-permute-done.5.r1_ref = bf16[12,8,256]{2,1,0:T(8,128)(2,1)S(1)} collective-permute-done((bf16[12,8,256]{2,1,0:T(8,128)(2,1)S(1)}, bf16[12,8,256]{2,1,0:T(8,128)(2,1)S(1)}, u32[]{:S(2)}, u32[]{:S(2)}) %collective-permute-start.5) | collective-permute-done | bytes 49184 | tf_op jit(solution)/shard_map/ppermute | solution.py:461
  59.6 0.6 pack_coarse.1
  60.2 4.7 %collective-permute-start.7 = (bf16[40,8,256]{2,1,0:T(8,128)(2,1)S(1)}, bf16[40,8,256]{2,1,0:T(8,128)(2,1)S(1)}, u32[]{:S(2)}, u32[]{:S(2)}) collective-permute-start(bf16[40,8,256]{2,1,0:T(8,128)(2,1)S(1)} %get-tuple-element.25), channel_id=1, source_target_pairs={{1,2},{2,1},{3,4},{4,3},{5,6},{6,5},{9,10},{10,9},{11,12},{12,11},... | collective-permute-start | bytes 491528 | tf_op jit(solution)/shard_map/ppermute | solution.py:461
  64.9 0.1 collective-permute-start.6
  65.0 2.9 %collective-permute-done.7.y1_ref = bf16[40,8,256]{2,1,0:T(8,128)(2,1)S(1)} collective-permute-done((bf16[40,8,256]{2,1,0:T(8,128)(2,1)S(1)}, bf16[40,8,256]{2,1,0:T(8,128)(2,1)S(1)}, u32[]{:S(2)}, u32[]{:S(2)}) %collective-permute-start.7) | collective-permute-done | bytes 163872 | tf_op jit(solution)/shard_map/ppermute | solution.py:461
  67.9 0.0 collective-permute-done.6.y0_ref
  67.9 10.3 %coarse.1 = f32[3,8,8,512]{3,2,1,0:T(8,128)} custom-call(s32[4]{0:T(128)S(1)} %pad_add_fusion.place, bf16[24,24]{1,0:T(8,128)(2,1)S(1)} %copy-done.3, f32[40,8,256]{2,1,0:T(8,128)S(1)} %get-tuple-element.24.full_ref, bf16[40,8,256]{2,1,0:T(8,128)(2,1)S(1)} %collective-permute-done.6.y0_ref, bf16[40,8,256]{2,1,0:T(8,128)(2,1)S(1)} %collective-permute-done.7.y1_ref, ...), custom_call_target="tpu_custom_call" | custom-call | tf_op jit(solution)/shard_map/coarse/pallas_call | solution.py:542
Async XLA Ops:
  0.1 1.0 %copy-start = (f32[3,8,8,512]{3,2,1,0:T(8,128)S(1)}, f32[3,8,8,512]{3,2,1,0:T(8,128)}, u32[]{:S(2)}) copy-start(f32[3,8,8,512]{3,2,1,0:T(8,128)} %x_in.1) | copy-start | bytes 1179652
  1.1 1.0 %copy-start.1 = (f32[3,8,8,512]{3,2,1,0:T(8,128)S(1)}, f32[3,8,8,512]{3,2,1,0:T(8,128)}, u32[]{:S(2)}) copy-start(f32[3,8,8,512]{3,2,1,0:T(8,128)} %b_in.1) | copy-start | bytes 1179652
  2.1 0.9 %copy-start.2 = (s32[8,8,512]{2,1,0:T(8,128)S(1)}, s32[8,8,512]{2,1,0:T(8,128)}, u32[]{:S(2)}) copy-start(s32[8,8,512]{2,1,0:T(8,128)} %m_in.1) | copy-start | bytes 393220
  3.6 6.0 %collective-permute-start = (bf16[25,8,512]{2,1,0:T(8,128)(2,1)S(1)}, bf16[25,8,512]{2,1,0:T(8,128)(2,1)S(1)}, u32[]{:S(2)}, u32[]{:S(2)}) collective-permute-start(bf16[25,8,512]{2,1,0:T(8,128)(2,1)S(1)} %get-tuple-element.16), channel_id=1, source_target_pairs={{0,8},{8,0},{16,24},{24,16},{32,40},{40,32},{48,56},{56,48},{64,72... | collective-permute-start | bytes 614408 | tf_op jit(solution)/shard_map/ppermute | solution.py:461
  4.9 9.6 %collective-permute-start.1 = (bf16[25,8,512]{2,1,0:T(8,128)(2,1)S(1)}, bf16[25,8,512]{2,1,0:T(8,128)(2,1)S(1)}, u32[]{:S(2)}, u32[]{:S(2)}) collective-permute-start(bf16[25,8,512]{2,1,0:T(8,128)(2,1)S(1)} %get-tuple-element.17), channel_id=1, source_target_pairs={{8,16},{16,8},{24,32},{32,24},{40,48},{48,40},{56,64},{64,56},{72,... | collective-permute-start | bytes 614408 | tf_op jit(solution)/shard_map/ppermute | solution.py:461
  14.6 12.3 %copy-start.3 = (bf16[24,24]{1,0:T(8,128)(2,1)S(1)}, bf16[24,24]{1,0:T(8,128)(2,1)}, u32[]{:S(2)}) copy-start(bf16[24,24]{1,0:T(8,128)(2,1)} %e_ref.3) | copy-start | bytes 3460
  15.4 5.4 %collective-permute-start.2 = (bf16[53,8,512]{2,1,0:T(8,128)(2,1)S(1)}, bf16[53,8,512]{2,1,0:T(8,128)(2,1)S(1)}, u32[]{:S(2)}, u32[]{:S(2)}) collective-permute-start(bf16[53,8,512]{2,1,0:T(8,128)(2,1)S(1)} %get-tuple-element.18), channel_id=1, source_target_pairs={{0,1},{1,0},{2,3},{3,2},{4,5},{5,4},{6,7},{7,6},{8,9},{9,8},{10,11... | collective-permute-start | bytes 1302536 | tf_op jit(solution)/shard_map/ppermute | solution.py:461
  17.3 9.5 %collective-permute-start.3 = (bf16[53,8,512]{2,1,0:T(8,128)(2,1)S(1)}, bf16[53,8,512]{2,1,0:T(8,128)(2,1)S(1)}, u32[]{:S(2)}, u32[]{:S(2)}) collective-permute-start(bf16[53,8,512]{2,1,0:T(8,128)(2,1)S(1)} %get-tuple-element.19), channel_id=1, source_target_pairs={{1,2},{2,1},{3,4},{4,3},{5,6},{6,5},{9,10},{10,9},{11,12},{12,11},... | collective-permute-start | bytes 1302536 | tf_op jit(solution)/shard_map/ppermute | solution.py:461
  52.6 4.2 %collective-permute-start.4 = (bf16[12,8,256]{2,1,0:T(8,128)(2,1)S(1)}, bf16[12,8,256]{2,1,0:T(8,128)(2,1)S(1)}, u32[]{:S(2)}, u32[]{:S(2)}) collective-permute-start(bf16[12,8,256]{2,1,0:T(8,128)(2,1)S(1)} %get-tuple-element.22), channel_id=1, source_target_pairs={{0,8},{8,0},{16,24},{24,16},{32,40},{40,32},{48,56},{56,48},{64,72... | collective-permute-start | bytes 147464 | tf_op jit(solution)/shard_map/ppermute | solution.py:461
  52.7 6.9 %collective-permute-start.5 = (bf16[12,8,256]{2,1,0:T(8,128)(2,1)S(1)}, bf16[12,8,256]{2,1,0:T(8,128)(2,1)S(1)}, u32[]{:S(2)}, u32[]{:S(2)}) collective-permute-start(bf16[12,8,256]{2,1,0:T(8,128)(2,1)S(1)} %get-tuple-element.23), channel_id=1, source_target_pairs={{8,16},{16,8},{24,32},{32,24},{40,48},{48,40},{56,64},{64,56},{72,... | collective-permute-start | bytes 147464 | tf_op jit(solution)/shard_map/ppermute | solution.py:461
  60.2 7.7 %collective-permute-start.7 = (bf16[40,8,256]{2,1,0:T(8,128)(2,1)S(1)}, bf16[40,8,256]{2,1,0:T(8,128)(2,1)S(1)}, u32[]{:S(2)}, u32[]{:S(2)}) collective-permute-start(bf16[40,8,256]{2,1,0:T(8,128)(2,1)S(1)} %get-tuple-element.25), channel_id=1, source_target_pairs={{1,2},{2,1},{3,4},{4,3},{5,6},{6,5},{9,10},{10,9},{11,12},{12,11},... | collective-permute-start | bytes 491528 | tf_op jit(solution)/shard_map/ppermute | solution.py:461
  64.9 3.0 %collective-permute-start.6 = (bf16[40,8,256]{2,1,0:T(8,128)(2,1)S(1)}, bf16[40,8,256]{2,1,0:T(8,128)(2,1)S(1)}, u32[]{:S(2)}, u32[]{:S(2)}) collective-permute-start(bf16[40,8,256]{2,1,0:T(8,128)(2,1)S(1)} %get-tuple-element.25), channel_id=1, source_target_pairs={{0,1},{1,0},{2,3},{3,2},{4,5},{5,4},{6,7},{7,6},{8,9},{9,8},{10,11... | collective-permute-start | bytes 491528 | tf_op jit(solution)/shard_map/ppermute | solution.py:461
where the time goes:
time: 78.4 us; the launch traced here: 78.1 us
  Pallas kernels  38 us (48%)
  starting transfers between devices  19.7 us (25%)
  waiting for transfers between devices  17.3 us (22%)
  local copies, waits for them, and re-layouts  2.9 us (4%)
    pallas_call x1, Pallas kernels, body(): call(fine_kernel, [shape(start_field.shape, F32), shape((15, 8, half), F3...  25.7 us
    ppermute x8, starting transfers between devices, swap(): return lax.ppermute(array, axis, pairs)  19.7 us
    ppermute x8, waiting for transfers between devices, swap(): return lax.ppermute(array, axis, pairs)  17.3 us
    pallas_call x1, Pallas kernels, body(): call(coarse_kernel, shape(start_field.shape, F32), 5, level_scratch(11, h...  10.3 us
    unnamed x8, local copies, waits for them, and re-layouts  2.9 us
  transfers between devices with their start and end apart: 8, of which 5 were waited for; matrix products, arithmetic and copies ran while one was open for 0% of the time, Pallas kernels for 0%

commit v1 on v0

--- a/solution.py
+++ b/solution.py
@@ -116,7 +116,7 @@
         use(z, plane)
         return token
 
-    lax.fori_loop(lo, hi + 1, step, 0)
+    lax.fori_loop(lo, hi + 1, step, 0, unroll=True)
 
 
 def invert_diagonal(
@@ -171,8 +171,23 @@
     return factors
 
 
-def pack_z_kernel(place, x_ref, b_ref, m_ref, q0_ref, q1_ref):
+def matrices_kernel(e_ref, token_ref, w_ref, wd_ref, bound_ref):
+    stiff = e_ref[...]
+    w_ref[...], wd_ref[...] = build_matrices(stiff)
+    bound_ref[...] = jnp.broadcast_to(spectral_bound(stiff), (8, 128))
+
+
+def pack_z_kernel(place, x_hbm, b_hbm, m_hbm, q0_ref, q1_ref, token_ref, x_ref, b_ref, m_ref, sem):
     even = 1 - place[0]
+    copies = [
+        pltpu.make_async_copy(src, dst, sem.at[i])
+        for i, (src, dst) in enumerate(((x_hbm, x_ref), (b_hbm, b_ref), (m_hbm, m_ref)))
+    ]
+    for copy in copies:
+        copy.start()
+    token_ref[...] = jnp.zeros(token_ref.shape, F32)
+    for copy in copies:
+        copy.wait()
     for out, up in ((q0_ref, even), (q1_ref, 1 - even)):
         for d in range(3):
             out[4 * d : 4 * d + 4] = x_ref[d, pl.ds(4 * up, 4)].astype(BF16)
@@ -261,14 +276,12 @@
 
 
 def fine_kernel(
-    place, e_ref, x_in, b_in, m_in, r0_ref, r1_ref, y0_ref, y1_ref,
+    place, w_ref, wd_ref, bound_ref, x_in, b_in, m_in, r0_ref, r1_ref, y0_ref, y1_ref,
     out_ref, rhs_ref, sc_ref, q0_ref, q1_ref,
-    w_ref, wd_ref, v_ref, s_ref, carry_ref, b_ref, x_ref, u_ref, inv_ref, idle_ref,
+    v_ref, s_ref, carry_ref, b_ref, x_ref, u_ref, inv_ref, idle_ref,
 ):
     width = x_in.shape[-1]
-    stiff = e_ref[...]
-    w_ref[...], wd_ref[...] = build_matrices(stiff)
-    bound = spectral_bound(stiff)
+    bound = bound_ref[0:1, 0:1]
     odd = place[1] == 1
     x_at, b_at, m_at = z_planes(place, x_in, b_in, m_in, r0_ref, r1_ref)
     head = iota((8, width), 0) < 4
@@ -299,7 +312,7 @@
         put_nodes(v_ref, z, x_ref[z], width)
         return token
 
-    lax.fori_loop(0, 16, spread, 0)
+    lax.fori_loop(0, 16, spread, 0, unroll=True)
     invert_diagonal(
         1, 14, wd_ref, s_ref, carry_ref, inv_ref, idle_ref, bound, width, place[2], place[3], 12, 12
     )
@@ -357,8 +370,11 @@
         out[9:12] = sc_ref[pl.ds(up, 3)].astype(BF16)
 
 
-def pack_coarse_kernel(place, rhs_ref, sc_ref, r0_ref, r1_ref, full_ref, q_ref):
+def pack_coarse_kernel(place, rhs_ref, sc_ref, r0_ref, r1_ref, full_ref, q0_ref, q1_ref):
     odd = place[0] == 1
+    even_y = place[1] == 0
+    head = iota(rhs_ref.shape[1:], 0) < 4
+    kept = []
 
     def low(i):
         return jnp.where(odd, r0_ref[i].astype(F32), r1_ref[i].astype(F32))
@@ -385,30 +401,36 @@
                 else:
                     value = sc_ref[c]
             full_ref[4 * z + d] = value
-            q_ref[4 * z + d] = value.astype(BF16)
+            kept.append(value)
+    for i in range(20):
+        a, b = kept[2 * i], kept[2 * i + 1]
+        up = jnp.where(head, flip(a), b)
+        down = jnp.where(head, pltpu.roll(a, 5, 0), pltpu.roll(b, 1, 0))
+        q0_ref[i] = jnp.where(even_y, up, down).astype(BF16)
+        q1_ref[i] = jnp.where(even_y, down, up).astype(BF16)
 
 
 def coarse_kernel(
-    place, e_ref, full_ref, y0_ref, y1_ref, smooth_ref, out_ref,
-    w_ref, wd_ref, v_ref, s_ref, carry_ref, b_ref, x_ref, u_ref, inv_ref, idle_ref,
+    place, w_ref, wd_ref, bound_ref, full_ref, y0_ref, y1_ref, smooth_ref, out_ref,
+    v_ref, s_ref, carry_ref, b_ref, x_ref, u_ref, inv_ref, idle_ref,
 ):
     half = full_ref.shape[-1]
     width = 2 * half
-    stiff = e_ref[...]
-    w_ref[...], wd_ref[...] = build_matrices(stiff)
-    bound = spectral_bound(stiff)
+    bound = bound_ref[0:1, 0:1]
     odd = place[1] == 1
     rows8 = iota((8, half), 0)
     for z in range(10):
         for d in range(4):
             i = 4 * z + d
-            low = jnp.where(odd, y0_ref[i].astype(F32), y1_ref[i].astype(F32))
-            high = jnp.where(odd, y1_ref[i].astype(F32), y0_ref[i].astype(F32))
-            low, high = flip(low), flip(high)
+            low = jnp.where(odd, y0_ref[i // 2].astype(F32), y1_ref[i // 2].astype(F32))
+            high = jnp.where(odd, y1_ref[i // 2].astype(F32), y0_ref[i // 2].astype(F32))
+            if i % 2:
+                low = flip(low)
+            high = pltpu.roll(high, 3 if i % 2 else 7, 0)
             first = (
                 full_ref[i] + jnp.where(rows8 < 4, low, 0.0) + jnp.where(rows8 == 7, high, 0.0)
             )
-            block = jnp.concatenate([first, jnp.where(rows8 < 4, high, 0.0)], axis=0)
+            block = jnp.concatenate([first, jnp.where(rows8 < 3, high, 0.0)], axis=0)
             if d < 3:
                 b_ref[z, ROWS * d : ROWS * (d + 1)] = block
             else:
@@ -424,7 +446,7 @@
         put_nodes(v_ref, z, update, half)
         return token
 
-    lax.fori_loop(1, 10, first_step, 0)
+    lax.fori_loop(1, 10, first_step, 0, unroll=True)
     refs = (w_ref, v_ref, s_ref, carry_ref, b_ref, x_ref, u_ref, inv_ref, idle_ref)
     (p1, c1), (p2, c2) = chebyshev_factors()
     sweep(2, 8, refs, half, p1, c1)
@@ -463,8 +485,6 @@
 
 def level_scratch(planes, width):
     return [
-        pltpu.VMEM((4 * BAND, 8 * BAND), BF16),
-        pltpu.VMEM((4 * BAND, 2 * ROWS), BF16),
         pltpu.VMEM((planes, 2 * BAND, width), BF16),
         pltpu.VMEM((planes, 2 * ROWS, width), BF16),
         pltpu.VMEM((2 * BAND, width), F32),
@@ -476,13 +496,14 @@
     ]
 
 
-def call(body, out_shape, n_in, scratch=(), name=None):
+def call(body, out_shape, n_in, scratch=(), name=None, place=True, space=pltpu.VMEM):
     vmem = pl.BlockSpec(memory_space=pltpu.VMEM)
     single = not isinstance(out_shape, (tuple, list))
+    lead = [pl.BlockSpec(memory_space=pltpu.SMEM)] if place else []
     return pl.pallas_call(
         body,
         out_shape=out_shape,
-        in_specs=[pl.BlockSpec(memory_space=pltpu.SMEM)] + [vmem] * n_in,
+        in_specs=lead + [pl.BlockSpec(memory_space=space)] * n_in,
         out_specs=vmem if single else [vmem] * len(out_shape),
         scratch_shapes=list(scratch),
         compiler_params=pltpu.CompilerParams(vmem_limit_bytes=48 << 20),
@@ -504,11 +525,32 @@
     ).astype(jnp.int32)
     shape = jax.ShapeDtypeStruct
     packet = shape((25, 8, width), BF16)
-    q0, q1 = call(pack_z_kernel, [packet, packet], 3, name="pack_z")(
-        place, start_field, applied_load, bone_mask
-    )
+    q0, q1, token = call(
+        pack_z_kernel,
+        [packet, packet, shape((8, 128), F32)],
+        3,
+        [
+            pltpu.VMEM(start_field.shape, F32),
+            pltpu.VMEM(applied_load.shape, F32),
+            pltpu.VMEM(bone_mask.shape, jnp.int32),
+            pltpu.SemaphoreType.DMA((3,)),
+        ],
+        name="pack_z",
+        space=pltpu.HBM,
+    )(place, *[pltpu.with_memory_space_constraint(a, pltpu.HBM) for a in (start_field, applied_load, bone_mask)])
     r1 = swap(q1, "gz", 1)
     r0 = swap(q0, "gz", 0)
+    matrices = call(
+        matrices_kernel,
+        [
+            shape((4 * BAND, 8 * BAND), BF16),
+            shape((4 * BAND, 2 * ROWS), BF16),
+            shape((8, 128), F32),
+        ],
+        2,
+        name="matrices",
+        place=False,
+    )(element_stiffness, token)
     packet = shape((53, 8, width), BF16)
     q0, q1 = call(pack_y_kernel, [packet, packet], 5, name="pack_y")(
         place, start_field, applied_load, bone_mask, r0, r1
@@ -525,23 +567,24 @@
             packet,
             packet,
         ],
-        8,
+        10,
         level_scratch(16, width),
         name="fine",
-    )(place, element_stiffness, start_field, applied_load, bone_mask, r0, r1, y0, y1)
+    )(place, *matrices, start_field, applied_load, bone_mask, r0, r1, y0, y1)
     r1 = swap(q1, "gz", 1)
     r0 = swap(q0, "gz", 0)
-    full, q = call(
+    packet = shape((20, 8, half), BF16)
+    full, q0, q1 = call(
         pack_coarse_kernel,
-        [shape((40, 8, half), F32), shape((40, 8, half), BF16)],
+        [shape((40, 8, half), F32), packet, packet],
         4,
         name="pack_coarse",
     )(place, rhs, scale, r0, r1)
-    y1 = swap(q, "gy", 1)
-    y0 = swap(q, "gy", 0)
+    y1 = swap(q1, "gy", 1)
+    y0 = swap(q0, "gy", 0)
     return call(
-        coarse_kernel, shape(start_field.shape, F32), 5, level_scratch(11, half), name="coarse"
-    )(place, element_stiffness, full, y0, y1, smoothed)
+        coarse_kernel, shape(start_field.shape, F32), 7, level_scratch(11, half), name="coarse"
+    )(place, *matrices, full, y0, y1, smoothed)
 
 
 def solution(mesh):

time: 78.4 us -> 52.1 us (0.66)
  Pallas kernels: 38 us -> 15.8 us
  local copies, waits for them, and re-layouts: 2.9 us -> 0.02 us
  waiting for transfers between devices: 17.3 us -> 16 us
    pallas_call x1, Pallas kernels: 25.7 us -> 8.06 us  [body(): call(fine_kernel, [shape(start_field.shape, F32), shape((15, 8, half), F3...]
    pallas_call x3 -> x4, Pallas kernels: 11.4 us -> 6.89 us  [the longest x1 4.02 us: body(): call(coarse_kernel, shape(start_field.shape, F32), 7, level_scratch(11, h...]
    unnamed x8, local copies, waits for them, and re-layouts: 2.9 us -> 0.02 us
    ppermute x8, waiting for transfers between devices: 17.3 us -> 16 us  [swap(): return lax.ppermute(array, axis, pairs)]
  transfers between devices with their start and end apart: 8 -> 8, of which waited for: 5 -> 5; matrix products, arithmetic and copies ran while one was open for 0% -> 0% of each run, Pallas kernels for 0% -> 1%
where the time goes in v1:
time: 52.1 us; the launch traced here: 51.8 us
  starting transfers between devices  19.7 us (38%)
  waiting for transfers between devices  16 us (31%)
  Pallas kernels  15.8 us (30%)
    ppermute x8, starting transfers between devices, swap(): return lax.ppermute(array, axis, pairs)  19.7 us
    ppermute x8, waiting for transfers between devices, swap(): return lax.ppermute(array, axis, pairs)  16 us
    pallas_call x1, Pallas kernels, body(): call(fine_kernel, [shape(start_field.shape, F32), shape((15, 8, half), F3...  8.06 us
    pallas_call x1, Pallas kernels, body(): call(coarse_kernel, shape(start_field.shape, F32), 7, level_scratch(11, h...  4.02 us
    pallas_call x1, Pallas kernels, body(): call(pack_z_kernel, [packet, packet, shape((8, 128), F32)], 3, [pltpu.VME...  1.75 us
  transfers between devices with their start and end apart: 8, of which 5 were waited for; matrix products, arithmetic and copies ran while one was open for 0% of the time, Pallas kernels for 1%

profile of v1, /device:TPU:7, one launch (start us, length us, event | category | flops | bytes accessed | tf_op | source)
XLA Modules:
  0.0 51.8 jit_solution(5234895029229307810)
XLA Ops:
  0.0 0.1 pad_add_fusion.place
  0.1 0.0 copy-start
  0.1 0.0 copy-start.1
  0.1 0.0 copy-start.2
  0.1 1.8 %pack_z.1 = (bf16[25,8,512]{2,1,0:T(8,128)(2,1)S(1)}, bf16[25,8,512]{2,1,0:T(8,128)(2,1)S(1)}, f32[8,128]{1,0:T(8,128)S(1)}) custom-call(s32[4]{0:T(128)S(1)} %pad_add_fusion.place, f32[3,8,8,512]{3,2,1,0:T(8,128)} %x_in.1, f32[3,8,8,512]{3,2,1,0:T(8,128)} %b_in.1, s32[8,8,512]{2,1,0:T(8,128)} %m_in.1), custom_call_target="tpu_custom_call" | custom-call | tf_op jit(solution)/shard_map/pack_z/pallas_call | solution.py:528
  1.8 1.4 %collective-permute-start = (bf16[25,8,512]{2,1,0:T(8,128)(2,1)S(1)}, bf16[25,8,512]{2,1,0:T(8,128)(2,1)S(1)}, u32[]{:S(2)}, u32[]{:S(2)}) collective-permute-start(bf16[25,8,512]{2,1,0:T(8,128)(2,1)S(1)} %get-tuple-element.25), channel_id=1, source_target_pairs={{0,8},{8,0},{16,24},{24,16},{32,40},{40,32},{48,56},{56,48},{64,72... | collective-permute-start | bytes 614408 | tf_op jit(solution)/shard_map/ppermute | solution.py:483
  3.2 4.1 %collective-permute-start.1 = (bf16[25,8,512]{2,1,0:T(8,128)(2,1)S(1)}, bf16[25,8,512]{2,1,0:T(8,128)(2,1)S(1)}, u32[]{:S(2)}, u32[]{:S(2)}) collective-permute-start(bf16[25,8,512]{2,1,0:T(8,128)(2,1)S(1)} %get-tuple-element.26), channel_id=1, source_target_pairs={{8,16},{16,8},{24,32},{32,24},{40,48},{48,40},{56,64},{64,56},{72,... | collective-permute-start | bytes 614408 | tf_op jit(solution)/shard_map/ppermute | solution.py:483
  7.3 0.6 %collective-permute-done.r0_ref = bf16[25,8,512]{2,1,0:T(8,128)(2,1)S(1)} collective-permute-done((bf16[25,8,512]{2,1,0:T(8,128)(2,1)S(1)}, bf16[25,8,512]{2,1,0:T(8,128)(2,1)S(1)}, u32[]{:S(2)}, u32[]{:S(2)}) %collective-permute-start) | collective-permute-done | bytes 204832 | tf_op jit(solution)/shard_map/ppermute | solution.py:483
  7.9 5.0 %collective-permute-done.1.r1_ref = bf16[25,8,512]{2,1,0:T(8,128)(2,1)S(1)} collective-permute-done((bf16[25,8,512]{2,1,0:T(8,128)(2,1)S(1)}, bf16[25,8,512]{2,1,0:T(8,128)(2,1)S(1)}, u32[]{:S(2)}, u32[]{:S(2)}) %collective-permute-start.1) | collective-permute-done | bytes 204832 | tf_op jit(solution)/shard_map/ppermute | solution.py:483
  12.8 0.0 copy-done
  12.8 0.0 copy-done.1
  12.8 0.0 copy-done.2
  12.8 0.0 copy-start.3
  12.9 0.8 %pack_y.1 = (bf16[53,8,512]{2,1,0:T(8,128)(2,1)S(1)}, bf16[53,8,512]{2,1,0:T(8,128)(2,1)S(1)}) custom-call(s32[4]{0:T(128)S(1)} %pad_add_fusion.place, f32[3,8,8,512]{3,2,1,0:T(8,128)S(1)} %copy-done, f32[3,8,8,512]{3,2,1,0:T(8,128)S(1)} %copy-done.1, s32[8,8,512]{2,1,0:T(8,128)S(1)} %copy-done.2, bf16[25,8,512]{2,1,0:T(8,128)(2,1)S(1)} %collective-permute-done.r0_ref, ...), custom_call_target="tpu_custom_call" | custom-call | tf_op jit(solution)/shard_map/pack_y/pallas_call | solution.py:555
  13.7 1.9 %collective-permute-start.2 = (bf16[53,8,512]{2,1,0:T(8,128)(2,1)S(1)}, bf16[53,8,512]{2,1,0:T(8,128)(2,1)S(1)}, u32[]{:S(2)}, u32[]{:S(2)}) collective-permute-start(bf16[53,8,512]{2,1,0:T(8,128)(2,1)S(1)} %get-tuple-element.27), channel_id=1, source_target_pairs={{0,1},{1,0},{2,3},{3,2},{4,5},{5,4},{6,7},{7,6},{8,9},{9,8},{10,11... | collective-permute-start | bytes 1302536 | tf_op jit(solution)/shard_map/ppermute | solution.py:483
  15.6 3.4 %collective-permute-start.3 = (bf16[53,8,512]{2,1,0:T(8,128)(2,1)S(1)}, bf16[53,8,512]{2,1,0:T(8,128)(2,1)S(1)}, u32[]{:S(2)}, u32[]{:S(2)}) collective-permute-start(bf16[53,8,512]{2,1,0:T(8,128)(2,1)S(1)} %get-tuple-element.28), channel_id=1, source_target_pairs={{1,2},{2,1},{3,4},{4,3},{5,6},{6,5},{9,10},{10,9},{11,12},{12,11},... | collective-permute-start | bytes 1302536 | tf_op jit(solution)/shard_map/ppermute | solution.py:483
  19.1 0.0 copy-done.3
  19.1 0.5 matrices.1
  19.6 0.0 collective-permute-done.2.y0_ref
  19.6 5.5 %collective-permute-done.3.y1_ref = bf16[53,8,512]{2,1,0:T(8,128)(2,1)S(1)} collective-permute-done((bf16[53,8,512]{2,1,0:T(8,128)(2,1)S(1)}, bf16[53,8,512]{2,1,0:T(8,128)(2,1)S(1)}, u32[]{:S(2)}, u32[]{:S(2)}) %collective-permute-start.3) | collective-permute-done | bytes 434208 | tf_op jit(solution)/shard_map/ppermute | solution.py:483
  25.1 8.1 %fine.1 = (f32[3,8,8,512]{3,2,1,0:T(8,128)S(1)}, f32[15,8,256]{2,1,0:T(8,128)S(1)}, f32[4,8,256]{2,1,0:T(8,128)S(1)}, bf16[12,8,256]{2,1,0:T(8,128)(2,1)S(1)}, bf16[12,8,256]{2,1,0:T(8,128)(2,1)S(1)}) custom-call(s32[4]{0:T(128)S(1)} %pad_add_fusion.place, bf16[192,384]{1,0:T(8,128)(2,1)S(1)} %get-tuple-element.22.w_ref, ...), custom_call_target="tpu_custom_call" | custom-call | tf_op jit(solution)/shard_map/fine/pallas_call | solution.py:561
  33.2 0.1 collective-permute-start.4
  33.3 4.1 %collective-permute-start.5 = (bf16[12,8,256]{2,1,0:T(8,128)(2,1)S(1)}, bf16[12,8,256]{2,1,0:T(8,128)(2,1)S(1)}, u32[]{:S(2)}, u32[]{:S(2)}) collective-permute-start(bf16[12,8,256]{2,1,0:T(8,128)(2,1)S(1)} %get-tuple-element.32), channel_id=1, source_target_pairs={{8,16},{16,8},{24,32},{32,24},{40,48},{48,40},{56,64},{64,56},{72,... | collective-permute-start | bytes 147464 | tf_op jit(solution)/shard_map/ppermute | solution.py:483
  37.4 0.0 collective-permute-done.4.r0_ref
  37.4 2.8 %collective-permute-done.5.r1_ref = bf16[12,8,256]{2,1,0:T(8,128)(2,1)S(1)} collective-permute-done((bf16[12,8,256]{2,1,0:T(8,128)(2,1)S(1)}, bf16[12,8,256]{2,1,0:T(8,128)(2,1)S(1)}, u32[]{:S(2)}, u32[]{:S(2)}) %collective-permute-start.5) | collective-permute-done | bytes 49184 | tf_op jit(solution)/shard_map/ppermute | solution.py:483
  40.2 0.6 %pack_coarse.1 = (f32[40,8,256]{2,1,0:T(8,128)S(1)}, bf16[20,8,256]{2,1,0:T(8,128)(2,1)S(1)}, bf16[20,8,256]{2,1,0:T(8,128)(2,1)S(1)}) custom-call(s32[4]{0:T(128)S(1)} %pad_add_fusion.place, f32[15,8,256]{2,1,0:T(8,128)S(1)} %get-tuple-element.29.rhs_ref, f32[4,8,256]{2,1,0:T(8,128)S(1)} %get-tuple-element.30.sc_ref, ...), custom_call_target="tpu_custom_call" | custom-call | tf_op jit(solution)/shard_map/pack_coarse/pallas_call | solution.py:577
  40.9 0.1 collective-permute-start.6
  41.0 4.7 %collective-permute-start.7 = (bf16[20,8,256]{2,1,0:T(8,128)(2,1)S(1)}, bf16[20,8,256]{2,1,0:T(8,128)(2,1)S(1)}, u32[]{:S(2)}, u32[]{:S(2)}) collective-permute-start(bf16[20,8,256]{2,1,0:T(8,128)(2,1)S(1)} %get-tuple-element.35), channel_id=1, source_target_pairs={{1,2},{2,1},{3,4},{4,3},{5,6},{6,5},{9,10},{10,9},{11,12},{12,11},... | collective-permute-start | bytes 245768 | tf_op jit(solution)/shard_map/ppermute | solution.py:483
  45.6 0.0 collective-permute-done.6.y0_ref
  45.6 2.1 %collective-permute-done.7.y1_ref = bf16[20,8,256]{2,1,0:T(8,128)(2,1)S(1)} collective-permute-done((bf16[20,8,256]{2,1,0:T(8,128)(2,1)S(1)}, bf16[20,8,256]{2,1,0:T(8,128)(2,1)S(1)}, u32[]{:S(2)}, u32[]{:S(2)}) %collective-permute-start.7) | collective-permute-done | bytes 81952 | tf_op jit(solution)/shard_map/ppermute | solution.py:483
  47.7 4.0 %coarse.1 = f32[3,8,8,512]{3,2,1,0:T(8,128)} custom-call(s32[4]{0:T(128)S(1)} %pad_add_fusion.place, bf16[192,384]{1,0:T(8,128)(2,1)S(1)} %get-tuple-element.22.w_ref, bf16[192,32]{1,0:T(8,128)(2,1)S(1)} %get-tuple-element.23.wd_ref, f32[8,128]{1,0:T(8,128)S(1)} %get-tuple-element.24.bound_ref, f32[40,8,256]{2,1,0:T(8,128)S(1)} %get-tuple-element.33.full_ref, ...), custom_call_target="tpu_custom_call" | custom-call | tf_op jit(solution)/shard_map/coarse/pallas_call | solution.py:585
Async XLA Ops:
  0.1 12.8 %copy-start = (f32[3,8,8,512]{3,2,1,0:T(8,128)S(1)}, f32[3,8,8,512]{3,2,1,0:T(8,128)}, u32[]{:S(2)}) copy-start(f32[3,8,8,512]{3,2,1,0:T(8,128)} %x_in.1) | copy-start | bytes 1179652
  0.1 12.8 %copy-start.1 = (f32[3,8,8,512]{3,2,1,0:T(8,128)S(1)}, f32[3,8,8,512]{3,2,1,0:T(8,128)}, u32[]{:S(2)}) copy-start(f32[3,8,8,512]{3,2,1,0:T(8,128)} %b_in.1) | copy-start | bytes 1179652
  0.1 12.8 %copy-start.2 = (s32[8,8,512]{2,1,0:T(8,128)S(1)}, s32[8,8,512]{2,1,0:T(8,128)}, u32[]{:S(2)}) copy-start(s32[8,8,512]{2,1,0:T(8,128)} %m_in.1) | copy-start | bytes 393220
  1.8 6.0 %collective-permute-start = (bf16[25,8,512]{2,1,0:T(8,128)(2,1)S(1)}, bf16[25,8,512]{2,1,0:T(8,128)(2,1)S(1)}, u32[]{:S(2)}, u32[]{:S(2)}) collective-permute-start(bf16[25,8,512]{2,1,0:T(8,128)(2,1)S(1)} %get-tuple-element.25), channel_id=1, source_target_pairs={{0,8},{8,0},{16,24},{24,16},{32,40},{40,32},{48,56},{56,48},{64,72... | collective-permute-start | bytes 614408 | tf_op jit(solution)/shard_map/ppermute | solution.py:483
  3.2 9.6 %collective-permute-start.1 = (bf16[25,8,512]{2,1,0:T(8,128)(2,1)S(1)}, bf16[25,8,512]{2,1,0:T(8,128)(2,1)S(1)}, u32[]{:S(2)}, u32[]{:S(2)}) collective-permute-start(bf16[25,8,512]{2,1,0:T(8,128)(2,1)S(1)} %get-tuple-element.26), channel_id=1, source_target_pairs={{8,16},{16,8},{24,32},{32,24},{40,48},{48,40},{56,64},{64,56},{72,... | collective-permute-start | bytes 614408 | tf_op jit(solution)/shard_map/ppermute | solution.py:483
  12.8 6.2 %copy-start.3 = (bf16[24,24]{1,0:T(8,128)(2,1)S(1)}, bf16[24,24]{1,0:T(8,128)(2,1)}, u32[]{:S(2)}) copy-start(bf16[24,24]{1,0:T(8,128)(2,1)} %e_ref.1) | copy-start | bytes 3460
  13.7 5.9 %collective-permute-start.2 = (bf16[53,8,512]{2,1,0:T(8,128)(2,1)S(1)}, bf16[53,8,512]{2,1,0:T(8,128)(2,1)S(1)}, u32[]{:S(2)}, u32[]{:S(2)}) collective-permute-start(bf16[53,8,512]{2,1,0:T(8,128)(2,1)S(1)} %get-tuple-element.27), channel_id=1, source_target_pairs={{0,1},{1,0},{2,3},{3,2},{4,5},{5,4},{6,7},{7,6},{8,9},{9,8},{10,11... | collective-permute-start | bytes 1302536 | tf_op jit(solution)/shard_map/ppermute | solution.py:483
  15.6 9.5 %collective-permute-start.3 = (bf16[53,8,512]{2,1,0:T(8,128)(2,1)S(1)}, bf16[53,8,512]{2,1,0:T(8,128)(2,1)S(1)}, u32[]{:S(2)}, u32[]{:S(2)}) collective-permute-start(bf16[53,8,512]{2,1,0:T(8,128)(2,1)S(1)} %get-tuple-element.28), channel_id=1, source_target_pairs={{1,2},{2,1},{3,4},{4,3},{5,6},{6,5},{9,10},{10,9},{11,12},{12,11},... | collective-permute-start | bytes 1302536 | tf_op jit(solution)/shard_map/ppermute | solution.py:483
  33.2 4.2 %collective-permute-start.4 = (bf16[12,8,256]{2,1,0:T(8,128)(2,1)S(1)}, bf16[12,8,256]{2,1,0:T(8,128)(2,1)S(1)}, u32[]{:S(2)}, u32[]{:S(2)}) collective-permute-start(bf16[12,8,256]{2,1,0:T(8,128)(2,1)S(1)} %get-tuple-element.31), channel_id=1, source_target_pairs={{0,8},{8,0},{16,24},{24,16},{32,40},{40,32},{48,56},{56,48},{64,72... | collective-permute-start | bytes 147464 | tf_op jit(solution)/shard_map/ppermute | solution.py:483
  33.3 6.9 %collective-permute-start.5 = (bf16[12,8,256]{2,1,0:T(8,128)(2,1)S(1)}, bf16[12,8,256]{2,1,0:T(8,128)(2,1)S(1)}, u32[]{:S(2)}, u32[]{:S(2)}) collective-permute-start(bf16[12,8,256]{2,1,0:T(8,128)(2,1)S(1)} %get-tuple-element.32), channel_id=1, source_target_pairs={{8,16},{16,8},{24,32},{32,24},{40,48},{48,40},{56,64},{64,56},{72,... | collective-permute-start | bytes 147464 | tf_op jit(solution)/shard_map/ppermute | solution.py:483
  40.9 4.8 %collective-permute-start.6 = (bf16[20,8,256]{2,1,0:T(8,128)(2,1)S(1)}, bf16[20,8,256]{2,1,0:T(8,128)(2,1)S(1)}, u32[]{:S(2)}, u32[]{:S(2)}) collective-permute-start(bf16[20,8,256]{2,1,0:T(8,128)(2,1)S(1)} %get-tuple-element.34), channel_id=1, source_target_pairs={{0,1},{1,0},{2,3},{3,2},{4,5},{5,4},{6,7},{7,6},{8,9},{9,8},{10,11... | collective-permute-start | bytes 245768 | tf_op jit(solution)/shard_map/ppermute | solution.py:483
  41.0 6.8 %collective-permute-start.7 = (bf16[20,8,256]{2,1,0:T(8,128)(2,1)S(1)}, bf16[20,8,256]{2,1,0:T(8,128)(2,1)S(1)}, u32[]{:S(2)}, u32[]{:S(2)}) collective-permute-start(bf16[20,8,256]{2,1,0:T(8,128)(2,1)S(1)} %get-tuple-element.35), channel_id=1, source_target_pairs={{1,2},{2,1},{3,4},{4,3},{5,6},{6,5},{9,10},{10,9},{11,12},{12,11},... | collective-permute-start | bytes 245768 | tf_op jit(solution)/shard_map/ppermute | solution.py:483

commit v2 on v1

--- a/solution.py
+++ b/solution.py
@@ -171,18 +171,60 @@
     return factors
 
 
-def matrices_kernel(e_ref, token_ref, w_ref, wd_ref, bound_ref):
+def weights(gap, where):
+    value = jnp.where(gap == 0, 1.0, jnp.where(gap == 1, 0.5, 0.0))
+    return jnp.where(where, value, 0.0)
+
+
+def own_rows(w_ref):
+    groups = [w_ref[ROWS * g : ROWS * (g + 1)].astype(F32)[4:12] for g in range(12)]
+    return jnp.concatenate(groups, axis=0).astype(BF16)
+
+
+def restrict_planes():
+    out, src = iota((120, 192), 0), iota((120, 192), 1)
+    gap_z = jnp.abs(src // 24 - 2 * (out // 24))
+    gap_y = jnp.abs(src % 8 - 2 * (out % 8 - 3))
+    same = (src // 8) % 3 == (out // 8) % 3
+    return (weights(gap_z, same) * weights(gap_y, same)).astype(BF16)
+
+
+def halve_planes():
+    out, src = iota((32, 64), 0), iota((32, 64), 1)
+    same = (src // 16 == out // 8) & ((src % 8) // 2 == out % 8 - 3)
+    return same.astype(F32).astype(BF16)
+
+
+def prolong_rows():
+    out, src = iota((120, 240), 0), iota((120, 240), 1)
+    gap = jnp.abs(out % 8 - 2 * (src % ROWS - 3))
+    same = (out // 24 == src // BAND) & ((out // 8) % 3 == (src // ROWS) % 3)
+    return weights(gap, same).astype(BF16)
+
+
+def matrices_kernel(
+    e_ref, token_ref, w_ref, wd_ref, bound_ref, wr_ref, rzy_ref, hzy_ref, py_ref, rx_ref, px_ref, pair_ref
+):
     stiff = e_ref[...]
     w_ref[...], wd_ref[...] = build_matrices(stiff)
     bound_ref[...] = jnp.broadcast_to(spectral_bound(stiff), (8, 128))
+    wr_ref[...] = own_rows(w_ref)
+    rzy_ref[...] = restrict_planes()
+    hzy_ref[...] = halve_planes()
+    py_ref[...] = prolong_rows()
+    fine, coarse = iota(rx_ref.shape, 0), iota(rx_ref.shape, 1)
+    rx_ref[...] = weights(jnp.abs(fine - 2 * coarse), fine >= 0).astype(BF16)
+    pair_ref[...] = (fine // 2 == coarse).astype(F32).astype(BF16)
+    coarse, fine = iota(px_ref.shape, 0), iota(px_ref.shape, 1)
+    px_ref[...] = weights(jnp.abs(fine - 2 * coarse), fine >= 0).astype(BF16)
 
 
 def pack_z_kernel(place, x_hbm, b_hbm, m_hbm, q0_ref, q1_ref, token_ref, x_ref, b_ref, m_ref, sem):
     even = 1 - place[0]
-    copies = [
-        pltpu.make_async_copy(src, dst, sem.at[i])
-        for i, (src, dst) in enumerate(((x_hbm, x_ref), (b_hbm, b_ref), (m_hbm, m_ref)))
-    ]
+    pairs = [(m_hbm, m_ref)]
+    for d in range(3):
+        pairs += [(x_hbm.at[d], x_ref.at[d]), (b_hbm.at[d], b_ref.at[d])]
+    copies = [pltpu.make_async_copy(src, dst, sem.at[i]) for i, (src, dst) in enumerate(pairs)]
     for copy in copies:
         copy.start()
     token_ref[...] = jnp.zeros(token_ref.shape, F32)
@@ -232,20 +274,18 @@
     return pltpu.roll(values, 4, 0)
 
 
-def y_fields(x_at, b_at, m_at):
-    fields = []
-    for d in range(3):
-        fields += [(x_at, (d,), w) for w in range(0, 16, 2)]
-    for d in range(3):
-        fields += [(b_at, (d,), w) for w in range(1, 15, 2)]
-    fields += [(m_at, (), w) for w in range(0, 16, 2)]
-    return fields
-
-
-def pack_y_kernel(place, x_ref, b_ref, m_ref, r0_ref, r1_ref, q0_ref, q1_ref):
+def node_fields(x_at, m_at):
+    fields = [(x_at, (d,), w) for d in range(3) for w in range(0, 16, 2)]
+    return fields + [(m_at, (), w) for w in range(0, 16, 2)]
+
+
+def load_fields(b_at):
+    return [(b_at, (d,), w) for d in range(3) for w in range(1, 15, 2)]
+
+
+def pack_rows(place, fields, q0_ref, q1_ref):
     even = place[1] == 0
-    x_at, b_at, m_at = z_planes(place, x_ref, b_ref, m_ref, r0_ref, r1_ref)
-    for index, (at, lead, w) in enumerate(y_fields(x_at, b_at, m_at)):
+    for index, (at, lead, w) in enumerate(fields):
         a, b = at(*lead, w), at(*lead, w + 1)
         head = iota(a.shape, 0) < 4
         up = jnp.where(head, flip(a), b)
@@ -254,36 +294,18 @@
         q1_ref[index] = jnp.where(even, down, up).astype(BF16)
 
 
-def restrict_rows():
-    out = iota((BAND, BAND), 0)
-    src = iota((BAND, BAND), 1)
-    gap = jnp.abs((src % ROWS) - 4 - 2 * ((out % ROWS) - 3))
-    own = ((src % ROWS) >= 4) & ((src % ROWS) < 12) & (out // ROWS == src // ROWS)
-    weight = jnp.where(gap == 0, 1.0, jnp.where(gap == 1, 0.5, 0.0))
-    return jnp.where(own, weight, 0.0).astype(BF16)
-
-
-def halve_rows():
-    out = iota((ROWS, ROWS), 0)
-    src = iota((ROWS, ROWS), 1)
-    own = (src >= 4) & (src < 12) & ((src - 4) // 2 == out - 3)
-    return own.astype(F32).astype(BF16)
-
-
-def split(values):
-    high = values.astype(BF16)
-    return high, (values - high.astype(F32)).astype(BF16)
-
-
-def fine_kernel(
-    place, w_ref, wd_ref, bound_ref, x_in, b_in, m_in, r0_ref, r1_ref, y0_ref, y1_ref,
-    out_ref, rhs_ref, sc_ref, q0_ref, q1_ref,
-    v_ref, s_ref, carry_ref, b_ref, x_ref, u_ref, inv_ref, idle_ref,
-):
-    width = x_in.shape[-1]
-    bound = bound_ref[0:1, 0:1]
+def pack_nodes_kernel(place, after_ref, x_ref, m_ref, r0_ref, r1_ref, q0_ref, q1_ref):
+    x_at, _, m_at = z_planes(place, x_ref, None, m_ref, r0_ref, r1_ref)
+    pack_rows(place, node_fields(x_at, m_at), q0_ref, q1_ref)
+
+
+def pack_load_kernel(place, b_ref, r0_ref, r1_ref, q0_ref, q1_ref):
+    _, b_at, _ = z_planes(place, None, b_ref, None, r0_ref, r1_ref)
+    pack_rows(place, load_fields(b_at), q0_ref, q1_ref)
+
+
+def window_maker(place, y0_ref, y1_ref, width):
     odd = place[1] == 1
-    x_at, b_at, m_at = z_planes(place, x_in, b_in, m_in, r0_ref, r1_ref)
     head = iota((8, width), 0) < 4
 
     def windows(at, lead, w, index):
@@ -299,71 +321,98 @@
             )
         return both
 
-    for index, (at, lead, w) in enumerate(y_fields(x_at, b_at, m_at)):
+    return windows
+
+
+def split(values):
+    high = values.astype(BF16)
+    return high, (values - high.astype(F32)).astype(BF16)
+
+
+def fine_start_kernel(
+    place, w_ref, wd_ref, bound_ref, hzy_ref, pair_ref, x_in, m_in, r0_ref, r1_ref, y0_ref, y1_ref,
+    x_ref, s_ref, inv_ref, idle_ref, first_ref, sc_ref,
+    v_ref, carry_ref,
+):
+    width = x_in.shape[-1]
+    x_at, _, m_at = z_planes(place, x_in, None, m_in, r0_ref, r1_ref)
+    windows = window_maker(place, y0_ref, y1_ref, width)
+    for index, (at, lead, w) in enumerate(node_fields(x_at, m_at)):
         for k, block in enumerate(windows(at, lead, w, index)):
             if at is m_at:
                 put_scale(s_ref, w + k, block)
-            elif at is b_at:
-                b_ref[w + k, ROWS * lead[0] : ROWS * (lead[0] + 1)] = block
             else:
                 x_ref[w + k, ROWS * lead[0] : ROWS * (lead[0] + 1)] = block
-
-    def spread(z, token):
+    for z in range(16):
         put_nodes(v_ref, z, x_ref[z], width)
-        return token
-
-    lax.fori_loop(0, 16, spread, 0, unroll=True)
     invert_diagonal(
-        1, 14, wd_ref, s_ref, carry_ref, inv_ref, idle_ref, bound, width, place[2], place[3], 12, 12
-    )
+        1, 14, wd_ref, s_ref, carry_ref, inv_ref, idle_ref, bound_ref[0:1, 0:1], width,
+        place[2], place[3], 12, 12,
+    )
+
+    def use(z, plane):
+        first_ref[z] = plane + tile3(idle_ref[z]) * x_ref[z]
+
+    plane_loop(
+        1, 14, lambda layer: layer_product(w_ref, v_ref, s_ref, layer, width), carry_ref, width, use
+    )
+    counts = jnp.dot(
+        hzy_ref[...], m_in[...].astype(F32).astype(BF16).reshape(64, width), preferred_element_type=F32
+    )
+    counts = jnp.dot(counts.astype(BF16), pair_ref[...], preferred_element_type=F32)
+    sc_ref[...] = (0.25 * counts).reshape(sc_ref.shape)
+
+
+def own_part(ref, z, d, head):
+    a = ref[z, ROWS * d : ROWS * d + 8]
+    b = ref[z, ROWS * d + 8 : ROWS * d + 16]
+    return flip(jnp.where(head, b, a))
+
+
+def fine_kernel(
+    place, w_ref, wr_ref, rzy_ref, rx_ref, x0_ref, s_ref, inv_ref, idle_ref, first_ref, sc_ref,
+    b_in, r0_ref, r1_ref, y0_ref, y1_ref,
+    out_ref, rhs_ref, q0_ref, q1_ref,
+    v_ref, carry_ref, b_ref, x_ref, u_ref,
+):
+    width = b_in.shape[-1]
+    _, b_at, _ = z_planes(place, None, b_in, None, r0_ref, r1_ref)
+    windows = window_maker(place, y0_ref, y1_ref, width)
+    for index, (at, lead, w) in enumerate(load_fields(b_at)):
+        for k, block in enumerate(windows(at, lead, w, index)):
+            b_ref[w + k, ROWS * lead[0] : ROWS * (lead[0] + 1)] = block
+    for z in range(1, 15):
+        update = (1.0 / MID) * (inv_ref[z] * (b_ref[z] - first_ref[z]))
+        x = x0_ref[z] + update
+        u_ref[z] = update
+        x_ref[z] = x
+        put_nodes(v_ref, z, x, width)
     refs = (w_ref, v_ref, s_ref, carry_ref, b_ref, x_ref, u_ref, inv_ref, idle_ref)
     (p1, c1), (p2, c2) = chebyshev_factors()
-    sweep(1, 14, refs, width, None, 1.0 / MID)
     sweep(2, 13, refs, width, p1, c1)
     sweep(3, 12, refs, width, p2, c2)
 
-    def use(z, plane):
-        u_ref[z] = b_ref[z] - plane - tile3(idle_ref[z]) * x_ref[z]
-
-    plane_loop(
-        4, 11, lambda layer: layer_product(w_ref, v_ref, s_ref, layer, width), carry_ref, width, use
-    )
+    head = iota((8, width), 0) < 4
+
+    def product(layer):
+        return layer_product(wr_ref, v_ref, s_ref, layer, width)
+
+    carry = product(3)[48:96]
+    parts = []
     for z in range(8):
+        both = product(4 + z)
+        plane = both[0:48] + carry
+        plane = plane[0:24] + shift_down(plane[24:48])
+        carry = both[48:96]
+        idle = own_part(idle_ref, 4 + z, 0, head)
         for d in range(3):
-            a = x_ref[4 + z, ROWS * d : ROWS * d + 8]
-            b = x_ref[4 + z, ROWS * d + 8 : ROWS * d + 16]
-            out_ref[d, z] = flip(jnp.where(head, b, a))
-
-    half = width // 2
-    fine_x = iota((width, half), 0)
-    coarse_x = iota((width, half), 1)
-    gap = jnp.abs(fine_x - 2 * coarse_x)
-    rx = jnp.where(gap == 0, 1.0, jnp.where(gap == 1, 0.5, 0.0)).astype(BF16)
-    pair = (fine_x // 2 == coarse_x).astype(F32).astype(BF16)
-    ry = restrict_rows()
-    sums = []
-    for k in range(5):
-        total = 0.0
-        if k > 0:
-            total = 0.5 * u_ref[4 + 2 * k - 1]
-        if k < 4:
-            total = total + u_ref[4 + 2 * k] + 0.5 * u_ref[4 + 2 * k + 1]
-        high, low = split(total)
-        rows = jnp.dot(ry, high, preferred_element_type=F32) + jnp.dot(
-            ry, low, preferred_element_type=F32
-        )
-        sums += [rows[ROWS * d : ROWS * d + 8] for d in range(3)]
-    high, low = split(jnp.concatenate(sums, axis=0))
-    rhs_ref[...] = (
-        jnp.dot(high, rx, preferred_element_type=F32) + jnp.dot(low, rx, preferred_element_type=F32)
-    ).reshape(15, 8, half)
-    hy = halve_rows()
-    counts = []
-    for k in range(4):
-        both = s_ref[4 + 2 * k, 0:ROWS] + s_ref[5 + 2 * k, 0:ROWS]
-        counts.append(jnp.dot(hy, both, preferred_element_type=F32)[0:8])
-    counts = jnp.concatenate(counts, axis=0).astype(BF16)
-    sc_ref[...] = (0.25 * jnp.dot(counts, pair, preferred_element_type=F32)).reshape(4, 8, half)
+            x = own_part(x_ref, 4 + z, d, head)
+            out_ref[d, z] = x
+            parts.append(b_in[d, z] - plane[8 * d : 8 * d + 8] - idle * x)
+    residual = jnp.concatenate(parts, axis=0).astype(BF16)
+    sums = jnp.dot(rzy_ref[...], residual, preferred_element_type=F32)
+    sums = jnp.dot(sums.astype(BF16), rx_ref[...], preferred_element_type=F32)
+    rhs_ref[...] = sums.reshape(rhs_ref.shape)
     even = 1 - place[0]
     for out, up in ((q0_ref, even), (q1_ref, 1 - even)):
         out[0:9] = rhs_ref[pl.ds(6 * up, 9)].astype(BF16)
@@ -411,8 +460,8 @@
 
 
 def coarse_kernel(
-    place, w_ref, wd_ref, bound_ref, full_ref, y0_ref, y1_ref, smooth_ref, out_ref,
-    v_ref, s_ref, carry_ref, b_ref, x_ref, u_ref, inv_ref, idle_ref,
+    place, w_ref, wd_ref, bound_ref, py_ref, px_ref, full_ref, y0_ref, y1_ref, smooth_ref, out_hbm,
+    v_ref, s_ref, carry_ref, b_ref, x_ref, u_ref, inv_ref, idle_ref, out_ref, sem,
 ):
     half = full_ref.shape[-1]
     width = 2 * half
@@ -452,27 +501,20 @@
     sweep(2, 8, refs, half, p1, c1)
     sweep(3, 7, refs, half, p2, c2)
 
-    coarse_x = iota((half, width), 0)
-    fine_x = iota((half, width), 1)
-    gap = jnp.abs(fine_x - 2 * coarse_x)
-    px = jnp.where(gap == 0, 1.0, jnp.where(gap == 1, 0.5, 0.0)).astype(BF16)
-    out_r = iota((24, BAND), 0)
-    src_r = iota((24, BAND), 1)
-    gap_y = jnp.abs((out_r % 8) - 2 * ((src_r % ROWS) - 3))
-    py = jnp.where(gap_y == 0, 1.0, jnp.where(gap_y == 1, 0.5, 0.0))
-    py = jnp.where(out_r // 8 == src_r // ROWS, py, 0.0).astype(BF16)
-    for k in range(5):
-        u_wide = jnp.dot(v_ref[3 + k, 0:BAND], px, preferred_element_type=F32)
-        if k > 0:
-            pieces = ((2 * k - 2, before), (2 * k - 1, 0.5 * (before + u_wide)))
-            for z, plane in pieces:
-                high, low = split(plane)
-                fine = jnp.dot(py, high, preferred_element_type=F32) + jnp.dot(
-                    py, low, preferred_element_type=F32
-                )
-                for d in range(3):
-                    out_ref[d, z] = smooth_ref[d, z] + fine[8 * d : 8 * d + 8]
-        before = u_wide
+    coarse = jnp.concatenate([v_ref[3 + k, 0:BAND] for k in range(5)], axis=0)
+    rows = jnp.dot(py_ref[...], coarse, preferred_element_type=F32)
+    high, low = split(rows)
+    wide = jnp.dot(jnp.concatenate([high, low], axis=0), px_ref[...], preferred_element_type=F32)
+    wide = (wide[0:120] + wide[120:240]).reshape(5, 3, 8, width)
+    copies = []
+    for z in range(8):
+        k = z // 2
+        plane = wide[k] if z % 2 == 0 else 0.5 * (wide[k] + wide[k + 1])
+        out_ref[z] = smooth_ref[:, z] + plane
+        copies.append(pltpu.make_async_copy(out_ref.at[z], out_hbm.at[:, z], sem.at[z]))
+        copies[-1].start()
+    for copy in copies:
+        copy.wait()
 
 
 def swap(array, axis, offset):
@@ -483,21 +525,10 @@
     return lax.ppermute(array, axis, pairs)
 
 
-def level_scratch(planes, width):
-    return [
-        pltpu.VMEM((planes, 2 * BAND, width), BF16),
-        pltpu.VMEM((planes, 2 * ROWS, width), BF16),
-        pltpu.VMEM((2 * BAND, width), F32),
-        pltpu.VMEM((planes, BAND, width), F32),
-        pltpu.VMEM((planes, BAND, width), F32),
-        pltpu.VMEM((planes, BAND, width), F32),
-        pltpu.VMEM((planes, BAND, width), F32),
-        pltpu.VMEM((planes, ROWS, width), F32),
-    ]
-
-
-def call(body, out_shape, n_in, scratch=(), name=None, place=True, space=pltpu.VMEM):
-    vmem = pl.BlockSpec(memory_space=pltpu.VMEM)
+def call(
+    body, out_shape, n_in, scratch=(), name=None, place=True, space=pltpu.VMEM, out_space=pltpu.VMEM
+):
+    vmem = pl.BlockSpec(memory_space=out_space)
     single = not isinstance(out_shape, (tuple, list))
     lead = [pl.BlockSpec(memory_space=pltpu.SMEM)] if place else []
     return pl.pallas_call(
@@ -506,7 +537,7 @@
         in_specs=lead + [pl.BlockSpec(memory_space=space)] * n_in,
         out_specs=vmem if single else [vmem] * len(out_shape),
         scratch_shapes=list(scratch),
-        compiler_params=pltpu.CompilerParams(vmem_limit_bytes=48 << 20),
+        compiler_params=pltpu.CompilerParams(vmem_limit_bytes=24 << 20),
         name=name,
     )
 
@@ -525,52 +556,73 @@
     ).astype(jnp.int32)
     shape = jax.ShapeDtypeStruct
     packet = shape((25, 8, width), BF16)
-    q0, q1, token = call(
+    arguments = (start_field, applied_load, bone_mask)
+    q0, q1, token, start_field, applied_load, bone_mask = call(
         pack_z_kernel,
-        [packet, packet, shape((8, 128), F32)],
+        [packet, packet, shape((8, 128), F32)] + [shape(a.shape, a.dtype) for a in arguments],
         3,
-        [
-            pltpu.VMEM(start_field.shape, F32),
-            pltpu.VMEM(applied_load.shape, F32),
-            pltpu.VMEM(bone_mask.shape, jnp.int32),
-            pltpu.SemaphoreType.DMA((3,)),
-        ],
+        [pltpu.SemaphoreType.DMA((7,))],
         name="pack_z",
         space=pltpu.HBM,
-    )(place, *[pltpu.with_memory_space_constraint(a, pltpu.HBM) for a in (start_field, applied_load, bone_mask)])
+    )(place, *[pltpu.with_memory_space_constraint(a, pltpu.HBM) for a in arguments])
     r1 = swap(q1, "gz", 1)
     r0 = swap(q0, "gz", 0)
-    matrices = call(
+    w, wd, bound, wr, rzy, hzy, py, rx, px, pair = call(
         matrices_kernel,
         [
             shape((4 * BAND, 8 * BAND), BF16),
             shape((4 * BAND, 2 * ROWS), BF16),
             shape((8, 128), F32),
+            shape((2 * BAND, 8 * BAND), BF16),
+            shape((120, 192), BF16),
+            shape((32, 64), BF16),
+            shape((120, 240), BF16),
+            shape((width, half), BF16),
+            shape((half, width), BF16),
+            shape((width, half), BF16),
         ],
         2,
         name="matrices",
         place=False,
     )(element_stiffness, token)
-    packet = shape((53, 8, width), BF16)
-    q0, q1 = call(pack_y_kernel, [packet, packet], 5, name="pack_y")(
-        place, start_field, applied_load, bone_mask, r0, r1
+    packet = shape((32, 8, width), BF16)
+    q0, q1 = call(pack_nodes_kernel, [packet, packet], 5, name="pack_nodes")(
+        place, bound, start_field, bone_mask, r0, r1
     )
     y1 = swap(q1, "gy", 1)
     y0 = swap(q0, "gy", 0)
+    packet = shape((21, 8, width), BF16)
+    q0, q1 = call(pack_load_kernel, [packet, packet], 3, name="pack_load")(
+        place, applied_load, r0, r1
+    )
+    yb1 = swap(q1, "gy", 1)
+    yb0 = swap(q0, "gy", 0)
+    plane16 = shape((16, BAND, width), F32)
+    carry = pltpu.VMEM((2 * BAND, width), F32)
+    shifted = pltpu.VMEM((16, 2 * BAND, width), BF16)
+    full_plane = pltpu.VMEM((16, BAND, width), F32)
+    x0, scales, inverse, idle, first, scale = call(
+        fine_start_kernel,
+        [
+            plane16,
+            shape((16, 2 * ROWS, width), BF16),
+            plane16,
+            shape((16, ROWS, width), F32),
+            plane16,
+            shape((4, 8, half), F32),
+        ],
+        11,
+        [shifted, carry],
+        name="fine_start",
+    )(place, w, wd, bound, hzy, pair, start_field, bone_mask, r0, r1, y0, y1)
     packet = shape((12, 8, half), BF16)
-    smoothed, rhs, scale, q0, q1 = call(
+    smoothed, rhs, q0, q1 = call(
         fine_kernel,
-        [
-            shape(start_field.shape, F32),
-            shape((15, 8, half), F32),
-            shape((4, 8, half), F32),
-            packet,
-            packet,
-        ],
-        10,
-        level_scratch(16, width),
+        [shape(start_field.shape, F32), shape((15, 8, half), F32), packet, packet],
+        15,
+        [shifted, carry, full_plane, full_plane, full_plane],
         name="fine",
-    )(place, *matrices, start_field, applied_load, bone_mask, r0, r1, y0, y1)
+    )(place, w, wr, rzy, rx, x0, scales, inverse, idle, first, scale, applied_load, r0, r1, yb0, yb1)
     r1 = swap(q1, "gz", 1)
     r0 = swap(q0, "gz", 0)
     packet = shape((20, 8, half), BF16)
@@ -582,9 +634,26 @@
     )(place, rhs, scale, r0, r1)
     y1 = swap(q1, "gy", 1)
     y0 = swap(q0, "gy", 0)
+    coarse_plane = pltpu.VMEM((11, BAND, half), F32)
     return call(
-        coarse_kernel, shape(start_field.shape, F32), 7, level_scratch(11, half), name="coarse"
-    )(place, *matrices, full, y0, y1, smoothed)
+        coarse_kernel,
+        shape(start_field.shape, F32),
+        9,
+        [
+            pltpu.VMEM((11, 2 * BAND, half), BF16),
+            pltpu.VMEM((11, 2 * ROWS, half), BF16),
+            pltpu.VMEM((2 * BAND, half), F32),
+            coarse_plane,
+            coarse_plane,
+            coarse_plane,
+            coarse_plane,
+            pltpu.VMEM((11, ROWS, half), F32),
+            pltpu.VMEM((8, 3, 8, width), F32),
+            pltpu.SemaphoreType.DMA((8,)),
+        ],
+        name="coarse",
+        out_space=pltpu.HBM,
+    )(place, w, wd, bound, py, px, full, y0, y1, smoothed)
 
 
 def solution(mesh):

time: 52.1 us -> 50.5 us (0.969)
  waiting for transfers between devices: 16 us -> 8.73 us
  starting transfers between devices: 19.7 us -> 23.5 us
  Pallas kernels: 15.8 us -> 16.9 us
  local copies, waits for them, and re-layouts: 0.02 us -> 0.69 us
    ppermute x8 -> x10, waiting for transfers between devices: 16 us -> 8.73 us  [swap(): return lax.ppermute(array, axis, pairs)]
    pallas_call x3 -> x5, Pallas kernels: 6.57 us -> 10.4 us  [the longest x1 3.7 us: body(): call(coarse_kernel, shape(start_field.shape, F32), 9, [pltpu.VMEM((11, 2...]
    ppermute x8 -> x10, starting transfers between devices: 19.7 us -> 23.5 us  [swap(): return lax.ppermute(array, axis, pairs)]
    pallas_call x1, Pallas kernels: 8.06 us -> 4.85 us  [body(): call(fine_kernel, [shape(start_field.shape, F32), shape((15, 8, half), F3...]
    unnamed x8 -> x2, local copies, waits for them, and re-layouts: 0.02 us -> 0.69 us
    pallas_call x1, Pallas kernels: 0.5 us -> 1.07 us  [body(): call(matrices_kernel, [shape((4 * BAND, 8 * BAND), BF16), shape((4 * BAND...]
  transfers between devices with their start and end apart: 8 -> 10, of which waited for: 5 -> 3; matrix products, arithmetic and copies ran while one was open for 0% -> 0% of each run, Pallas kernels for 1% -> 10%
where the time goes in v2:
time: 50.5 us; the launch traced here: 50 us
  starting transfers between devices  23.5 us (47%)
  Pallas kernels  16.9 us (33%)
  waiting for transfers between devices  8.73 us (17%)
  local copies, waits for them, and re-layouts  0.69 us (1%)
    ppermute x10, starting transfers between devices, swap(): return lax.ppermute(array, axis, pairs)  23.5 us
    ppermute x10, waiting for transfers between devices, swap(): return lax.ppermute(array, axis, pairs)  8.73 us
    pallas_call x1, Pallas kernels, body(): call(fine_kernel, [shape(start_field.shape, F32), shape((15, 8, half), F3...  4.85 us
    pallas_call x1, Pallas kernels, body(): call(coarse_kernel, shape(start_field.shape, F32), 9, [pltpu.VMEM((11, 2...  3.7 us
    pallas_call x1, Pallas kernels, body(): call(fine_start_kernel, [plane16, shape((16, 2 * ROWS, width), BF16), pla...  3.44 us
    pallas_call x1, Pallas kernels, body(): call(pack_z_kernel, [packet, packet, shape((8, 128), F32)] + [shape(a.sha...  1.89 us
    pallas_call x1, Pallas kernels, body(): call(matrices_kernel, [shape((4 * BAND, 8 * BAND), BF16), shape((4 * BAND...  1.07 us
  transfers between devices with their start and end apart: 10, of which 3 were waited for; matrix products, arithmetic and copies ran while one was open for 0% of the time, Pallas kernels for 10%

profile of v2, /device:TPU:7, one launch (start us, length us, event | category | flops | bytes accessed | tf_op | source)
XLA Modules:
  0.0 50.0 jit_solution(17105008678032632146)
XLA Ops:
  0.0 0.1 pad_add_fusion.place
  0.1 1.9 %pack_z.1 = (bf16[25,8,512]{2,1,0:T(8,128)(2,1)S(1)}, bf16[25,8,512]{2,1,0:T(8,128)(2,1)S(1)}, f32[8,128]{1,0:T(8,128)S(1)}, f32[3,8,8,512]{3,2,1,0:T(8,128)S(1)...) custom-call(s32[4]{0:T(128)S(1)} %pad_add_fusion.place, f32[3,8,8,512]{3,2,1,0:T(8,128)} %x_hbm.1, ...), custom_call_target="tpu_custom_call" | custom-call | tf_op jit(solution)/shard_map/pack_z/pallas_call | solution.py:560
  2.0 1.4 %collective-permute-start = (bf16[25,8,512]{2,1,0:T(8,128)(2,1)S(1)}, bf16[25,8,512]{2,1,0:T(8,128)(2,1)S(1)}, u32[]{:S(2)}, u32[]{:S(2)}) collective-permute-start(bf16[25,8,512]{2,1,0:T(8,128)(2,1)S(1)} %get-tuple-element.51), channel_id=1, source_target_pairs={{0,8},{8,0},{16,24},{24,16},{32,40},{40,32},{48,56},{56,48},{64,72... | collective-permute-start | bytes 614408 | tf_op jit(solution)/shard_map/ppermute | solution.py:525
  3.3 4.1 %collective-permute-start.1 = (bf16[25,8,512]{2,1,0:T(8,128)(2,1)S(1)}, bf16[25,8,512]{2,1,0:T(8,128)(2,1)S(1)}, u32[]{:S(2)}, u32[]{:S(2)}) collective-permute-start(bf16[25,8,512]{2,1,0:T(8,128)(2,1)S(1)} %get-tuple-element.52), channel_id=1, source_target_pairs={{8,16},{16,8},{24,32},{32,24},{40,48},{48,40},{56,64},{64,56},{72,... | collective-permute-start | bytes 614408 | tf_op jit(solution)/shard_map/ppermute | solution.py:525
  7.4 0.0 copy-start
  7.4 0.7 %copy-done = bf16[24,24]{1,0:T(8,128)(2,1)S(1)} copy-done((bf16[24,24]{1,0:T(8,128)(2,1)S(1)}, bf16[24,24]{1,0:T(8,128)(2,1)}, u32[]{:S(2)}) %copy-start) | copy-done | bytes 1176
  8.1 1.1 %matrices.1 = (bf16[192,384]{1,0:T(8,128)(2,1)S(1)}, bf16[192,32]{1,0:T(8,128)(2,1)S(1)}, f32[8,128]{1,0:T(8,128)S(1)}, bf16[96,384]{1,0:T(8,128)(2,1)S(1)}, bf1...) custom-call(bf16[24,24]{1,0:T(8,128)(2,1)S(1)} %copy-done, ...), custom_call_target="tpu_custom_call" | custom-call | tf_op jit(solution)/shard_map/matrices/pallas_call | solution.py:570
  9.2 0.0 collective-permute-done.r0_ref
  9.2 3.8 %collective-permute-done.1.r1_ref = bf16[25,8,512]{2,1,0:T(8,128)(2,1)S(1)} collective-permute-done((bf16[25,8,512]{2,1,0:T(8,128)(2,1)S(1)}, bf16[25,8,512]{2,1,0:T(8,128)(2,1)S(1)}, u32[]{:S(2)}, u32[]{:S(2)}) %collective-permute-start.1) | collective-permute-done | bytes 204832 | tf_op jit(solution)/shard_map/ppermute | solution.py:525
  13.0 0.7 %pack_nodes.1 = (bf16[32,8,512]{2,1,0:T(8,128)(2,1)S(1)}, bf16[32,8,512]{2,1,0:T(8,128)(2,1)S(1)}) custom-call(s32[4]{0:T(128)S(1)} %pad_add_fusion.place, f32[8,128]{1,0:T(8,128)S(1)} %get-tuple-element.41.after_ref.bound_ref, f32[3,8,8,512]{3,2,1,0:T(8,128)S(1)} %get-tuple-element.49.x_ref.x_in, s32[8,8,512]{2,1,0:T(8,128)S(1)} %get-tuple-element.50.m_ref.m_in, ...), custom_call_target="tpu_custom_call" | custom-call | tf_op jit(solution)/shard_map/pack_nodes/pallas_call | solution.py:589
  13.7 1.9 %collective-permute-start.2 = (bf16[32,8,512]{2,1,0:T(8,128)(2,1)S(1)}, bf16[32,8,512]{2,1,0:T(8,128)(2,1)S(1)}, u32[]{:S(2)}, u32[]{:S(2)}) collective-permute-start(bf16[32,8,512]{2,1,0:T(8,128)(2,1)S(1)} %get-tuple-element.53), channel_id=1, source_target_pairs={{0,1},{1,0},{2,3},{3,2},{4,5},{5,4},{6,7},{7,6},{8,9},{9,8},{10,11... | collective-permute-start | bytes 786440 | tf_op jit(solution)/shard_map/ppermute | solution.py:525
  15.6 3.4 %collective-permute-start.3 = (bf16[32,8,512]{2,1,0:T(8,128)(2,1)S(1)}, bf16[32,8,512]{2,1,0:T(8,128)(2,1)S(1)}, u32[]{:S(2)}, u32[]{:S(2)}) collective-permute-start(bf16[32,8,512]{2,1,0:T(8,128)(2,1)S(1)} %get-tuple-element.54), channel_id=1, source_target_pairs={{1,2},{2,1},{3,4},{4,3},{5,6},{6,5},{9,10},{10,9},{11,12},{12,11},... | collective-permute-start | bytes 786440 | tf_op jit(solution)/shard_map/ppermute | solution.py:525
  19.1 0.6 %pack_load.1 = (bf16[21,8,512]{2,1,0:T(8,128)(2,1)S(1)}, bf16[21,8,512]{2,1,0:T(8,128)(2,1)S(1)}) custom-call(s32[4]{0:T(128)S(1)} %pad_add_fusion.place, f32[3,8,8,512]{3,2,1,0:T(8,128)S(1)} %get-tuple-element.61.b_ref.b_in, bf16[25,8,512]{2,1,0:T(8,128)(2,1)S(1)} %collective-permute-done.r0_ref, bf16[25,8,512]{2,1,0:T(8,128)(2,1)S(1)} %collective-permute-done.1.r1_ref), custom_call_target="tpu_custom_call" | custom-call | tf_op jit(solution)/shard_map/pack_load/pallas_call | solution.py:595
  19.7 0.1 collective-permute-start.4
  19.8 3.9 %collective-permute-start.5 = (bf16[21,8,512]{2,1,0:T(8,128)(2,1)S(1)}, bf16[21,8,512]{2,1,0:T(8,128)(2,1)S(1)}, u32[]{:S(2)}, u32[]{:S(2)}) collective-permute-start(bf16[21,8,512]{2,1,0:T(8,128)(2,1)S(1)} %get-tuple-element.63), channel_id=1, source_target_pairs={{1,2},{2,1},{3,4},{4,3},{5,6},{6,5},{9,10},{10,9},{11,12},{12,11},... | collective-permute-start | bytes 516104 | tf_op jit(solution)/shard_map/ppermute | solution.py:525
  23.7 0.0 collective-permute-done.2.y0_ref
  23.8 0.0 collective-permute-done.3.y1_ref
  23.8 3.4 %fine_start.1 = (f32[16,48,512]{2,1,0:T(8,128)S(1)}, bf16[16,32,512]{2,1,0:T(8,128)(2,1)S(1)}, f32[16,48,512]{2,1,0:T(8,128)S(1)}, f32[16,16,512]{2,1,0:T(8,128)...) custom-call(s32[4]{0:T(128)S(1)} %pad_add_fusion.place, bf16[192,384]{1,0:T(8,128)(2,1)S(1)} %get-tuple-element.39.w_ref, ...), custom_call_target="tpu_custom_call" | custom-call | tf_op jit(solution)/shard_map/fine_start/pallas_call | solution.py:604
  27.2 0.0 collective-permute-done.4.y0_ref
  27.2 0.0 collective-permute-done.5.y1_ref
  27.2 4.9 %fine.1 = (f32[3,8,8,512]{3,2,1,0:T(8,128)S(1)}, f32[15,8,256]{2,1,0:T(8,128)S(1)}, bf16[12,8,256]{2,1,0:T(8,128)(2,1)S(1)}, bf16[12,8,256]{2,1,0:T(8,128)(2,1)S(1)}) custom-call(s32[4]{0:T(128)S(1)} %pad_add_fusion.place, bf16[192,384]{1,0:T(8,128)(2,1)S(1)} %get-tuple-element.39.w_ref, bf16[96,384]{1,0:T(8,128)(2,1)S(1)} %get-tuple-element.44.wr_ref, ...), custom_call_target="tpu_custom_call" | custom-call | tf_op jit(solution)/shard_map/fine/pallas_call | solution.py:619
  32.1 0.1 collective-permute-start.6
  32.2 4.1 %collective-permute-start.7 = (bf16[12,8,256]{2,1,0:T(8,128)(2,1)S(1)}, bf16[12,8,256]{2,1,0:T(8,128)(2,1)S(1)}, u32[]{:S(2)}, u32[]{:S(2)}) collective-permute-start(bf16[12,8,256]{2,1,0:T(8,128)(2,1)S(1)} %get-tuple-element.66), channel_id=1, source_target_pairs={{8,16},{16,8},{24,32},{32,24},{40,48},{48,40},{56,64},{64,56},{72,... | collective-permute-start | bytes 147464 | tf_op jit(solution)/shard_map/ppermute | solution.py:525
  36.3 0.0 collective-permute-done.6.r0_ref
  36.3 2.9 %collective-permute-done.7.r1_ref = bf16[12,8,256]{2,1,0:T(8,128)(2,1)S(1)} collective-permute-done((bf16[12,8,256]{2,1,0:T(8,128)(2,1)S(1)}, bf16[12,8,256]{2,1,0:T(8,128)(2,1)S(1)}, u32[]{:S(2)}, u32[]{:S(2)}) %collective-permute-start.7) | collective-permute-done | bytes 49184 | tf_op jit(solution)/shard_map/ppermute | solution.py:525
  39.1 0.6 %pack_coarse.1 = (f32[40,8,256]{2,1,0:T(8,128)S(1)}, bf16[20,8,256]{2,1,0:T(8,128)(2,1)S(1)}, bf16[20,8,256]{2,1,0:T(8,128)(2,1)S(1)}) custom-call(s32[4]{0:T(128)S(1)} %pad_add_fusion.place, f32[15,8,256]{2,1,0:T(8,128)S(1)} %get-tuple-element.64.rhs_ref, f32[4,8,256]{2,1,0:T(8,128)S(1)} %get-tuple-element.60.sc_ref, ...), custom_call_target="tpu_custom_call" | custom-call | tf_op jit(solution)/shard_map/pack_coarse/pallas_call | solution.py:629
  39.7 0.1 collective-permute-start.8
  39.8 4.4 %collective-permute-start.9 = (bf16[20,8,256]{2,1,0:T(8,128)(2,1)S(1)}, bf16[20,8,256]{2,1,0:T(8,128)(2,1)S(1)}, u32[]{:S(2)}, u32[]{:S(2)}) collective-permute-start(bf16[20,8,256]{2,1,0:T(8,128)(2,1)S(1)} %get-tuple-element.69), channel_id=1, source_target_pairs={{1,2},{2,1},{3,4},{4,3},{5,6},{6,5},{9,10},{10,9},{11,12},{12,11},... | collective-permute-start | bytes 245768 | tf_op jit(solution)/shard_map/ppermute | solution.py:525
  44.2 0.0 collective-permute-done.8.y0_ref
  44.2 2.1 %collective-permute-done.9.y1_ref = bf16[20,8,256]{2,1,0:T(8,128)(2,1)S(1)} collective-permute-done((bf16[20,8,256]{2,1,0:T(8,128)(2,1)S(1)}, bf16[20,8,256]{2,1,0:T(8,128)(2,1)S(1)}, u32[]{:S(2)}, u32[]{:S(2)}) %collective-permute-start.9) | collective-permute-done | bytes 81952 | tf_op jit(solution)/shard_map/ppermute | solution.py:525
  46.3 3.7 %coarse.1 = f32[3,8,8,512]{3,2,1,0:T(8,128)} custom-call(s32[4]{0:T(128)S(1)} %pad_add_fusion.place, bf16[192,384]{1,0:T(8,128)(2,1)S(1)} %get-tuple-element.39.w_ref, bf16[192,32]{1,0:T(8,128)(2,1)S(1)} %get-tuple-element.40.wd_ref, f32[8,128]{1,0:T(8,128)S(1)} %get-tuple-element.41.after_ref.bound_ref, bf16[120,240]{1,0:T(8,128)(2,1)S(1)} %get-tuple-element.42.py_ref, ...), custom_call_target="tpu_custom_call" | custom-call | tf_op jit(solution)/shard_map/coarse/pallas_call | solution.py:638
Async XLA Ops:
  2.0 7.2 %collective-permute-start = (bf16[25,8,512]{2,1,0:T(8,128)(2,1)S(1)}, bf16[25,8,512]{2,1,0:T(8,128)(2,1)S(1)}, u32[]{:S(2)}, u32[]{:S(2)}) collective-permute-start(bf16[25,8,512]{2,1,0:T(8,128)(2,1)S(1)} %get-tuple-element.51), channel_id=1, source_target_pairs={{0,8},{8,0},{16,24},{24,16},{32,40},{40,32},{48,56},{56,48},{64,72... | collective-permute-start | bytes 614408 | tf_op jit(solution)/shard_map/ppermute | solution.py:525
  3.3 9.6 %collective-permute-start.1 = (bf16[25,8,512]{2,1,0:T(8,128)(2,1)S(1)}, bf16[25,8,512]{2,1,0:T(8,128)(2,1)S(1)}, u32[]{:S(2)}, u32[]{:S(2)}) collective-permute-start(bf16[25,8,512]{2,1,0:T(8,128)(2,1)S(1)} %get-tuple-element.52), channel_id=1, source_target_pairs={{8,16},{16,8},{24,32},{32,24},{40,48},{48,40},{56,64},{64,56},{72,... | collective-permute-start | bytes 614408 | tf_op jit(solution)/shard_map/ppermute | solution.py:525
  7.4 0.7 %copy-start = (bf16[24,24]{1,0:T(8,128)(2,1)S(1)}, bf16[24,24]{1,0:T(8,128)(2,1)}, u32[]{:S(2)}) copy-start(bf16[24,24]{1,0:T(8,128)(2,1)} %e_ref.1) | copy-start | bytes 3460
  13.7 10.1 %collective-permute-start.2 = (bf16[32,8,512]{2,1,0:T(8,128)(2,1)S(1)}, bf16[32,8,512]{2,1,0:T(8,128)(2,1)S(1)}, u32[]{:S(2)}, u32[]{:S(2)}) collective-permute-start(bf16[32,8,512]{2,1,0:T(8,128)(2,1)S(1)} %get-tuple-element.53), channel_id=1, source_target_pairs={{0,1},{1,0},{2,3},{3,2},{4,5},{5,4},{6,7},{7,6},{8,9},{9,8},{10,11... | collective-permute-start | bytes 786440 | tf_op jit(solution)/shard_map/ppermute | solution.py:525
  15.6 8.1 %collective-permute-start.3 = (bf16[32,8,512]{2,1,0:T(8,128)(2,1)S(1)}, bf16[32,8,512]{2,1,0:T(8,128)(2,1)S(1)}, u32[]{:S(2)}, u32[]{:S(2)}) collective-permute-start(bf16[32,8,512]{2,1,0:T(8,128)(2,1)S(1)} %get-tuple-element.54), channel_id=1, source_target_pairs={{1,2},{2,1},{3,4},{4,3},{5,6},{6,5},{9,10},{10,9},{11,12},{12,11},... | collective-permute-start | bytes 786440 | tf_op jit(solution)/shard_map/ppermute | solution.py:525
  19.7 7.5 %collective-permute-start.4 = (bf16[21,8,512]{2,1,0:T(8,128)(2,1)S(1)}, bf16[21,8,512]{2,1,0:T(8,128)(2,1)S(1)}, u32[]{:S(2)}, u32[]{:S(2)}) collective-permute-start(bf16[21,8,512]{2,1,0:T(8,128)(2,1)S(1)} %get-tuple-element.62), channel_id=1, source_target_pairs={{0,1},{1,0},{2,3},{3,2},{4,5},{5,4},{6,7},{7,6},{8,9},{9,8},{10,11... | collective-permute-start | bytes 516104 | tf_op jit(solution)/shard_map/ppermute | solution.py:525
  19.8 7.4 %collective-permute-start.5 = (bf16[21,8,512]{2,1,0:T(8,128)(2,1)S(1)}, bf16[21,8,512]{2,1,0:T(8,128)(2,1)S(1)}, u32[]{:S(2)}, u32[]{:S(2)}) collective-permute-start(bf16[21,8,512]{2,1,0:T(8,128)(2,1)S(1)} %get-tuple-element.63), channel_id=1, source_target_pairs={{1,2},{2,1},{3,4},{4,3},{5,6},{6,5},{9,10},{10,9},{11,12},{12,11},... | collective-permute-start | bytes 516104 | tf_op jit(solution)/shard_map/ppermute | solution.py:525
  32.1 4.2 %collective-permute-start.6 = (bf16[12,8,256]{2,1,0:T(8,128)(2,1)S(1)}, bf16[12,8,256]{2,1,0:T(8,128)(2,1)S(1)}, u32[]{:S(2)}, u32[]{:S(2)}) collective-permute-start(bf16[12,8,256]{2,1,0:T(8,128)(2,1)S(1)} %get-tuple-element.65), channel_id=1, source_target_pairs={{0,8},{8,0},{16,24},{24,16},{32,40},{40,32},{48,56},{56,48},{64,72... | collective-permute-start | bytes 147464 | tf_op jit(solution)/shard_map/ppermute | solution.py:525
  32.2 6.9 %collective-permute-start.7 = (bf16[12,8,256]{2,1,0:T(8,128)(2,1)S(1)}, bf16[12,8,256]{2,1,0:T(8,128)(2,1)S(1)}, u32[]{:S(2)}, u32[]{:S(2)}) collective-permute-start(bf16[12,8,256]{2,1,0:T(8,128)(2,1)S(1)} %get-tuple-element.66), channel_id=1, source_target_pairs={{8,16},{16,8},{24,32},{32,24},{40,48},{48,40},{56,64},{64,56},{72,... | collective-permute-start | bytes 147464 | tf_op jit(solution)/shard_map/ppermute | solution.py:525
  39.7 4.5 %collective-permute-start.8 = (bf16[20,8,256]{2,1,0:T(8,128)(2,1)S(1)}, bf16[20,8,256]{2,1,0:T(8,128)(2,1)S(1)}, u32[]{:S(2)}, u32[]{:S(2)}) collective-permute-start(bf16[20,8,256]{2,1,0:T(8,128)(2,1)S(1)} %get-tuple-element.68), channel_id=1, source_target_pairs={{0,1},{1,0},{2,3},{3,2},{4,5},{5,4},{6,7},{7,6},{8,9},{9,8},{10,11... | collective-permute-start | bytes 245768 | tf_op jit(solution)/shard_map/ppermute | solution.py:525
  39.8 6.5 %collective-permute-start.9 = (bf16[20,8,256]{2,1,0:T(8,128)(2,1)S(1)}, bf16[20,8,256]{2,1,0:T(8,128)(2,1)S(1)}, u32[]{:S(2)}, u32[]{:S(2)}) collective-permute-start(bf16[20,8,256]{2,1,0:T(8,128)(2,1)S(1)} %get-tuple-element.69), channel_id=1, source_target_pairs={{1,2},{2,1},{3,4},{4,3},{5,6},{6,5},{9,10},{10,9},{11,12},{12,11},... | collective-permute-start | bytes 245768 | tf_op jit(solution)/shard_map/ppermute | solution.py:525

commit v3 on v2

v3 whole, which is shorter than its diff:
```python
import jax
import jax.numpy as jnp
from jax import lax
from jax.sharding import PartitionSpec as P
from jax.experimental import pallas as pl
from jax.experimental.pallas import tpu as pltpu

F32 = jnp.float32
BF16 = jnp.bfloat16
CHEB = 3
LOW = 0.1
MID = 0.5 * (1.0 + LOW)
HALF = 0.5 * (1.0 - LOW)
RATIO = (1.0 + LOW) / (1.0 - LOW)
ROWS = 16
BAND = 3 * ROWS
DEEP = 4


def iota(shape, dim):
    return lax.broadcasted_iota(jnp.int32, shape, dim)


def build_matrices(stiff):
    m = 4 * BAND
    row_m = iota((m, 24), 0)
    base_row = 12 * (row_m // (2 * BAND)) + 3 * ((row_m // BAND) % 2) + (row_m // ROWS) % 3
    col_e = iota((m, 24), 1)
    row_k = iota((24, m), 0)
    col_k = iota((24, m), 1)
    base_col = 6 * (col_k // (2 * BAND)) + 3 * ((col_k // BAND) % 2) + (col_k // ROWS) % 3
    mm = iota((m, m), 0)
    kk = iota((m, m), 1)
    gap = (mm % ROWS) - (kk % ROWS) + kk // (2 * BAND)
    blocks = []
    left = []
    for cy in range(2):
        pick = (col_e == base_row + 6 * cy).astype(BF16)
        left.append(jnp.dot(pick, stiff, preferred_element_type=F32).astype(BF16))
    for p in range(2):
        pick = (row_k == base_col + 12 * p).astype(BF16)
        block = jnp.zeros((m, m), F32)
        for cy in range(2):
            full = jnp.dot(left[cy], pick, preferred_element_type=F32)
            block = jnp.where(gap == cy, full, block)
        blocks.append(block.astype(BF16))
    md = iota((m, 2 * ROWS), 0)
    kd = iota((m, 2 * ROWS), 1)
    diag = jnp.zeros((m, 2 * ROWS), F32)
    for cy in range(2):
        own = jnp.sum(
            jnp.where(col_e == base_row + 6 * cy, left[cy].astype(F32), 0.0), axis=1, keepdims=True
        )
        diag = jnp.where((kd // ROWS == cy) & (kd % ROWS == md % ROWS), own, diag)
    return jnp.concatenate(blocks, axis=1), diag.astype(BF16)


def spectral_bound(stiff):
    wide = stiff.astype(F32)
    eye = iota((24, 24), 0) == iota((24, 24), 1)
    own = jnp.sum(jnp.where(eye, wide, 0.0), axis=1, keepdims=True)
    total = jnp.sum(jnp.abs(wide), axis=1, keepdims=True)
    return jnp.max(total / own, axis=0, keepdims=True)


def shift_up(values, width):
    rolled = pltpu.roll(values, width - 1, 1)
    return jnp.where(iota(values.shape, 1) == width - 1, 0.0, rolled)


def shift_down(values):
    rolled = pltpu.roll(values, 1, 1)
    return jnp.where(iota(values.shape, 1) == 0, 0.0, rolled)


def shifted_nodes(values, width):
    return jnp.concatenate([values.astype(BF16), shift_up(values, width).astype(BF16)], axis=0)


def scale_rows(scale):
    down = pltpu.roll(scale, 1, 0)
    down = jnp.where(iota(scale.shape, 0) == 0, 0.0, down)
    return jnp.concatenate([scale.astype(BF16), down.astype(BF16)], axis=0)


def layer_operator(w_ref, nodes, scales):
    def product(layer):
        scale = scales(layer)
        width = scale.shape[-1]
        parts = []
        for p in range(2):
            plane = nodes(layer + p).reshape(6, ROWS, width)
            for cy in range(2):
                masked = plane * scale[cy * ROWS : (cy + 1) * ROWS][None]
                parts.append(masked.reshape(2 * BAND, width))
        return jnp.dot(w_ref[...], jnp.concatenate(parts, axis=0), preferred_element_type=F32)

    return product


def diagonal_operator(wd_ref, scales):
    def product(layer):
        return jnp.dot(wd_ref[...], scales(layer), preferred_element_type=F32)

    return product


def planes_of(lo, hi, product, use, band=BAND):
    carry = product(lo - 1)[2 * band : 4 * band]
    for z in range(lo, hi + 1):
        both = product(z)
        plane = both[0 : 2 * band] + carry
        carry = both[2 * band : 4 * band]
        use(z, plane[0:band] + shift_down(plane[band : 2 * band]))


def inverter(inv_ref, idle_ref, bound, width, past_z, past_y, first, base=0):
    rows = iota((BAND, width), 0) % ROWS
    keep_y = jnp.where((rows >= first) & (past_y == 1), 0.0, 1.0)

    def use(z, diag):
        idle = (diag == 0.0).astype(F32)
        inverse = keep_y / ((diag + idle) * bound)
        if z >= first:
            inverse = inverse * jnp.where(past_z == 1, 0.0, 1.0)
        inv_ref[z - base] = inverse
        idle_ref[z - base] = idle[0:ROWS]

    return use


def tile3(values):
    return jnp.concatenate([values, values, values], axis=0)


def advance(plane, b, x, update, inverse, idle, factors):
    previous, current = factors
    new = current * (inverse * (b - plane - tile3(idle) * x))
    if previous is not None:
        new = previous * update + new
    return x + new, new


def chebyshev_factors():
    factors = [(None, 1.0 / MID)]
    rho = 1.0 / RATIO
    for _ in range(CHEB - 1):
        nxt = 1.0 / (2.0 * RATIO - rho)
        factors.append((nxt * rho, 2.0 * nxt / HALF))
        rho = nxt
    return factors


def weights(gap, where):
    value = jnp.where(gap == 0, 1.0, jnp.where(gap == 1, 0.5, 0.0))
    return jnp.where(where, value, 0.0)


def own_rows(w_ref):
    groups = [w_ref[ROWS * g : ROWS * (g + 1)].astype(F32)[4:12] for g in range(12)]
    return jnp.concatenate(groups, axis=0).astype(BF16)


def restrict_planes():
    out, src = iota((120, 192), 0), iota((120, 192), 1)
    gap_z = jnp.abs(src // 24 - 2 * (out // 24))
    gap_y = jnp.abs(src % 8 - 2 * (out % 8 - 3))
    same = (src // 8) % 3 == (out // 8) % 3
    return (weights(gap_z, same) * weights(gap_y, same)).astype(BF16)


def halve_planes():
    out, src = iota((32, 64), 0), iota((32, 64), 1)
    same = (src // 16 == out // 8) & ((src % 8) // 2 == out % 8 - 3)
    return same.astype(F32).astype(BF16)


def prolong_rows():
    out, src = iota((120, 240), 0), iota((120, 240), 1)
    gap = jnp.abs(out % 8 - 2 * (src % ROWS - 3))
    same = (out // 24 == src // BAND) & ((out // 8) % 3 == (src // ROWS) % 3)
    return weights(gap, same).astype(BF16)


def matrices_kernel(
    e_ref, token_ref, w_ref, wd_ref, bound_ref, wr_ref, rzy_ref, hzy_ref, py_ref, rx_ref, px_ref, pair_ref
):
    stiff = e_ref[...]
    w_ref[...], wd_ref[...] = build_matrices(stiff)
    bound_ref[...] = jnp.broadcast_to(spectral_bound(stiff), (8, 128))
    wr_ref[...] = own_rows(w_ref)
    rzy_ref[...] = restrict_planes()
    hzy_ref[...] = halve_planes()
    py_ref[...] = prolong_rows()
    fine, coarse = iota(rx_ref.shape, 0), iota(rx_ref.shape, 1)
    rx_ref[...] = weights(jnp.abs(fine - 2 * coarse), fine >= 0).astype(BF16)
    pair_ref[...] = (fine // 2 == coarse).astype(F32).astype(BF16)
    coarse, fine = iota(px_ref.shape, 0), iota(px_ref.shape, 1)
    px_ref[...] = weights(jnp.abs(fine - 2 * coarse), fine >= 0).astype(BF16)


def pack_z_kernel(
    place, x_hbm, b_hbm, m_hbm, e_hbm, q0_ref, q1_ref, x_ref, b_ref, m_ref, e_ref, sem
):
    even = 1 - place[0]
    pairs = [(m_hbm, m_ref), (e_hbm, e_ref)]
    for d in range(3):
        pairs += [(x_hbm.at[d], x_ref.at[d]), (b_hbm.at[d], b_ref.at[d])]
    copies = [pltpu.make_async_copy(src, dst, sem.at[i]) for i, (src, dst) in enumerate(pairs)]
    for copy in copies:
        copy.start()
    for copy in copies:
        copy.wait()
    for out, up in ((q0_ref, even), (q1_ref, 1 - even)):
        for d in range(3):
            out[4 * d : 4 * d + 4] = x_ref[d, pl.ds(4 * up, 4)].astype(BF16)
            out[12 + 3 * d : 15 + 3 * d] = b_ref[d, pl.ds(5 * up, 3)].astype(BF16)
        out[21:25] = m_ref[pl.ds(4 * up, 4)].astype(F32).astype(BF16)


def own_planes(x_ref, b_ref, m_ref):
    def at(kind, d, w):
        if kind == "m":
            return m_ref[w - 4].astype(F32)
        return (x_ref if kind == "x" else b_ref)[d, w - 4]

    return at


def borrowed_planes(place, r0_ref, r1_ref):
    odd = place[0] == 1

    def at(kind, d, w):
        low = w < 4
        if kind == "x":
            i = 4 * d + w % 4
        elif kind == "b":
            i = 12 + 3 * d + (w - 1 if low else w - 12)
        else:
            i = 21 + w % 4
        first, second = (r0_ref, r1_ref) if low else (r1_ref, r0_ref)
        return jnp.where(odd, first[i].astype(F32), second[i].astype(F32))

    return at


def flip(values):
    return pltpu.roll(values, 4, 0)


def tiles_of(pairs, load_pairs):
    return (
        [("x", d, pair) for d in range(3) for pair in pairs]
        + [("b", d, pair) for d in range(3) for pair in load_pairs]
        + [("m", 0, pair) for pair in pairs]
    )


OWN_PAIRS = ((4, 5), (6, 7), (8, 9), (10, 11))
OWN_TILES = tiles_of(OWN_PAIRS, OWN_PAIRS)
FAR_TILES = tiles_of(((0, 1), (2, 3), (12, 13), (14, 15)), ((1, 2), (3, 12), (13, 14)))


def pack_rows(place, at, tiles, q0_ref, q1_ref):
    even = place[1] == 0
    for index, (kind, d, (first, second)) in enumerate(tiles):
        a, b = at(kind, d, first), at(kind, d, second)
        head = iota(a.shape, 0) < 4
        up = jnp.where(head, flip(a), b)
        down = jnp.where(head, a, flip(b))
        q0_ref[index] = jnp.where(even, up, down).astype(BF16)
        q1_ref[index] = jnp.where(even, down, up).astype(BF16)


def pack_own_kernel(place, x_ref, b_ref, m_ref, q0_ref, q1_ref, token_ref):
    pack_rows(place, own_planes(x_ref, b_ref, m_ref), OWN_TILES, q0_ref, q1_ref)
    token_ref[...] = jnp.zeros(token_ref.shape, F32)


def pack_far_kernel(place, after_ref, r0_ref, r1_ref, q0_ref, q1_ref):
    pack_rows(place, borrowed_planes(place, r0_ref, r1_ref), FAR_TILES, q0_ref, q1_ref)


def unpack_rows(place, at, tiles, y0_ref, y1_ref, width, use):
    odd = place[1] == 1
    head = iota((8, width), 0) < 4
    for index, (kind, d, pair) in enumerate(tiles):
        low = jnp.where(odd, y0_ref[index].astype(F32), y1_ref[index].astype(F32))
        high = jnp.where(odd, y1_ref[index].astype(F32), y0_ref[index].astype(F32))
        for k, w in enumerate(pair):
            own = flip(at(kind, d, w))
            below = low if k == 0 else flip(low)
            above = flip(high) if k == 0 else high
            block = jnp.concatenate(
                [jnp.where(head, below, own), jnp.where(head, own, above)], axis=0
            )
            use(kind, d, w, block)


def split(values):
    high = values.astype(BF16)
    return high, (values - high.astype(F32)).astype(BF16)


def fine_own_kernel(
    place, w_ref, wd_ref, bound_ref, hzy_ref, pair_ref, x_in, b_in, m_in, y0_ref, y1_ref,
    v0_ref, v1_ref, v2_ref, v3_ref, s_ref, b_ref, x_ref, u_ref, inv_ref, idle_ref, sc_ref,
):
    width = x_in.shape[-1]

    def keep(kind, d, w, block):
        if kind == "m":
            s_ref[w - 4] = scale_rows(block)
        else:
            (x_ref if kind == "x" else b_ref)[w - 4, ROWS * d : ROWS * (d + 1)] = block

    unpack_rows(
        place, own_planes(x_in, b_in, m_in), OWN_TILES, y0_ref, y1_ref, width, keep
    )
    for z in range(8):
        v0_ref[z] = shifted_nodes(x_ref[z], width)

    def scales(layer):
        return s_ref[layer - 4]

    planes_of(
        5, 11, diagonal_operator(wd_ref, scales),
        inverter(inv_ref, idle_ref, bound_ref[0:1, 0:1], width, place[2], place[3], 12, 4),
    )
    levels = (v0_ref, v1_ref, v2_ref, v3_ref)
    for level, factors in enumerate(chebyshev_factors()):
        source, target = levels[level], levels[level + 1]

        def use(w, plane):
            z = w - 4
            update = None if level == 0 else u_ref[z]
            x_ref[z], u_ref[z] = advance(
                plane, b_ref[z], x_ref[z], update, inv_ref[z], idle_ref[z], factors
            )
            target[z] = shifted_nodes(x_ref[z], width)

        planes_of(
            5 + level, 10 - level,
            layer_operator(w_ref, lambda w: source[w - 4], scales), use,
        )
    counts = jnp.dot(
        hzy_ref[...], m_in[...].astype(F32).astype(BF16).reshape(64, width), preferred_element_type=F32
    )
    counts = jnp.dot(counts.astype(BF16), pair_ref[...], preferred_element_type=F32)
    sc_ref[...] = (0.25 * counts).reshape(sc_ref.shape)


def own_part(values, d, head):
    a = values[ROWS * d : ROWS * d + 8]
    b = values[ROWS * d + 8 : ROWS * d + 16]
    return flip(jnp.where(head, b, a))


def fine_rest_kernel(
    place, w_ref, wd_ref, bound_ref, wr_ref, rzy_ref, rx_ref,
    v0_in, v1_in, v2_in, v3_in, s_in, b_mid, x_in, u_in, inv_in, idle_in, sc_ref,
    b_in, r0_ref, r1_ref, y0_ref, y1_ref,
    out_ref, rhs_ref, q0_ref, q1_ref,
    v0_ref, v1_ref, v2_ref, v3_ref, s_ref, b_ref, x_ref, u_ref, inv_ref, idle_ref,
):
    width = b_in.shape[-1]

    def either(mid, far, lo, hi):
        return lambda w: mid[w - 4] if lo <= w <= hi else far[w]

    def keep(kind, d, w, block):
        if kind == "m":
            s_ref[w] = scale_rows(block)
        else:
            (x_ref if kind == "x" else b_ref)[w, ROWS * d : ROWS * (d + 1)] = block

    unpack_rows(
        place, borrowed_planes(place, r0_ref, r1_ref), FAR_TILES, y0_ref, y1_ref, width, keep
    )
    for w in (0, 1, 2, 3, 12, 13, 14, 15):
        v0_ref[w] = shifted_nodes(x_ref[w], width)
    scales = either(s_in, s_ref, 4, 11)
    invert = inverter(inv_ref, idle_ref, bound_ref[0:1, 0:1], width, place[2], place[3], 12)
    planes_of(1, 4, diagonal_operator(wd_ref, scales), invert)
    planes_of(12, 14, diagonal_operator(wd_ref, scales), invert)
    inverse, idles = either(inv_in, inv_ref, 5, 11), either(idle_in, idle_ref, 5, 11)
    loads = either(b_mid, b_ref, 4, 11)
    state = {w: (x_ref, u_ref, w) for w in range(16)}
    state.update({w: (x_in, u_in, w - 4) for w in range(4, 12)})
    near = (v0_in, v1_in, v2_in, v3_in)
    far = (v0_ref, v1_ref, v2_ref, v3_ref)
    for level, factors in enumerate(chebyshev_factors()):
        target = far[level + 1]

        def use(w, plane):
            xs, us, z = state[w]
            update = None if level == 0 else us[z]
            x_ref[w], u_ref[w] = advance(
                plane, loads(w), xs[z], update, inverse(w), idles(w), factors
            )
            state[w] = (x_ref, u_ref, w)
            target[w] = shifted_nodes(x_ref[w], width)

        product = layer_operator(
            w_ref, either(near[level], far[level], 4 + level, 11 - level), scales
        )
        planes_of(1 + level, 4 + level, product, use)
        planes_of(11 - level, 14 - level, product, use)

    head = iota((8, width), 0) < 4
    parts = []

    def use(w, plane):
        idle = own_part(idles(w), 0, head)
        xs, _, z = state[w]
        final = xs[z]
        for d in range(3):
            x = own_part(final, d, head)
            out_ref[d, w - 4] = x
            parts.append(b_in[d, w - 4] - plane[8 * d : 8 * d + 8] - idle * x)

    planes_of(4, 11, layer_operator(wr_ref, either(near[3], far[3], 7, 8), scales), use, 24)
    residual = jnp.concatenate(parts, axis=0).astype(BF16)
    sums = jnp.dot(rzy_ref[...], residual, preferred_element_type=F32)
    sums = jnp.dot(sums.astype(BF16), rx_ref[...], preferred_element_type=F32)
    rhs_ref[...] = sums.reshape(rhs_ref.shape)
    even = 1 - place[0]
    for out, up in ((q0_ref, even), (q1_ref, 1 - even)):
        out[0:9] = rhs_ref[pl.ds(6 * up, 9)].astype(BF16)
        out[9:12] = sc_ref[pl.ds(up, 3)].astype(BF16)


def pack_coarse_kernel(place, rhs_ref, sc_ref, r0_ref, r1_ref, full_ref, q0_ref, q1_ref):
    odd = place[0] == 1
    even_y = place[1] == 0
    head = iota(rhs_ref.shape[1:], 0) < 4
    kept = []

    def low(i):
        return jnp.where(odd, r0_ref[i].astype(F32), r1_ref[i].astype(F32))

    def high(i):
        return jnp.where(odd, r1_ref[i].astype(F32), r0_ref[i].astype(F32))

    for z in range(10):
        c = z - 3
        for d in range(4):
            value = jnp.zeros(rhs_ref.shape[1:], F32)
            if d < 3:
                if -2 <= c <= 0:
                    value = value + low(3 * (c + 2) + d)
                if 4 <= c <= 6:
                    value = value + high(3 * (c - 4) + d)
                if 0 <= c <= 4:
                    value = value + rhs_ref[3 * c + d]
            else:
                if c <= -1:
                    value = low(9 + c + 3)
                elif c >= 4:
                    value = high(9 + c - 4)
                else:
                    value = sc_ref[c]
            full_ref[4 * z + d] = value
            kept.append(value)
    for i in range(20):
        a, b = kept[2 * i], kept[2 * i + 1]
        up = jnp.where(head, flip(a), b)
        down = jnp.where(head, pltpu.roll(a, 5, 0), pltpu.roll(b, 1, 0))
        q0_ref[i] = jnp.where(even_y, up, down).astype(BF16)
        q1_ref[i] = jnp.where(even_y, down, up).astype(BF16)


def coarse_kernel(
    place, w_ref, wd_ref, bound_ref, py_ref, px_ref, full_ref, y0_ref, y1_ref, smooth_ref, out_hbm,
    v_ref, s_ref, b_ref, x_ref, u_ref, inv_ref, idle_ref, out_ref, sem,
):
    half = full_ref.shape[-1]
    width = 2 * half
    bound = bound_ref[0:1, 0:1]
    odd = place[1] == 1
    rows8 = iota((8, half), 0)
    for z in range(10):
        for d in range(4):
            i = 4 * z + d
            low = jnp.where(odd, y0_ref[i // 2].astype(F32), y1_ref[i // 2].astype(F32))
            high = jnp.where(odd, y1_ref[i // 2].astype(F32), y0_ref[i // 2].astype(F32))
            if i % 2:
                low = flip(low)
            high = pltpu.roll(high, 3 if i % 2 else 7, 0)
            first = (
                full_ref[i] + jnp.where(rows8 < 4, low, 0.0) + jnp.where(rows8 == 7, high, 0.0)
            )
            block = jnp.concatenate([first, jnp.where(rows8 < 3, high, 0.0)], axis=0)
            if d < 3:
                b_ref[z, ROWS * d : ROWS * (d + 1)] = block
            else:
                s_ref[z] = scale_rows(block)
    def scales(layer):
        return s_ref[layer]

    planes_of(
        1, 9, diagonal_operator(wd_ref, scales),
        inverter(inv_ref, idle_ref, bound, half, place[2], place[3], 7),
    )
    factors = chebyshev_factors()
    for z in range(1, 10):
        update = factors[0][1] * (inv_ref[z] * b_ref[z])
        u_ref[z] = update
        x_ref[z] = update
        v_ref[z] = shifted_nodes(update, half)
    product = layer_operator(w_ref, lambda z: v_ref[z], scales)
    for level in (1, 2):

        def use(z, plane):
            x_ref[z], u_ref[z] = advance(
                plane, b_ref[z], x_ref[z], u_ref[z], inv_ref[z], idle_ref[z], factors[level]
            )
            v_ref[z] = shifted_nodes(x_ref[z], half)

        planes_of(1 + level, 9 - level if level == 1 else 7, product, use)

    coarse = jnp.concatenate([v_ref[3 + k, 0:BAND] for k in range(5)], axis=0)
    rows = jnp.dot(py_ref[...], coarse, preferred_element_type=F32)
    high, low = split(rows)
    wide = jnp.dot(jnp.concatenate([high, low], axis=0), px_ref[...], preferred_element_type=F32)
    wide = (wide[0:120] + wide[120:240]).reshape(5, 3, 8, width)
    copies = []
    for z in range(8):
        k = z // 2
        plane = wide[k] if z % 2 == 0 else 0.5 * (wide[k] + wide[k + 1])
        out_ref[z] = smooth_ref[:, z] + plane
        copies.append(pltpu.make_async_copy(out_ref.at[z], out_hbm.at[:, z], sem.at[z]))
        copies[-1].start()
    for copy in copies:
        copy.wait()


def swap(array, axis, offset):
    length = lax.axis_size(axis)
    pairs = []
    for i in range(offset, length - 1, 2):
        pairs += [(i, i + 1), (i + 1, i)]
    return lax.ppermute(array, axis, pairs)


def whereabouts():
    gz, gy = lax.axis_index("gz"), lax.axis_index("gy")
    return (
        lax.rem(gz, 2),
        lax.rem(gy, 2),
        (gz == lax.axis_size("gz") - 1).astype(jnp.int32),
        (gy == lax.axis_size("gy") - 1).astype(jnp.int32),
    )


def call(
    body, out_shape, n_in, scratch=(), name=None, place=True, space=pltpu.VMEM, out_space=pltpu.VMEM
):
    vmem = pl.BlockSpec(memory_space=out_space)
    single = not isinstance(out_shape, (tuple, list))
    return pl.pallas_call(
        (lambda *refs: body(whereabouts(), *refs)) if place else body,
        out_shape=out_shape,
        in_specs=[pl.BlockSpec(memory_space=space)] * n_in,
        out_specs=vmem if single else [vmem] * len(out_shape),
        scratch_shapes=list(scratch),
        compiler_params=pltpu.CompilerParams(vmem_limit_bytes=24 << 20),
        name=name,
    )


def body(applied_load, start_field, bone_mask, element_stiffness):
    width = applied_load.shape[-1]
    half = width // 2
    shape = jax.ShapeDtypeStruct
    packet = shape((25, 8, width), BF16)
    arguments = (start_field, applied_load, bone_mask, element_stiffness)
    q0, q1, start_field, applied_load, bone_mask, stiff = call(
        pack_z_kernel,
        [packet, packet] + [shape(a.shape, a.dtype) for a in arguments],
        4,
        [pltpu.SemaphoreType.DMA((8,))],
        name="pack_z",
        space=pltpu.HBM,
    )(*[pltpu.with_memory_space_constraint(a, pltpu.HBM) for a in arguments])
    r1 = swap(q1, "gz", 1)
    r0 = swap(q0, "gz", 0)
    packet = shape((len(OWN_TILES), 8, width), BF16)
    q0, q1, token = call(
        pack_own_kernel, [packet, packet, shape((8, 128), F32)], 3, name="pack_own"
    )(start_field, applied_load, bone_mask)
    yn1 = swap(q1, "gy", 1)
    yn0 = swap(q0, "gy", 0)
    w, wd, bound, wr, rzy, hzy, py, rx, px, pair = call(
        matrices_kernel,
        [
            shape((4 * BAND, 8 * BAND), BF16),
            shape((4 * BAND, 2 * ROWS), BF16),
            shape((8, 128), F32),
            shape((2 * BAND, 8 * BAND), BF16),
            shape((120, 192), BF16),
            shape((32, 64), BF16),
            shape((120, 240), BF16),
            shape((width, half), BF16),
            shape((half, width), BF16),
            shape((width, half), BF16),
        ],
        2,
        name="matrices",
        place=False,
    )(stiff, token)

    packet = shape((len(FAR_TILES), 8, width), BF16)
    q0, q1 = call(pack_far_kernel, [packet, packet], 3, name="pack_far")(bound, r0, r1)
    yf1 = swap(q1, "gy", 1)
    yf0 = swap(q0, "gy", 0)
    def field(count, rows, dtype):
        return (count, rows, width), dtype

    kinds = [(2 * BAND, BF16)] * 4 + [(2 * ROWS, BF16)] + [(BAND, F32)] * 4 + [(ROWS, F32)]
    *middle, scale = call(
        fine_own_kernel,
        [shape(*field(8, *kind)) for kind in kinds] + [shape((4, 8, half), F32)],
        10,
        name="fine_own",
    )(w, wd, bound, hzy, pair, start_field, applied_load, bone_mask, yn0, yn1)
    packet = shape((12, 8, half), BF16)
    smoothed, rhs, q0, q1 = call(
        fine_rest_kernel,
        [shape(start_field.shape, F32), shape((15, 8, half), F32), packet, packet],
        22,
        [pltpu.VMEM(*field(16, *kind)) for kind in kinds],
        name="fine_rest",
    )(w, wd, bound, wr, rzy, rx, *middle, scale, applied_load, r0, r1, yf0, yf1)
    r1 = swap(q1, "gz", 1)
    r0 = swap(q0, "gz", 0)
    packet = shape((20, 8, half), BF16)
    full, q0, q1 = call(
        pack_coarse_kernel,
        [shape((40, 8, half), F32), packet, packet],
        4,
        name="pack_coarse",
    )(rhs, scale, r0, r1)
    y1 = swap(q1, "gy", 1)
    y0 = swap(q0, "gy", 0)
    coarse_plane = pltpu.VMEM((11, BAND, half), F32)
    return call(
        coarse_kernel,
        shape(start_field.shape, F32),
        9,
        [
            pltpu.VMEM((11, 2 * BAND, half), BF16),
            pltpu.VMEM((11, 2 * ROWS, half), BF16),
            coarse_plane,
            coarse_plane,
            coarse_plane,
            coarse_plane,
            pltpu.VMEM((11, ROWS, half), F32),
            pltpu.VMEM((8, 3, 8, width), F32),
            pltpu.SemaphoreType.DMA((8,)),
        ],
        name="coarse",
        out_space=pltpu.HBM,
    )(w, wd, bound, py, px, full, y0, y1, smoothed)


def solution(mesh):
    in_specs = (P(None, "gz", "gy", None), P(None, "gz", "gy", None), P("gz", "gy", None), P())
    out_specs = P(None, "gz", "gy", None)
    return jax.shard_map(body, mesh=mesh, in_specs=in_specs, out_specs=out_specs, check_vma=False)
```

time: 50.5 us -> 44.4 us (0.88)
  Pallas kernels: 16.9 us -> 13.9 us
  waiting for transfers between devices: 8.73 us -> 5.88 us
  local copies, waits for them, and re-layouts: 0.69 us -> 0 us
    ppermute x10, waiting for transfers between devices: 8.73 us -> 5.88 us  [swap(): return lax.ppermute(array, axis, pairs)]
    pallas_call x5, Pallas kernels: 11.5 us -> 9.53 us  [the longest x1 5.21 us: body(): call(fine_rest_kernel, [shape(start_field.shape, F32), shape((15, 8, half...]
    unnamed x2 -> x0, local copies, waits for them, and re-layouts: 0.69 us -> none
    ppermute x10, starting transfers between devices: 23.5 us -> 24 us  [swap(): return lax.ppermute(array, axis, pairs)]
    pallas_call x1, Pallas kernels: 0.62 us -> 0.08 us  [body(): call(pack_coarse_kernel, [shape((40, 8, half), F32), packet, packet], 4,...]
    pallas_call x1, Pallas kernels: 3.7 us -> 3.17 us  [body(): call(coarse_kernel, shape(start_field.shape, F32), 9, [pltpu.VMEM((11, 2...]
  transfers between devices with their start and end apart: 10 -> 10, of which waited for: 3 -> 3; matrix products, arithmetic and copies ran while one was open for 0% -> 0% of each run, Pallas kernels for 10% -> 9%
where the time goes in v3:
time: 44.4 us; the launch traced here: 43.9 us
  starting transfers between devices  24 us (54%)
  Pallas kernels  13.9 us (31%)
  waiting for transfers between devices  5.88 us (13%)
    ppermute x10, starting transfers between devices, swap(): return lax.ppermute(array, axis, pairs)  24 us
    ppermute x10, waiting for transfers between devices, swap(): return lax.ppermute(array, axis, pairs)  5.88 us
    pallas_call x1, Pallas kernels, body(): call(fine_rest_kernel, [shape(start_field.shape, F32), shape((15, 8, half...  5.21 us
    pallas_call x1, Pallas kernels, body(): call(coarse_kernel, shape(start_field.shape, F32), 9, [pltpu.VMEM((11, 2...  3.17 us
    pallas_call x1, Pallas kernels, body(): call(fine_own_kernel, [shape(*field(8, *kind)) for kind in kinds] + [shap...  2.66 us
    pallas_call x1, Pallas kernels, body(): call(pack_z_kernel, [packet, packet] + [shape(a.shape, a.dtype) for a in...  1.37 us
    pallas_call x1, Pallas kernels, body(): call(matrices_kernel, [shape((4 * BAND, 8 * BAND), BF16), shape((4 * BAND...  1.08 us
  transfers between devices with their start and end apart: 10, of which 3 were waited for; matrix products, arithmetic and copies ran while one was open for 0% of the time, Pallas kernels for 9%

profile of v3, /device:TPU:7, one launch (start us, length us, event | category | flops | bytes accessed | tf_op | source)
XLA Modules:
  0.0 43.9 jit_solution(16861247276033614160)
XLA Ops:
  0.0 1.4 %pack_z.1 = (bf16[25,8,512]{2,1,0:T(8,128)(2,1)S(1)}, bf16[25,8,512]{2,1,0:T(8,128)(2,1)S(1)}, f32[3,8,8,512]{3,2,1,0:T(8,128)S(1)}, f32[3,8,8,512]{3,2,1,0:T(8,...) custom-call(f32[3,8,8,512]{3,2,1,0:T(8,128)} %refs_0_.1, f32[3,8,8,512]{3,2,1,0:T(8,128)} %refs_1_.1, ...), custom_call_target="tpu_custom_call" | custom-call | tf_op jit(solution)/shard_map/pack_z/pallas_call | solution.py:578
  1.4 1.4 %collective-permute-start.2 = (bf16[25,8,512]{2,1,0:T(8,128)(2,1)S(1)}, bf16[25,8,512]{2,1,0:T(8,128)(2,1)S(1)}, u32[]{:S(2)}, u32[]{:S(2)}) collective-permute-start(bf16[25,8,512]{2,1,0:T(8,128)(2,1)S(1)} %get-tuple-element.72), channel_id=1, source_target_pairs={{0,8},{8,0},{16,24},{24,16},{32,40},{40,32},{48,56},{56,48},{64,72... | collective-permute-start | bytes 614408 | tf_op jit(solution)/shard_map/ppermute | solution.py:543
  2.8 4.1 %collective-permute-start.3 = (bf16[25,8,512]{2,1,0:T(8,128)(2,1)S(1)}, bf16[25,8,512]{2,1,0:T(8,128)(2,1)S(1)}, u32[]{:S(2)}, u32[]{:S(2)}) collective-permute-start(bf16[25,8,512]{2,1,0:T(8,128)(2,1)S(1)} %get-tuple-element.73), channel_id=1, source_target_pairs={{8,16},{16,8},{24,32},{32,24},{40,48},{48,40},{56,64},{64,56},{72,... | collective-permute-start | bytes 614408 | tf_op jit(solution)/shard_map/ppermute | solution.py:543
  6.8 0.1 pack_own.1
  6.9 1.3 %collective-permute-start = (bf16[28,8,512]{2,1,0:T(8,128)(2,1)S(1)}, bf16[28,8,512]{2,1,0:T(8,128)(2,1)S(1)}, u32[]{:S(2)}, u32[]{:S(2)}) collective-permute-start(bf16[28,8,512]{2,1,0:T(8,128)(2,1)S(1)} %get-tuple-element.59), channel_id=1, source_target_pairs={{0,1},{1,0},{2,3},{3,2},{4,5},{5,4},{6,7},{7,6},{8,9},{9,8},{10,11... | collective-permute-start | bytes 688136 | tf_op jit(solution)/shard_map/ppermute | solution.py:543
  8.3 3.4 %collective-permute-start.1 = (bf16[28,8,512]{2,1,0:T(8,128)(2,1)S(1)}, bf16[28,8,512]{2,1,0:T(8,128)(2,1)S(1)}, u32[]{:S(2)}, u32[]{:S(2)}) collective-permute-start(bf16[28,8,512]{2,1,0:T(8,128)(2,1)S(1)} %get-tuple-element.60), channel_id=1, source_target_pairs={{1,2},{2,1},{3,4},{4,3},{5,6},{6,5},{9,10},{10,9},{11,12},{12,11},... | collective-permute-start | bytes 688136 | tf_op jit(solution)/shard_map/ppermute | solution.py:543
  11.7 1.1 %matrices.1 = (bf16[192,384]{1,0:T(8,128)(2,1)S(1)}, bf16[192,32]{1,0:T(8,128)(2,1)S(1)}, f32[8,128]{1,0:T(8,128)S(1)}, bf16[96,384]{1,0:T(8,128)(2,1)S(1)}, bf1...) custom-call(bf16[24,24]{1,0:T(8,128)(2,1)S(1)} %get-tuple-element.44, ...), custom_call_target="tpu_custom_call" | custom-call | tf_op jit(solution)/shard_map/matrices/pallas_call | solution.py:594
  12.8 0.0 collective-permute-done.2.refs_1_.refs_18_
  12.8 0.0 collective-permute-done.3.refs_2_.refs_19_
  12.8 0.2 pack_far.1
  13.0 1.5 %collective-permute-start.4 = (bf16[25,8,512]{2,1,0:T(8,128)(2,1)S(1)}, bf16[25,8,512]{2,1,0:T(8,128)(2,1)S(1)}, u32[]{:S(2)}, u32[]{:S(2)}) collective-permute-start(bf16[25,8,512]{2,1,0:T(8,128)(2,1)S(1)} %get-tuple-element.74), channel_id=1, source_target_pairs={{0,1},{1,0},{2,3},{3,2},{4,5},{5,4},{6,7},{7,6},{8,9},{9,8},{10,11... | collective-permute-start | bytes 614408 | tf_op jit(solution)/shard_map/ppermute | solution.py:543
  14.5 3.4 %collective-permute-start.5 = (bf16[25,8,512]{2,1,0:T(8,128)(2,1)S(1)}, bf16[25,8,512]{2,1,0:T(8,128)(2,1)S(1)}, u32[]{:S(2)}, u32[]{:S(2)}) collective-permute-start(bf16[25,8,512]{2,1,0:T(8,128)(2,1)S(1)} %get-tuple-element.75), channel_id=1, source_target_pairs={{1,2},{2,1},{3,4},{4,3},{5,6},{6,5},{9,10},{10,9},{11,12},{12,11},... | collective-permute-start | bytes 614408 | tf_op jit(solution)/shard_map/ppermute | solution.py:543
  17.9 0.0 collective-permute-done.refs_8_
  18.0 0.0 collective-permute-done.1.refs_9_
  18.0 2.7 %fine_own.1 = (bf16[8,96,512]{2,1,0:T(8,128)(2,1)S(1)}, bf16[8,96,512]{2,1,0:T(8,128)(2,1)S(1)}, bf16[8,96,512]{2,1,0:T(8,128)(2,1)S(1)}, bf16[8,96,512]{2,1,0:T...) custom-call(bf16[192,384]{1,0:T(8,128)(2,1)S(1)} %get-tuple-element., ...), custom_call_target="tpu_custom_call" | custom-call | tf_op jit(solution)/shard_map/fine_own/pallas_call | solution.py:621
  20.6 0.0 collective-permute-done.4.refs_20_
  20.6 0.9 %collective-permute-done.5.refs_21_ = bf16[25,8,512]{2,1,0:T(8,128)(2,1)S(1)} collective-permute-done((bf16[25,8,512]{2,1,0:T(8,128)(2,1)S(1)}, bf16[25,8,512]{2,1,0:T(8,128)(2,1)S(1)}, u32[]{:S(2)}, u32[]{:S(2)}) %collective-permute-start.5) | collective-permute-done | bytes 204832 | tf_op jit(solution)/shard_map/ppermute | solution.py:543
  21.6 5.2 %fine_rest.1 = (f32[3,8,8,512]{3,2,1,0:T(8,128)S(1)}, f32[15,8,256]{2,1,0:T(8,128)S(1)}, bf16[12,8,256]{2,1,0:T(8,128)(2,1)S(1)}, bf16[12,8,256]{2,1,0:T(8,128)(2,1)S(1)}) custom-call(bf16[192,384]{1,0:T(8,128)(2,1)S(1)} %get-tuple-element.49.refs_0_, bf16[192,32]{1,0:T(8,128)(2,1)S(1)} %get-tuple-element.50.refs_1_, ...), custom_call_target="tpu_custom_call" | custom-call | tf_op jit(solution)/shard_map/fine_rest/pallas_call | solution.py:628
  26.8 0.1 collective-permute-start.6
  26.9 4.1 %collective-permute-start.7 = (bf16[12,8,256]{2,1,0:T(8,128)(2,1)S(1)}, bf16[12,8,256]{2,1,0:T(8,128)(2,1)S(1)}, u32[]{:S(2)}, u32[]{:S(2)}) collective-permute-start(bf16[12,8,256]{2,1,0:T(8,128)(2,1)S(1)} %get-tuple-element.78), channel_id=1, source_target_pairs={{8,16},{16,8},{24,32},{32,24},{40,48},{48,40},{56,64},{64,56},{72,... | collective-permute-start | bytes 147464 | tf_op jit(solution)/shard_map/ppermute | solution.py:543
  31.0 0.0 collective-permute-done.6.refs_2_
  31.0 2.9 %collective-permute-done.7.refs_3_ = bf16[12,8,256]{2,1,0:T(8,128)(2,1)S(1)} collective-permute-done((bf16[12,8,256]{2,1,0:T(8,128)(2,1)S(1)}, bf16[12,8,256]{2,1,0:T(8,128)(2,1)S(1)}, u32[]{:S(2)}, u32[]{:S(2)}) %collective-permute-start.7) | collective-permute-done | bytes 49184 | tf_op jit(solution)/shard_map/ppermute | solution.py:543
  33.8 0.1 pack_coarse.1
  33.9 0.1 collective-permute-start.8
  34.0 4.6 %collective-permute-start.9 = (bf16[20,8,256]{2,1,0:T(8,128)(2,1)S(1)}, bf16[20,8,256]{2,1,0:T(8,128)(2,1)S(1)}, u32[]{:S(2)}, u32[]{:S(2)}) collective-permute-start(bf16[20,8,256]{2,1,0:T(8,128)(2,1)S(1)} %get-tuple-element.81), channel_id=1, source_target_pairs={{1,2},{2,1},{3,4},{4,3},{5,6},{6,5},{9,10},{10,9},{11,12},{12,11},... | collective-permute-start | bytes 245768 | tf_op jit(solution)/shard_map/ppermute | solution.py:543
  38.6 0.0 collective-permute-done.8.refs_6_
  38.7 2.1 %collective-permute-done.9.refs_7_ = bf16[20,8,256]{2,1,0:T(8,128)(2,1)S(1)} collective-permute-done((bf16[20,8,256]{2,1,0:T(8,128)(2,1)S(1)}, bf16[20,8,256]{2,1,0:T(8,128)(2,1)S(1)}, u32[]{:S(2)}, u32[]{:S(2)}) %collective-permute-start.9) | collective-permute-done | bytes 81952 | tf_op jit(solution)/shard_map/ppermute | solution.py:543
  40.8 3.2 %coarse.1 = f32[3,8,8,512]{3,2,1,0:T(8,128)} custom-call(bf16[192,384]{1,0:T(8,128)(2,1)S(1)} %get-tuple-element.49.refs_0_, bf16[192,32]{1,0:T(8,128)(2,1)S(1)} %get-tuple-element.50.refs_1_, f32[8,128]{1,0:T(8,128)S(1)} %get-tuple-element.51.refs_2_.refs_0_, bf16[120,240]{1,0:T(8,128)(2,1)S(1)} %get-tuple-element.52.refs_3_, ...), custom_call_target="tpu_custom_call" | custom-call | tf_op jit(solution)/shard_map/coarse/pallas_call | solution.py:647
Async XLA Ops:
  1.4 11.4 %collective-permute-start.2 = (bf16[25,8,512]{2,1,0:T(8,128)(2,1)S(1)}, bf16[25,8,512]{2,1,0:T(8,128)(2,1)S(1)}, u32[]{:S(2)}, u32[]{:S(2)}) collective-permute-start(bf16[25,8,512]{2,1,0:T(8,128)(2,1)S(1)} %get-tuple-element.72), channel_id=1, source_target_pairs={{0,8},{8,0},{16,24},{24,16},{32,40},{40,32},{48,56},{56,48},{64,72... | collective-permute-start | bytes 614408 | tf_op jit(solution)/shard_map/ppermute | solution.py:543
  2.8 10.1 %collective-permute-start.3 = (bf16[25,8,512]{2,1,0:T(8,128)(2,1)S(1)}, bf16[25,8,512]{2,1,0:T(8,128)(2,1)S(1)}, u32[]{:S(2)}, u32[]{:S(2)}) collective-permute-start(bf16[25,8,512]{2,1,0:T(8,128)(2,1)S(1)} %get-tuple-element.73), channel_id=1, source_target_pairs={{8,16},{16,8},{24,32},{32,24},{40,48},{48,40},{56,64},{64,56},{72,... | collective-permute-start | bytes 614408 | tf_op jit(solution)/shard_map/ppermute | solution.py:543
  6.9 11.0 %collective-permute-start = (bf16[28,8,512]{2,1,0:T(8,128)(2,1)S(1)}, bf16[28,8,512]{2,1,0:T(8,128)(2,1)S(1)}, u32[]{:S(2)}, u32[]{:S(2)}) collective-permute-start(bf16[28,8,512]{2,1,0:T(8,128)(2,1)S(1)} %get-tuple-element.59), channel_id=1, source_target_pairs={{0,1},{1,0},{2,3},{3,2},{4,5},{5,4},{6,7},{7,6},{8,9},{9,8},{10,11... | collective-permute-start | bytes 688136 | tf_op jit(solution)/shard_map/ppermute | solution.py:543
  8.3 9.7 %collective-permute-start.1 = (bf16[28,8,512]{2,1,0:T(8,128)(2,1)S(1)}, bf16[28,8,512]{2,1,0:T(8,128)(2,1)S(1)}, u32[]{:S(2)}, u32[]{:S(2)}) collective-permute-start(bf16[28,8,512]{2,1,0:T(8,128)(2,1)S(1)} %get-tuple-element.60), channel_id=1, source_target_pairs={{1,2},{2,1},{3,4},{4,3},{5,6},{6,5},{9,10},{10,9},{11,12},{12,11},... | collective-permute-start | bytes 688136 | tf_op jit(solution)/shard_map/ppermute | solution.py:543
  13.0 7.6 %collective-permute-start.4 = (bf16[25,8,512]{2,1,0:T(8,128)(2,1)S(1)}, bf16[25,8,512]{2,1,0:T(8,128)(2,1)S(1)}, u32[]{:S(2)}, u32[]{:S(2)}) collective-permute-start(bf16[25,8,512]{2,1,0:T(8,128)(2,1)S(1)} %get-tuple-element.74), channel_id=1, source_target_pairs={{0,1},{1,0},{2,3},{3,2},{4,5},{5,4},{6,7},{7,6},{8,9},{9,8},{10,11... | collective-permute-start | bytes 614408 | tf_op jit(solution)/shard_map/ppermute | solution.py:543
  14.5 7.1 %collective-permute-start.5 = (bf16[25,8,512]{2,1,0:T(8,128)(2,1)S(1)}, bf16[25,8,512]{2,1,0:T(8,128)(2,1)S(1)}, u32[]{:S(2)}, u32[]{:S(2)}) collective-permute-start(bf16[25,8,512]{2,1,0:T(8,128)(2,1)S(1)} %get-tuple-element.75), channel_id=1, source_target_pairs={{1,2},{2,1},{3,4},{4,3},{5,6},{6,5},{9,10},{10,9},{11,12},{12,11},... | collective-permute-start | bytes 614408 | tf_op jit(solution)/shard_map/ppermute | solution.py:543
  26.8 4.2 %collective-permute-start.6 = (bf16[12,8,256]{2,1,0:T(8,128)(2,1)S(1)}, bf16[12,8,256]{2,1,0:T(8,128)(2,1)S(1)}, u32[]{:S(2)}, u32[]{:S(2)}) collective-permute-start(bf16[12,8,256]{2,1,0:T(8,128)(2,1)S(1)} %get-tuple-element.77), channel_id=1, source_target_pairs={{0,8},{8,0},{16,24},{24,16},{32,40},{40,32},{48,56},{56,48},{64,72... | collective-permute-start | bytes 147464 | tf_op jit(solution)/shard_map/ppermute | solution.py:543
  26.9 6.9 %collective-permute-start.7 = (bf16[12,8,256]{2,1,0:T(8,128)(2,1)S(1)}, bf16[12,8,256]{2,1,0:T(8,128)(2,1)S(1)}, u32[]{:S(2)}, u32[]{:S(2)}) collective-permute-start(bf16[12,8,256]{2,1,0:T(8,128)(2,1)S(1)} %get-tuple-element.78), channel_id=1, source_target_pairs={{8,16},{16,8},{24,32},{32,24},{40,48},{48,40},{56,64},{64,56},{72,... | collective-permute-start | bytes 147464 | tf_op jit(solution)/shard_map/ppermute | solution.py:543
  33.9 4.8 %collective-permute-start.8 = (bf16[20,8,256]{2,1,0:T(8,128)(2,1)S(1)}, bf16[20,8,256]{2,1,0:T(8,128)(2,1)S(1)}, u32[]{:S(2)}, u32[]{:S(2)}) collective-permute-start(bf16[20,8,256]{2,1,0:T(8,128)(2,1)S(1)} %get-tuple-element.80), channel_id=1, source_target_pairs={{0,1},{1,0},{2,3},{3,2},{4,5},{5,4},{6,7},{7,6},{8,9},{9,8},{10,11... | collective-permute-start | bytes 245768 | tf_op jit(solution)/shard_map/ppermute | solution.py:543
  34.0 6.8 %collective-permute-start.9 = (bf16[20,8,256]{2,1,0:T(8,128)(2,1)S(1)}, bf16[20,8,256]{2,1,0:T(8,128)(2,1)S(1)}, u32[]{:S(2)}, u32[]{:S(2)}) collective-permute-start(bf16[20,8,256]{2,1,0:T(8,128)(2,1)S(1)} %get-tuple-element.81), channel_id=1, source_target_pairs={{1,2},{2,1},{3,4},{4,3},{5,6},{6,5},{9,10},{10,9},{11,12},{12,11},... | collective-permute-start | bytes 245768 | tf_op jit(solution)/shard_map/ppermute | solution.py:543

commit v4 on v3

--- a/solution.py
+++ b/solution.py
@@ -83,8 +83,15 @@
     return jnp.concatenate([scale.astype(BF16), down.astype(BF16)], axis=0)
 
 
+def half_of(matrix_ref, half):
+    if half is None:
+        return matrix_ref[...]
+    rows = matrix_ref.shape[0] // 2
+    return matrix_ref[half * rows : (half + 1) * rows]
+
+
 def layer_operator(w_ref, nodes, scales):
-    def product(layer):
+    def product(layer, half=None):
         scale = scales(layer)
         width = scale.shape[-1]
         parts = []
@@ -93,24 +100,29 @@
             for cy in range(2):
                 masked = plane * scale[cy * ROWS : (cy + 1) * ROWS][None]
                 parts.append(masked.reshape(2 * BAND, width))
-        return jnp.dot(w_ref[...], jnp.concatenate(parts, axis=0), preferred_element_type=F32)
+        matrix = half_of(w_ref, half)
+        return jnp.dot(matrix, jnp.concatenate(parts, axis=0), preferred_element_type=F32)
 
     return product
 
 
 def diagonal_operator(wd_ref, scales):
-    def product(layer):
-        return jnp.dot(wd_ref[...], scales(layer), preferred_element_type=F32)
+    def product(layer, half=None):
+        return jnp.dot(half_of(wd_ref, half), scales(layer), preferred_element_type=F32)
 
     return product
 
 
-def planes_of(lo, hi, product, use, band=BAND):
-    carry = product(lo - 1)[2 * band : 4 * band]
+def planes_of(lo, hi, product, use, band=BAND, below=None, above=None):
+    carry = product(lo - 1, 1) if below is None else below
     for z in range(lo, hi + 1):
-        both = product(z)
-        plane = both[0 : 2 * band] + carry
-        carry = both[2 * band : 4 * band]
+        if z < hi:
+            both = product(z)
+            part, rest = both[0 : 2 * band], both[2 * band : 4 * band]
+        else:
+            part, rest = product(z, 0) if above is None else above, None
+        plane = part + carry
+        carry = rest
         use(z, plane[0:band] + shift_down(plane[band : 2 * band]))
 
 
@@ -304,7 +316,7 @@
 
 def fine_own_kernel(
     place, w_ref, wd_ref, bound_ref, hzy_ref, pair_ref, x_in, b_in, m_in, y0_ref, y1_ref,
-    v0_ref, v1_ref, v2_ref, v3_ref, s_ref, b_ref, x_ref, u_ref, inv_ref, idle_ref, sc_ref,
+    v0_ref, v1_ref, v2_ref, v3_ref, s_ref, b_ref, x_ref, u_ref, inv_ref, idle_ref, seam_ref, sc_ref,
 ):
     width = x_in.shape[-1]
 
@@ -339,9 +351,13 @@
             )
             target[z] = shifted_nodes(x_ref[z], width)
 
+        lo, hi = 5 + level, 10 - level
+        product = layer_operator(w_ref, lambda w: source[w - 4], scales)
+        first, last = product(lo - 1), product(hi)
+        seam_ref[2 * level] = first[0 : 2 * BAND]
+        seam_ref[2 * level + 1] = last[2 * BAND : 4 * BAND]
         planes_of(
-            5 + level, 10 - level,
-            layer_operator(w_ref, lambda w: source[w - 4], scales), use,
+            lo, hi, product, use, below=first[2 * BAND : 4 * BAND], above=last[0 : 2 * BAND]
         )
     counts = jnp.dot(
         hzy_ref[...], m_in[...].astype(F32).astype(BF16).reshape(64, width), preferred_element_type=F32
@@ -358,7 +374,7 @@
 
 def fine_rest_kernel(
     place, w_ref, wd_ref, bound_ref, wr_ref, rzy_ref, rx_ref,
-    v0_in, v1_in, v2_in, v3_in, s_in, b_mid, x_in, u_in, inv_in, idle_in, sc_ref,
+    v0_in, v1_in, v2_in, v3_in, s_in, b_mid, x_in, u_in, inv_in, idle_in, seam_ref, sc_ref,
     b_in, r0_ref, r1_ref, y0_ref, y1_ref,
     out_ref, rhs_ref, q0_ref, q1_ref,
     v0_ref, v1_ref, v2_ref, v3_ref, s_ref, b_ref, x_ref, u_ref, inv_ref, idle_ref,
@@ -404,8 +420,8 @@
         product = layer_operator(
             w_ref, either(near[level], far[level], 4 + level, 11 - level), scales
         )
-        planes_of(1 + level, 4 + level, product, use)
-        planes_of(11 - level, 14 - level, product, use)
+        planes_of(1 + level, 4 + level, product, use, above=seam_ref[2 * level])
+        planes_of(11 - level, 14 - level, product, use, below=seam_ref[2 * level + 1])
 
     head = iota((8, width), 0) < 4
     parts = []
@@ -620,7 +636,8 @@
     kinds = [(2 * BAND, BF16)] * 4 + [(2 * ROWS, BF16)] + [(BAND, F32)] * 4 + [(ROWS, F32)]
     *middle, scale = call(
         fine_own_kernel,
-        [shape(*field(8, *kind)) for kind in kinds] + [shape((4, 8, half), F32)],
+        [shape(*field(8, *kind)) for kind in kinds]
+        + [shape(*field(6, 2 * BAND, F32)), shape((4, 8, half), F32)],
         10,
         name="fine_own",
     )(w, wd, bound, hzy, pair, start_field, applied_load, bone_mask, yn0, yn1)
@@ -628,7 +645,7 @@
     smoothed, rhs, q0, q1 = call(
         fine_rest_kernel,
         [shape(start_field.shape, F32), shape((15, 8, half), F32), packet, packet],
-        22,
+        23,
         [pltpu.VMEM(*field(16, *kind)) for kind in kinds],
         name="fine_rest",
     )(w, wd, bound, wr, rzy, rx, *middle, scale, applied_load, r0, r1, yf0, yf1)

time: 44.4 us -> 43.4 us (0.977)
  Pallas kernels: 13.9 us -> 13.4 us
  waiting for transfers between devices: 5.88 us -> 5.41 us
    pallas_call x1, Pallas kernels: 5.21 us -> 4.48 us  [body(): call(fine_rest_kernel, [shape(start_field.shape, F32), shape((15, 8, half...]
    ppermute x10, waiting for transfers between devices: 5.88 us -> 5.41 us  [swap(): return lax.ppermute(array, axis, pairs)]
    pallas_call x1, Pallas kernels: 2.66 us -> 3.13 us  [body(): call(fine_own_kernel, [shape(*field(8, *kind)) for kind in kinds] + [shap...]
  transfers between devices with their start and end apart: 10 -> 10, of which waited for: 3 -> 3; matrix products, arithmetic and copies ran while one was open for 0% -> 0% of each run, Pallas kernels for 9% -> 10%
where the time goes in v4:
time: 43.4 us; the launch traced here: 43 us
  starting transfers between devices  24 us (55%)
  Pallas kernels  13.4 us (31%)
  waiting for transfers between devices  5.41 us (12%)
    ppermute x10, starting transfers between devices, swap(): return lax.ppermute(array, axis, pairs)  24 us
    ppermute x10, waiting for transfers between devices, swap(): return lax.ppermute(array, axis, pairs)  5.41 us
    pallas_call x1, Pallas kernels, body(): call(fine_rest_kernel, [shape(start_field.shape, F32), shape((15, 8, half...  4.48 us
    pallas_call x1, Pallas kernels, body(): call(fine_own_kernel, [shape(*field(8, *kind)) for kind in kinds] + [shap...  3.13 us
    pallas_call x1, Pallas kernels, body(): call(coarse_kernel, shape(start_field.shape, F32), 9, [pltpu.VMEM((11, 2...  2.98 us
    pallas_call x1, Pallas kernels, body(): call(pack_z_kernel, [packet, packet] + [shape(a.shape, a.dtype) for a in...  1.37 us
    pallas_call x1, Pallas kernels, body(): call(matrices_kernel, [shape((4 * BAND, 8 * BAND), BF16), shape((4 * BAND...  1.08 us
  transfers between devices with their start and end apart: 10, of which 3 were waited for; matrix products, arithmetic and copies ran while one was open for 0% of the time, Pallas kernels for 10%

profile of v4, /device:TPU:7, one launch (start us, length us, event | category | flops | bytes accessed | tf_op | source)
XLA Modules:
  0.0 43.0 jit_solution(16675818169181956736)
XLA Ops:
  0.0 1.4 %pack_z.1 = (bf16[25,8,512]{2,1,0:T(8,128)(2,1)S(1)}, bf16[25,8,512]{2,1,0:T(8,128)(2,1)S(1)}, f32[3,8,8,512]{3,2,1,0:T(8,128)S(1)}, f32[3,8,8,512]{3,2,1,0:T(8,...) custom-call(f32[3,8,8,512]{3,2,1,0:T(8,128)} %refs_0_.1, f32[3,8,8,512]{3,2,1,0:T(8,128)} %refs_1_.1, ...), custom_call_target="tpu_custom_call" | custom-call | tf_op jit(solution)/shard_map/pack_z/pallas_call | solution.py:594
  1.4 1.4 %collective-permute-start.2 = (bf16[25,8,512]{2,1,0:T(8,128)(2,1)S(1)}, bf16[25,8,512]{2,1,0:T(8,128)(2,1)S(1)}, u32[]{:S(2)}, u32[]{:S(2)}) collective-permute-start(bf16[25,8,512]{2,1,0:T(8,128)(2,1)S(1)} %get-tuple-element.74), channel_id=1, source_target_pairs={{0,8},{8,0},{16,24},{24,16},{32,40},{40,32},{48,56},{56,48},{64,72... | collective-permute-start | bytes 614408 | tf_op jit(solution)/shard_map/ppermute | solution.py:559
  2.8 4.1 %collective-permute-start.3 = (bf16[25,8,512]{2,1,0:T(8,128)(2,1)S(1)}, bf16[25,8,512]{2,1,0:T(8,128)(2,1)S(1)}, u32[]{:S(2)}, u32[]{:S(2)}) collective-permute-start(bf16[25,8,512]{2,1,0:T(8,128)(2,1)S(1)} %get-tuple-element.75), channel_id=1, source_target_pairs={{8,16},{16,8},{24,32},{32,24},{40,48},{48,40},{56,64},{64,56},{72,... | collective-permute-start | bytes 614408 | tf_op jit(solution)/shard_map/ppermute | solution.py:559
  6.8 0.1 pack_own.1
  6.9 1.3 %collective-permute-start = (bf16[28,8,512]{2,1,0:T(8,128)(2,1)S(1)}, bf16[28,8,512]{2,1,0:T(8,128)(2,1)S(1)}, u32[]{:S(2)}, u32[]{:S(2)}) collective-permute-start(bf16[28,8,512]{2,1,0:T(8,128)(2,1)S(1)} %get-tuple-element.60), channel_id=1, source_target_pairs={{0,1},{1,0},{2,3},{3,2},{4,5},{5,4},{6,7},{7,6},{8,9},{9,8},{10,11... | collective-permute-start | bytes 688136 | tf_op jit(solution)/shard_map/ppermute | solution.py:559
  8.3 3.4 %collective-permute-start.1 = (bf16[28,8,512]{2,1,0:T(8,128)(2,1)S(1)}, bf16[28,8,512]{2,1,0:T(8,128)(2,1)S(1)}, u32[]{:S(2)}, u32[]{:S(2)}) collective-permute-start(bf16[28,8,512]{2,1,0:T(8,128)(2,1)S(1)} %get-tuple-element.61), channel_id=1, source_target_pairs={{1,2},{2,1},{3,4},{4,3},{5,6},{6,5},{9,10},{10,9},{11,12},{12,11},... | collective-permute-start | bytes 688136 | tf_op jit(solution)/shard_map/ppermute | solution.py:559
  11.7 1.1 %matrices.1 = (bf16[192,384]{1,0:T(8,128)(2,1)S(1)}, bf16[192,32]{1,0:T(8,128)(2,1)S(1)}, f32[8,128]{1,0:T(8,128)S(1)}, bf16[96,384]{1,0:T(8,128)(2,1)S(1)}, bf1...) custom-call(bf16[24,24]{1,0:T(8,128)(2,1)S(1)} %get-tuple-element.45, ...), custom_call_target="tpu_custom_call" | custom-call | tf_op jit(solution)/shard_map/matrices/pallas_call | solution.py:610
  12.8 0.0 collective-permute-done.2.refs_1_.refs_19_
  12.8 0.0 collective-permute-done.3.refs_2_.refs_20_
  12.8 0.2 pack_far.1
  13.0 1.5 %collective-permute-start.4 = (bf16[25,8,512]{2,1,0:T(8,128)(2,1)S(1)}, bf16[25,8,512]{2,1,0:T(8,128)(2,1)S(1)}, u32[]{:S(2)}, u32[]{:S(2)}) collective-permute-start(bf16[25,8,512]{2,1,0:T(8,128)(2,1)S(1)} %get-tuple-element.76), channel_id=1, source_target_pairs={{0,1},{1,0},{2,3},{3,2},{4,5},{5,4},{6,7},{7,6},{8,9},{9,8},{10,11... | collective-permute-start | bytes 614408 | tf_op jit(solution)/shard_map/ppermute | solution.py:559
  14.5 3.4 %collective-permute-start.5 = (bf16[25,8,512]{2,1,0:T(8,128)(2,1)S(1)}, bf16[25,8,512]{2,1,0:T(8,128)(2,1)S(1)}, u32[]{:S(2)}, u32[]{:S(2)}) collective-permute-start(bf16[25,8,512]{2,1,0:T(8,128)(2,1)S(1)} %get-tuple-element.77), channel_id=1, source_target_pairs={{1,2},{2,1},{3,4},{4,3},{5,6},{6,5},{9,10},{10,9},{11,12},{12,11},... | collective-permute-start | bytes 614408 | tf_op jit(solution)/shard_map/ppermute | solution.py:559
  18.0 0.0 collective-permute-done.refs_8_
  18.0 0.0 collective-permute-done.1.refs_9_
  18.0 3.1 %fine_own.1 = (bf16[8,96,512]{2,1,0:T(8,128)(2,1)S(1)}, bf16[8,96,512]{2,1,0:T(8,128)(2,1)S(1)}, bf16[8,96,512]{2,1,0:T(8,128)(2,1)S(1)}, bf16[8,96,512]{2,1,0:T...) custom-call(bf16[192,384]{1,0:T(8,128)(2,1)S(1)} %get-tuple-element., ...), custom_call_target="tpu_custom_call" | custom-call | tf_op jit(solution)/shard_map/fine_own/pallas_call | solution.py:637
  21.1 0.0 collective-permute-done.4.refs_21_
  21.1 0.4 %collective-permute-done.5.refs_22_ = bf16[25,8,512]{2,1,0:T(8,128)(2,1)S(1)} collective-permute-done((bf16[25,8,512]{2,1,0:T(8,128)(2,1)S(1)}, bf16[25,8,512]{2,1,0:T(8,128)(2,1)S(1)}, u32[]{:S(2)}, u32[]{:S(2)}) %collective-permute-start.5) | collective-permute-done | bytes 204832 | tf_op jit(solution)/shard_map/ppermute | solution.py:559
  21.6 4.5 %fine_rest.1 = (f32[3,8,8,512]{3,2,1,0:T(8,128)S(1)}, f32[15,8,256]{2,1,0:T(8,128)S(1)}, bf16[12,8,256]{2,1,0:T(8,128)(2,1)S(1)}, bf16[12,8,256]{2,1,0:T(8,128)(2,1)S(1)}) custom-call(bf16[192,384]{1,0:T(8,128)(2,1)S(1)} %get-tuple-element.50.refs_0_, bf16[192,32]{1,0:T(8,128)(2,1)S(1)} %get-tuple-element.51.refs_1_, ...), custom_call_target="tpu_custom_call" | custom-call | tf_op jit(solution)/shard_map/fine_rest/pallas_call | solution.py:645
  26.1 0.1 collective-permute-start.6
  26.1 4.1 %collective-permute-start.7 = (bf16[12,8,256]{2,1,0:T(8,128)(2,1)S(1)}, bf16[12,8,256]{2,1,0:T(8,128)(2,1)S(1)}, u32[]{:S(2)}, u32[]{:S(2)}) collective-permute-start(bf16[12,8,256]{2,1,0:T(8,128)(2,1)S(1)} %get-tuple-element.80), channel_id=1, source_target_pairs={{8,16},{16,8},{24,32},{32,24},{40,48},{48,40},{56,64},{64,56},{72,... | collective-permute-start | bytes 147464 | tf_op jit(solution)/shard_map/ppermute | solution.py:559
  30.2 0.0 collective-permute-done.6.refs_2_
  30.2 2.8 %collective-permute-done.7.refs_3_ = bf16[12,8,256]{2,1,0:T(8,128)(2,1)S(1)} collective-permute-done((bf16[12,8,256]{2,1,0:T(8,128)(2,1)S(1)}, bf16[12,8,256]{2,1,0:T(8,128)(2,1)S(1)}, u32[]{:S(2)}, u32[]{:S(2)}) %collective-permute-start.7) | collective-permute-done | bytes 49184 | tf_op jit(solution)/shard_map/ppermute | solution.py:559
  33.1 0.1 pack_coarse.1
  33.2 0.1 collective-permute-start.8
  33.3 4.7 %collective-permute-start.9 = (bf16[20,8,256]{2,1,0:T(8,128)(2,1)S(1)}, bf16[20,8,256]{2,1,0:T(8,128)(2,1)S(1)}, u32[]{:S(2)}, u32[]{:S(2)}) collective-permute-start(bf16[20,8,256]{2,1,0:T(8,128)(2,1)S(1)} %get-tuple-element.83), channel_id=1, source_target_pairs={{1,2},{2,1},{3,4},{4,3},{5,6},{6,5},{9,10},{10,9},{11,12},{12,11},... | collective-permute-start | bytes 245768 | tf_op jit(solution)/shard_map/ppermute | solution.py:559
  37.9 0.0 collective-permute-done.8.refs_6_
  37.9 2.1 %collective-permute-done.9.refs_7_ = bf16[20,8,256]{2,1,0:T(8,128)(2,1)S(1)} collective-permute-done((bf16[20,8,256]{2,1,0:T(8,128)(2,1)S(1)}, bf16[20,8,256]{2,1,0:T(8,128)(2,1)S(1)}, u32[]{:S(2)}, u32[]{:S(2)}) %collective-permute-start.9) | collective-permute-done | bytes 81952 | tf_op jit(solution)/shard_map/ppermute | solution.py:559
  40.0 3.0 %coarse.1 = f32[3,8,8,512]{3,2,1,0:T(8,128)} custom-call(bf16[192,384]{1,0:T(8,128)(2,1)S(1)} %get-tuple-element.50.refs_0_, bf16[192,32]{1,0:T(8,128)(2,1)S(1)} %get-tuple-element.51.refs_1_, f32[8,128]{1,0:T(8,128)S(1)} %get-tuple-element.52.refs_2_.refs_0_, bf16[120,240]{1,0:T(8,128)(2,1)S(1)} %get-tuple-element.53.refs_3_, ...), custom_call_target="tpu_custom_call" | custom-call | tf_op jit(solution)/shard_map/coarse/pallas_call | solution.py:664
Async XLA Ops:
  1.4 11.4 %collective-permute-start.2 = (bf16[25,8,512]{2,1,0:T(8,128)(2,1)S(1)}, bf16[25,8,512]{2,1,0:T(8,128)(2,1)S(1)}, u32[]{:S(2)}, u32[]{:S(2)}) collective-permute-start(bf16[25,8,512]{2,1,0:T(8,128)(2,1)S(1)} %get-tuple-element.74), channel_id=1, source_target_pairs={{0,8},{8,0},{16,24},{24,16},{32,40},{40,32},{48,56},{56,48},{64,72... | collective-permute-start | bytes 614408 | tf_op jit(solution)/shard_map/ppermute | solution.py:559
  2.8 10.1 %collective-permute-start.3 = (bf16[25,8,512]{2,1,0:T(8,128)(2,1)S(1)}, bf16[25,8,512]{2,1,0:T(8,128)(2,1)S(1)}, u32[]{:S(2)}, u32[]{:S(2)}) collective-permute-start(bf16[25,8,512]{2,1,0:T(8,128)(2,1)S(1)} %get-tuple-element.75), channel_id=1, source_target_pairs={{8,16},{16,8},{24,32},{32,24},{40,48},{48,40},{56,64},{64,56},{72,... | collective-permute-start | bytes 614408 | tf_op jit(solution)/shard_map/ppermute | solution.py:559
  6.9 11.0 %collective-permute-start = (bf16[28,8,512]{2,1,0:T(8,128)(2,1)S(1)}, bf16[28,8,512]{2,1,0:T(8,128)(2,1)S(1)}, u32[]{:S(2)}, u32[]{:S(2)}) collective-permute-start(bf16[28,8,512]{2,1,0:T(8,128)(2,1)S(1)} %get-tuple-element.60), channel_id=1, source_target_pairs={{0,1},{1,0},{2,3},{3,2},{4,5},{5,4},{6,7},{7,6},{8,9},{9,8},{10,11... | collective-permute-start | bytes 688136 | tf_op jit(solution)/shard_map/ppermute | solution.py:559
  8.3 9.7 %collective-permute-start.1 = (bf16[28,8,512]{2,1,0:T(8,128)(2,1)S(1)}, bf16[28,8,512]{2,1,0:T(8,128)(2,1)S(1)}, u32[]{:S(2)}, u32[]{:S(2)}) collective-permute-start(bf16[28,8,512]{2,1,0:T(8,128)(2,1)S(1)} %get-tuple-element.61), channel_id=1, source_target_pairs={{1,2},{2,1},{3,4},{4,3},{5,6},{6,5},{9,10},{10,9},{11,12},{12,11},... | collective-permute-start | bytes 688136 | tf_op jit(solution)/shard_map/ppermute | solution.py:559
  13.0 8.1 %collective-permute-start.4 = (bf16[25,8,512]{2,1,0:T(8,128)(2,1)S(1)}, bf16[25,8,512]{2,1,0:T(8,128)(2,1)S(1)}, u32[]{:S(2)}, u32[]{:S(2)}) collective-permute-start(bf16[25,8,512]{2,1,0:T(8,128)(2,1)S(1)} %get-tuple-element.76), channel_id=1, source_target_pairs={{0,1},{1,0},{2,3},{3,2},{4,5},{5,4},{6,7},{7,6},{8,9},{9,8},{10,11... | collective-permute-start | bytes 614408 | tf_op jit(solution)/shard_map/ppermute | solution.py:559
  14.5 7.1 %collective-permute-start.5 = (bf16[25,8,512]{2,1,0:T(8,128)(2,1)S(1)}, bf16[25,8,512]{2,1,0:T(8,128)(2,1)S(1)}, u32[]{:S(2)}, u32[]{:S(2)}) collective-permute-start(bf16[25,8,512]{2,1,0:T(8,128)(2,1)S(1)} %get-tuple-element.77), channel_id=1, source_target_pairs={{1,2},{2,1},{3,4},{4,3},{5,6},{6,5},{9,10},{10,9},{11,12},{12,11},... | collective-permute-start | bytes 614408 | tf_op jit(solution)/shard_map/ppermute | solution.py:559
  26.1 4.2 %collective-permute-start.6 = (bf16[12,8,256]{2,1,0:T(8,128)(2,1)S(1)}, bf16[12,8,256]{2,1,0:T(8,128)(2,1)S(1)}, u32[]{:S(2)}, u32[]{:S(2)}) collective-permute-start(bf16[12,8,256]{2,1,0:T(8,128)(2,1)S(1)} %get-tuple-element.79), channel_id=1, source_target_pairs={{0,8},{8,0},{16,24},{24,16},{32,40},{40,32},{48,56},{56,48},{64,72... | collective-permute-start | bytes 147464 | tf_op jit(solution)/shard_map/ppermute | solution.py:559
  26.1 6.9 %collective-permute-start.7 = (bf16[12,8,256]{2,1,0:T(8,128)(2,1)S(1)}, bf16[12,8,256]{2,1,0:T(8,128)(2,1)S(1)}, u32[]{:S(2)}, u32[]{:S(2)}) collective-permute-start(bf16[12,8,256]{2,1,0:T(8,128)(2,1)S(1)} %get-tuple-element.80), channel_id=1, source_target_pairs={{8,16},{16,8},{24,32},{32,24},{40,48},{48,40},{56,64},{64,56},{72,... | collective-permute-start | bytes 147464 | tf_op jit(solution)/shard_map/ppermute | solution.py:559
  33.2 4.8 %collective-permute-start.8 = (bf16[20,8,256]{2,1,0:T(8,128)(2,1)S(1)}, bf16[20,8,256]{2,1,0:T(8,128)(2,1)S(1)}, u32[]{:S(2)}, u32[]{:S(2)}) collective-permute-start(bf16[20,8,256]{2,1,0:T(8,128)(2,1)S(1)} %get-tuple-element.82), channel_id=1, source_target_pairs={{0,1},{1,0},{2,3},{3,2},{4,5},{5,4},{6,7},{7,6},{8,9},{9,8},{10,11... | collective-permute-start | bytes 245768 | tf_op jit(solution)/shard_map/ppermute | solution.py:559
  33.3 6.8 %collective-permute-start.9 = (bf16[20,8,256]{2,1,0:T(8,128)(2,1)S(1)}, bf16[20,8,256]{2,1,0:T(8,128)(2,1)S(1)}, u32[]{:S(2)}, u32[]{:S(2)}) collective-permute-start(bf16[20,8,256]{2,1,0:T(8,128)(2,1)S(1)} %get-tuple-element.83), channel_id=1, source_target_pairs={{1,2},{2,1},{3,4},{4,3},{5,6},{6,5},{9,10},{10,9},{11,12},{12,11},... | collective-permute-start | bytes 245768 | tf_op jit(solution)/shard_map/ppermute | solution.py:559

commit v5 on v4

--- a/solution.py
+++ b/solution.py
@@ -113,7 +113,7 @@
     return product
 
 
-def planes_of(lo, hi, product, use, band=BAND, below=None, above=None):
+def plane_steps(lo, hi, product, use, band=BAND, below=None, above=None):
     carry = product(lo - 1, 1) if below is None else below
     for z in range(lo, hi + 1):
         if z < hi:
@@ -124,6 +124,12 @@
         plane = part + carry
         carry = rest
         use(z, plane[0:band] + shift_down(plane[band : 2 * band]))
+        yield
+
+
+def planes_of(*args, **options):
+    for _ in plane_steps(*args, **options):
+        pass
 
 
 def inverter(inv_ref, idle_ref, bound, width, past_z, past_y, first, base=0):
@@ -289,7 +295,7 @@
     token_ref[...] = jnp.zeros(token_ref.shape, F32)
 
 
-def pack_far_kernel(place, after_ref, r0_ref, r1_ref, q0_ref, q1_ref):
+def pack_far_kernel(place, after_ref, r1_ref, r0_ref, q0_ref, q1_ref):
     pack_rows(place, borrowed_planes(place, r0_ref, r1_ref), FAR_TILES, q0_ref, q1_ref)
 
 
@@ -309,11 +315,6 @@
             use(kind, d, w, block)
 
 
-def split(values):
-    high = values.astype(BF16)
-    return high, (values - high.astype(F32)).astype(BF16)
-
-
 def fine_own_kernel(
     place, w_ref, wd_ref, bound_ref, hzy_ref, pair_ref, x_in, b_in, m_in, y0_ref, y1_ref,
     v0_ref, v1_ref, v2_ref, v3_ref, s_ref, b_ref, x_ref, u_ref, inv_ref, idle_ref, seam_ref, sc_ref,
@@ -375,7 +376,7 @@
 def fine_rest_kernel(
     place, w_ref, wd_ref, bound_ref, wr_ref, rzy_ref, rx_ref,
     v0_in, v1_in, v2_in, v3_in, s_in, b_mid, x_in, u_in, inv_in, idle_in, seam_ref, sc_ref,
-    b_in, r0_ref, r1_ref, y0_ref, y1_ref,
+    b_in, r1_ref, r0_ref, y1_ref, y0_ref,
     out_ref, rhs_ref, q0_ref, q1_ref,
     v0_ref, v1_ref, v2_ref, v3_ref, s_ref, b_ref, x_ref, u_ref, inv_ref, idle_ref,
 ):
@@ -405,23 +406,30 @@
     state.update({w: (x_in, u_in, w - 4) for w in range(4, 12)})
     near = (v0_in, v1_in, v2_in, v3_in)
     far = (v0_ref, v1_ref, v2_ref, v3_ref)
-    for level, factors in enumerate(chebyshev_factors()):
+    all_factors = chebyshev_factors()
+
+    def run(level, lo, hi, **seam):
         target = far[level + 1]
 
         def use(w, plane):
             xs, us, z = state[w]
             update = None if level == 0 else us[z]
             x_ref[w], u_ref[w] = advance(
-                plane, loads(w), xs[z], update, inverse(w), idles(w), factors
+                plane, loads(w), xs[z], update, inverse(w), idles(w), all_factors[level]
             )
             state[w] = (x_ref, u_ref, w)
             target[w] = shifted_nodes(x_ref[w], width)
 
-        product = layer_operator(
-            w_ref, either(near[level], far[level], 4 + level, 11 - level), scales
-        )
-        planes_of(1 + level, 4 + level, product, use, above=seam_ref[2 * level])
-        planes_of(11 - level, 14 - level, product, use, below=seam_ref[2 * level + 1])
+        nodes = either(near[level], far[level], 4 + level, 11 - level)
+        return plane_steps(lo, hi, layer_operator(w_ref, nodes, scales), use, **seam)
+
+    low = [run(k, 1 + k, 4 + k, above=seam_ref[2 * k]) for k in range(CHEB)]
+    high = [run(k, 11 - k, 14 - k, below=seam_ref[2 * k + 1]) for k in range(CHEB)]
+    for k in range(CHEB):
+        for _ in low[k]:
+            pass
+        for _ in high[k]:
+            pass
 
     head = iota((8, width), 0) < 4
     parts = []
@@ -446,7 +454,7 @@
         out[9:12] = sc_ref[pl.ds(up, 3)].astype(BF16)
 
 
-def pack_coarse_kernel(place, rhs_ref, sc_ref, r0_ref, r1_ref, full_ref, q0_ref, q1_ref):
+def pack_coarse_kernel(place, rhs_ref, sc_ref, r1_ref, r0_ref, full_ref, q0_ref, q1_ref):
     odd = place[0] == 1
     even_y = place[1] == 0
     head = iota(rhs_ref.shape[1:], 0) < 4
@@ -487,8 +495,8 @@
 
 
 def coarse_kernel(
-    place, w_ref, wd_ref, bound_ref, py_ref, px_ref, full_ref, y0_ref, y1_ref, smooth_ref, out_hbm,
-    v_ref, s_ref, b_ref, x_ref, u_ref, inv_ref, idle_ref, out_ref, sem,
+    place, w_ref, wd_ref, bound_ref, py_ref, px_ref, full_ref, y1_ref, y0_ref, smooth_ref, out_hbm,
+    v_ref, v1_ref, v2_ref, s_ref, b_ref, x_ref, u_ref, inv_ref, idle_ref, out_ref, sem,
 ):
     half = full_ref.shape[-1]
     width = 2 * half
@@ -514,32 +522,37 @@
     def scales(layer):
         return s_ref[layer]
 
-    planes_of(
-        1, 9, diagonal_operator(wd_ref, scales),
-        inverter(inv_ref, idle_ref, bound, half, place[2], place[3], 7),
-    )
     factors = chebyshev_factors()
-    for z in range(1, 10):
+    levels = (v_ref, v1_ref, v2_ref)
+    invert = inverter(inv_ref, idle_ref, bound, half, place[2], place[3], 7)
+
+    def start(z, diag):
+        invert(z, diag)
         update = factors[0][1] * (inv_ref[z] * b_ref[z])
         u_ref[z] = update
         x_ref[z] = update
         v_ref[z] = shifted_nodes(update, half)
-    product = layer_operator(w_ref, lambda z: v_ref[z], scales)
-    for level in (1, 2):
-
+
+    def run(level, lo, hi):
         def use(z, plane):
             x_ref[z], u_ref[z] = advance(
                 plane, b_ref[z], x_ref[z], u_ref[z], inv_ref[z], idle_ref[z], factors[level]
             )
-            v_ref[z] = shifted_nodes(x_ref[z], half)
-
-        planes_of(1 + level, 9 - level if level == 1 else 7, product, use)
-
-    coarse = jnp.concatenate([v_ref[3 + k, 0:BAND] for k in range(5)], axis=0)
+            levels[level][z] = shifted_nodes(x_ref[z], half)
+
+        nodes = levels[level - 1]
+        return plane_steps(lo, hi, layer_operator(w_ref, lambda z: nodes[z], scales), use)
+
+    steps = (
+        plane_steps(1, 9, diagonal_operator(wd_ref, scales), start), run(1, 2, 8), run(2, 3, 7)
+    )
+    for k in (0,) * 9 + (1,) * 7 + (2,) * 5:
+        next(steps[k])
+
+    coarse = jnp.concatenate([v2_ref[3 + k, 0:BAND] for k in range(5)], axis=0)
     rows = jnp.dot(py_ref[...], coarse, preferred_element_type=F32)
-    high, low = split(rows)
-    wide = jnp.dot(jnp.concatenate([high, low], axis=0), px_ref[...], preferred_element_type=F32)
-    wide = (wide[0:120] + wide[120:240]).reshape(5, 3, 8, width)
+    wide = jnp.dot(rows.astype(BF16), px_ref[...], preferred_element_type=F32)
+    wide = wide.reshape(5, 3, 8, width)
     copies = []
     for z in range(8):
         k = z // 2
@@ -627,7 +640,7 @@
     )(stiff, token)
 
     packet = shape((len(FAR_TILES), 8, width), BF16)
-    q0, q1 = call(pack_far_kernel, [packet, packet], 3, name="pack_far")(bound, r0, r1)
+    q0, q1 = call(pack_far_kernel, [packet, packet], 3, name="pack_far")(bound, r1, r0)
     yf1 = swap(q1, "gy", 1)
     yf0 = swap(q0, "gy", 0)
     def field(count, rows, dtype):
@@ -648,7 +661,7 @@
         23,
         [pltpu.VMEM(*field(16, *kind)) for kind in kinds],
         name="fine_rest",
-    )(w, wd, bound, wr, rzy, rx, *middle, scale, applied_load, r0, r1, yf0, yf1)
+    )(w, wd, bound, wr, rzy, rx, *middle, scale, applied_load, r1, r0, yf1, yf0)
     r1 = swap(q1, "gz", 1)
     r0 = swap(q0, "gz", 0)
     packet = shape((20, 8, half), BF16)
@@ -657,7 +670,7 @@
         [shape((40, 8, half), F32), packet, packet],
         4,
         name="pack_coarse",
-    )(rhs, scale, r0, r1)
+    )(rhs, scale, r1, r0)
     y1 = swap(q1, "gy", 1)
     y0 = swap(q0, "gy", 0)
     coarse_plane = pltpu.VMEM((11, BAND, half), F32)
@@ -666,6 +679,8 @@
         shape(start_field.shape, F32),
         9,
         [
+            pltpu.VMEM((11, 2 * BAND, half), BF16),
+            pltpu.VMEM((11, 2 * BAND, half), BF16),
             pltpu.VMEM((11, 2 * BAND, half), BF16),
             pltpu.VMEM((11, 2 * ROWS, half), BF16),
             coarse_plane,
@@ -678,7 +693,7 @@
         ],
         name="coarse",
         out_space=pltpu.HBM,
-    )(w, wd, bound, py, px, full, y0, y1, smoothed)
+    )(w, wd, bound, py, px, full, y1, y0, smoothed)
 
 
 def solution(mesh):

time: 43.4 us -> 42.9 us (0.988)
  transfers between devices with their start and end apart: 10 -> 10, of which waited for: 3 -> 4; matrix products, arithmetic and copies ran while one was open for 0% -> 0% of each run, Pallas kernels for 10% -> 11%
where the time goes in v5:
time: 42.9 us; the launch traced here: 42.7 us
  starting transfers between devices  23.7 us (55%)
  Pallas kernels  13.4 us (31%)
  waiting for transfers between devices  5.43 us (13%)
    ppermute x10, starting transfers between devices, swap(): return lax.ppermute(array, axis, pairs)  23.7 us
    ppermute x10, waiting for transfers between devices, swap(): return lax.ppermute(array, axis, pairs)  5.43 us
    pallas_call x1, Pallas kernels, body(): call(fine_rest_kernel, [shape(start_field.shape, F32), shape((15, 8, half...  4.49 us
    pallas_call x1, Pallas kernels, body(): call(fine_own_kernel, [shape(*field(8, *kind)) for kind in kinds] + [shap...  3.13 us
    pallas_call x1, Pallas kernels, body(): call(coarse_kernel, shape(start_field.shape, F32), 9, [pltpu.VMEM((11, 2...  2.93 us
    pallas_call x1, Pallas kernels, body(): call(pack_z_kernel, [packet, packet] + [shape(a.shape, a.dtype) for a in...  1.37 us
    pallas_call x1, Pallas kernels, body(): call(matrices_kernel, [shape((4 * BAND, 8 * BAND), BF16), shape((4 * BAND...  1.08 us
  transfers between devices with their start and end apart: 10, of which 4 were waited for; matrix products, arithmetic and copies ran while one was open for 0% of the time, Pallas kernels for 11%

profile of v5, /device:TPU:7, one launch (start us, length us, event | category | flops | bytes accessed | tf_op | source)
XLA Modules:
  0.0 42.7 jit_solution(13658209374800174019)
XLA Ops:
  0.0 1.4 %pack_z.1 = (bf16[25,8,512]{2,1,0:T(8,128)(2,1)S(1)}, bf16[25,8,512]{2,1,0:T(8,128)(2,1)S(1)}, f32[3,8,8,512]{3,2,1,0:T(8,128)S(1)}, f32[3,8,8,512]{3,2,1,0:T(8,...) custom-call(f32[3,8,8,512]{3,2,1,0:T(8,128)} %refs_0_.1, f32[3,8,8,512]{3,2,1,0:T(8,128)} %refs_1_.1, ...), custom_call_target="tpu_custom_call" | custom-call | tf_op jit(solution)/shard_map/pack_z/pallas_call | solution.py:607
  1.4 4.9 %collective-permute-start.2 = (bf16[25,8,512]{2,1,0:T(8,128)(2,1)S(1)}, bf16[25,8,512]{2,1,0:T(8,128)(2,1)S(1)}, u32[]{:S(2)}, u32[]{:S(2)}) collective-permute-start(bf16[25,8,512]{2,1,0:T(8,128)(2,1)S(1)} %get-tuple-element.74), channel_id=1, source_target_pairs={{8,16},{16,8},{24,32},{32,24},{40,48},{48,40},{56,64},{64,56},{72,... | collective-permute-start | bytes 614408 | tf_op jit(solution)/shard_map/ppermute | solution.py:572
  6.3 0.1 collective-permute-start.3
  6.4 0.1 pack_own.1
  6.5 1.0 %collective-permute-start = (bf16[28,8,512]{2,1,0:T(8,128)(2,1)S(1)}, bf16[28,8,512]{2,1,0:T(8,128)(2,1)S(1)}, u32[]{:S(2)}, u32[]{:S(2)}) collective-permute-start(bf16[28,8,512]{2,1,0:T(8,128)(2,1)S(1)} %get-tuple-element.60), channel_id=1, source_target_pairs={{0,1},{1,0},{2,3},{3,2},{4,5},{5,4},{6,7},{7,6},{8,9},{9,8},{10,11... | collective-permute-start | bytes 688136 | tf_op jit(solution)/shard_map/ppermute | solution.py:572
  7.5 3.4 %collective-permute-start.1 = (bf16[28,8,512]{2,1,0:T(8,128)(2,1)S(1)}, bf16[28,8,512]{2,1,0:T(8,128)(2,1)S(1)}, u32[]{:S(2)}, u32[]{:S(2)}) collective-permute-start(bf16[28,8,512]{2,1,0:T(8,128)(2,1)S(1)} %get-tuple-element.61), channel_id=1, source_target_pairs={{1,2},{2,1},{3,4},{4,3},{5,6},{6,5},{9,10},{10,9},{11,12},{12,11},... | collective-permute-start | bytes 688136 | tf_op jit(solution)/shard_map/ppermute | solution.py:572
  11.0 1.1 %matrices.1 = (bf16[192,384]{1,0:T(8,128)(2,1)S(1)}, bf16[192,32]{1,0:T(8,128)(2,1)S(1)}, f32[8,128]{1,0:T(8,128)S(1)}, bf16[96,384]{1,0:T(8,128)(2,1)S(1)}, bf1...) custom-call(bf16[24,24]{1,0:T(8,128)(2,1)S(1)} %get-tuple-element.45, ...), custom_call_target="tpu_custom_call" | custom-call | tf_op jit(solution)/shard_map/matrices/pallas_call | solution.py:623
  12.1 0.0 collective-permute-done.2.refs_1_.refs_19_
  12.1 0.0 collective-permute-done.3.refs_2_.refs_20_
  12.1 0.2 pack_far.1
  12.3 5.2 %collective-permute-start.4 = (bf16[25,8,512]{2,1,0:T(8,128)(2,1)S(1)}, bf16[25,8,512]{2,1,0:T(8,128)(2,1)S(1)}, u32[]{:S(2)}, u32[]{:S(2)}) collective-permute-start(bf16[25,8,512]{2,1,0:T(8,128)(2,1)S(1)} %get-tuple-element.76), channel_id=1, source_target_pairs={{1,2},{2,1},{3,4},{4,3},{5,6},{6,5},{9,10},{10,9},{11,12},{12,11},... | collective-permute-start | bytes 614408 | tf_op jit(solution)/shard_map/ppermute | solution.py:572
  17.5 0.1 collective-permute-start.5
  17.6 0.0 collective-permute-done.refs_8_
  17.6 0.0 collective-permute-done.1.refs_9_
  17.6 3.1 %fine_own.1 = (bf16[8,96,512]{2,1,0:T(8,128)(2,1)S(1)}, bf16[8,96,512]{2,1,0:T(8,128)(2,1)S(1)}, bf16[8,96,512]{2,1,0:T(8,128)(2,1)S(1)}, bf16[8,96,512]{2,1,0:T...) custom-call(bf16[192,384]{1,0:T(8,128)(2,1)S(1)} %get-tuple-element., ...), custom_call_target="tpu_custom_call" | custom-call | tf_op jit(solution)/shard_map/fine_own/pallas_call | solution.py:650
  20.7 0.2 collective-permute-done.4.refs_21_
  20.9 0.0 collective-permute-done.5.refs_22_
  20.9 4.5 %fine_rest.1 = (f32[3,8,8,512]{3,2,1,0:T(8,128)S(1)}, f32[15,8,256]{2,1,0:T(8,128)S(1)}, bf16[12,8,256]{2,1,0:T(8,128)(2,1)S(1)}, bf16[12,8,256]{2,1,0:T(8,128)(2,1)S(1)}) custom-call(bf16[192,384]{1,0:T(8,128)(2,1)S(1)} %get-tuple-element.50.refs_0_, bf16[192,32]{1,0:T(8,128)(2,1)S(1)} %get-tuple-element.51.refs_1_, ...), custom_call_target="tpu_custom_call" | custom-call | tf_op jit(solution)/shard_map/fine_rest/pallas_call | solution.py:658
  25.4 3.9 %collective-permute-start.6 = (bf16[12,8,256]{2,1,0:T(8,128)(2,1)S(1)}, bf16[12,8,256]{2,1,0:T(8,128)(2,1)S(1)}, u32[]{:S(2)}, u32[]{:S(2)}) collective-permute-start(bf16[12,8,256]{2,1,0:T(8,128)(2,1)S(1)} %get-tuple-element.79), channel_id=1, source_target_pairs={{8,16},{16,8},{24,32},{32,24},{40,48},{48,40},{56,64},{64,56},{72,... | collective-permute-start | bytes 147464 | tf_op jit(solution)/shard_map/ppermute | solution.py:572
  29.3 0.1 collective-permute-start.7
  29.4 2.9 %collective-permute-done.6.refs_2_ = bf16[12,8,256]{2,1,0:T(8,128)(2,1)S(1)} collective-permute-done((bf16[12,8,256]{2,1,0:T(8,128)(2,1)S(1)}, bf16[12,8,256]{2,1,0:T(8,128)(2,1)S(1)}, u32[]{:S(2)}, u32[]{:S(2)}) %collective-permute-start.6) | collective-permute-done | bytes 49184 | tf_op jit(solution)/shard_map/ppermute | solution.py:572
  32.4 0.3 collective-permute-done.7.refs_3_
  32.7 0.1 pack_coarse.1
  32.7 4.9 %collective-permute-start.8 = (bf16[20,8,256]{2,1,0:T(8,128)(2,1)S(1)}, bf16[20,8,256]{2,1,0:T(8,128)(2,1)S(1)}, u32[]{:S(2)}, u32[]{:S(2)}) collective-permute-start(bf16[20,8,256]{2,1,0:T(8,128)(2,1)S(1)} %get-tuple-element.82), channel_id=1, source_target_pairs={{1,2},{2,1},{3,4},{4,3},{5,6},{6,5},{9,10},{10,9},{11,12},{12,11},... | collective-permute-start | bytes 245768 | tf_op jit(solution)/shard_map/ppermute | solution.py:572
  37.6 0.1 collective-permute-start.9
  37.7 2.0 %collective-permute-done.8.refs_6_ = bf16[20,8,256]{2,1,0:T(8,128)(2,1)S(1)} collective-permute-done((bf16[20,8,256]{2,1,0:T(8,128)(2,1)S(1)}, bf16[20,8,256]{2,1,0:T(8,128)(2,1)S(1)}, u32[]{:S(2)}, u32[]{:S(2)}) %collective-permute-start.8) | collective-permute-done | bytes 81952 | tf_op jit(solution)/shard_map/ppermute | solution.py:572
  39.8 0.0 collective-permute-done.9.refs_7_
  39.8 2.9 %coarse.1 = f32[3,8,8,512]{3,2,1,0:T(8,128)} custom-call(bf16[192,384]{1,0:T(8,128)(2,1)S(1)} %get-tuple-element.50.refs_0_, bf16[192,32]{1,0:T(8,128)(2,1)S(1)} %get-tuple-element.51.refs_1_, f32[8,128]{1,0:T(8,128)S(1)} %get-tuple-element.52.refs_2_.refs_0_, bf16[120,240]{1,0:T(8,128)(2,1)S(1)} %get-tuple-element.53.refs_3_, ...), custom_call_target="tpu_custom_call" | custom-call | tf_op jit(solution)/shard_map/coarse/pallas_call | solution.py:677
Async XLA Ops:
  1.4 10.7 %collective-permute-start.2 = (bf16[25,8,512]{2,1,0:T(8,128)(2,1)S(1)}, bf16[25,8,512]{2,1,0:T(8,128)(2,1)S(1)}, u32[]{:S(2)}, u32[]{:S(2)}) collective-permute-start(bf16[25,8,512]{2,1,0:T(8,128)(2,1)S(1)} %get-tuple-element.74), channel_id=1, source_target_pairs={{8,16},{16,8},{24,32},{32,24},{40,48},{48,40},{56,64},{64,56},{72,... | collective-permute-start | bytes 614408 | tf_op jit(solution)/shard_map/ppermute | solution.py:572
  6.3 5.8 %collective-permute-start.3 = (bf16[25,8,512]{2,1,0:T(8,128)(2,1)S(1)}, bf16[25,8,512]{2,1,0:T(8,128)(2,1)S(1)}, u32[]{:S(2)}, u32[]{:S(2)}) collective-permute-start(bf16[25,8,512]{2,1,0:T(8,128)(2,1)S(1)} %get-tuple-element.75), channel_id=1, source_target_pairs={{0,8},{8,0},{16,24},{24,16},{32,40},{40,32},{48,56},{56,48},{64,72... | collective-permute-start | bytes 614408 | tf_op jit(solution)/shard_map/ppermute | solution.py:572
  6.5 11.1 %collective-permute-start = (bf16[28,8,512]{2,1,0:T(8,128)(2,1)S(1)}, bf16[28,8,512]{2,1,0:T(8,128)(2,1)S(1)}, u32[]{:S(2)}, u32[]{:S(2)}) collective-permute-start(bf16[28,8,512]{2,1,0:T(8,128)(2,1)S(1)} %get-tuple-element.60), channel_id=1, source_target_pairs={{0,1},{1,0},{2,3},{3,2},{4,5},{5,4},{6,7},{7,6},{8,9},{9,8},{10,11... | collective-permute-start | bytes 688136 | tf_op jit(solution)/shard_map/ppermute | solution.py:572
  7.5 10.0 %collective-permute-start.1 = (bf16[28,8,512]{2,1,0:T(8,128)(2,1)S(1)}, bf16[28,8,512]{2,1,0:T(8,128)(2,1)S(1)}, u32[]{:S(2)}, u32[]{:S(2)}) collective-permute-start(bf16[28,8,512]{2,1,0:T(8,128)(2,1)S(1)} %get-tuple-element.61), channel_id=1, source_target_pairs={{1,2},{2,1},{3,4},{4,3},{5,6},{6,5},{9,10},{10,9},{11,12},{12,11},... | collective-permute-start | bytes 688136 | tf_op jit(solution)/shard_map/ppermute | solution.py:572
  12.3 8.6 %collective-permute-start.4 = (bf16[25,8,512]{2,1,0:T(8,128)(2,1)S(1)}, bf16[25,8,512]{2,1,0:T(8,128)(2,1)S(1)}, u32[]{:S(2)}, u32[]{:S(2)}) collective-permute-start(bf16[25,8,512]{2,1,0:T(8,128)(2,1)S(1)} %get-tuple-element.76), channel_id=1, source_target_pairs={{1,2},{2,1},{3,4},{4,3},{5,6},{6,5},{9,10},{10,9},{11,12},{12,11},... | collective-permute-start | bytes 614408 | tf_op jit(solution)/shard_map/ppermute | solution.py:572
  17.5 3.4 %collective-permute-start.5 = (bf16[25,8,512]{2,1,0:T(8,128)(2,1)S(1)}, bf16[25,8,512]{2,1,0:T(8,128)(2,1)S(1)}, u32[]{:S(2)}, u32[]{:S(2)}) collective-permute-start(bf16[25,8,512]{2,1,0:T(8,128)(2,1)S(1)} %get-tuple-element.77), channel_id=1, source_target_pairs={{0,1},{1,0},{2,3},{3,2},{4,5},{5,4},{6,7},{7,6},{8,9},{9,8},{10,11... | collective-permute-start | bytes 614408 | tf_op jit(solution)/shard_map/ppermute | solution.py:572
  25.4 6.9 %collective-permute-start.6 = (bf16[12,8,256]{2,1,0:T(8,128)(2,1)S(1)}, bf16[12,8,256]{2,1,0:T(8,128)(2,1)S(1)}, u32[]{:S(2)}, u32[]{:S(2)}) collective-permute-start(bf16[12,8,256]{2,1,0:T(8,128)(2,1)S(1)} %get-tuple-element.79), channel_id=1, source_target_pairs={{8,16},{16,8},{24,32},{32,24},{40,48},{48,40},{56,64},{64,56},{72,... | collective-permute-start | bytes 147464 | tf_op jit(solution)/shard_map/ppermute | solution.py:572
  29.3 3.3 %collective-permute-start.7 = (bf16[12,8,256]{2,1,0:T(8,128)(2,1)S(1)}, bf16[12,8,256]{2,1,0:T(8,128)(2,1)S(1)}, u32[]{:S(2)}, u32[]{:S(2)}) collective-permute-start(bf16[12,8,256]{2,1,0:T(8,128)(2,1)S(1)} %get-tuple-element.80), channel_id=1, source_target_pairs={{0,8},{8,0},{16,24},{24,16},{32,40},{40,32},{48,56},{56,48},{64,72... | collective-permute-start | bytes 147464 | tf_op jit(solution)/shard_map/ppermute | solution.py:572
  32.7 7.0 %collective-permute-start.8 = (bf16[20,8,256]{2,1,0:T(8,128)(2,1)S(1)}, bf16[20,8,256]{2,1,0:T(8,128)(2,1)S(1)}, u32[]{:S(2)}, u32[]{:S(2)}) collective-permute-start(bf16[20,8,256]{2,1,0:T(8,128)(2,1)S(1)} %get-tuple-element.82), channel_id=1, source_target_pairs={{1,2},{2,1},{3,4},{4,3},{5,6},{6,5},{9,10},{10,9},{11,12},{12,11},... | collective-permute-start | bytes 245768 | tf_op jit(solution)/shard_map/ppermute | solution.py:572
  37.6 2.1 %collective-permute-start.9 = (bf16[20,8,256]{2,1,0:T(8,128)(2,1)S(1)}, bf16[20,8,256]{2,1,0:T(8,128)(2,1)S(1)}, u32[]{:S(2)}, u32[]{:S(2)}) collective-permute-start(bf16[20,8,256]{2,1,0:T(8,128)(2,1)S(1)} %get-tuple-element.83), channel_id=1, source_target_pairs={{0,1},{1,0},{2,3},{3,2},{4,5},{5,4},{6,7},{7,6},{8,9},{9,8},{10,11... | collective-permute-start | bytes 245768 | tf_op jit(solution)/shard_map/ppermute | solution.py:572

commit v6 on v5

--- a/solution.py
+++ b/solution.py
@@ -221,19 +221,28 @@
     place, x_hbm, b_hbm, m_hbm, e_hbm, q0_ref, q1_ref, x_ref, b_ref, m_ref, e_ref, sem
 ):
     even = 1 - place[0]
-    pairs = [(m_hbm, m_ref), (e_hbm, e_ref)]
+    pairs = []
     for d in range(3):
-        pairs += [(x_hbm.at[d], x_ref.at[d]), (b_hbm.at[d], b_ref.at[d])]
+        pairs += [(x_hbm.at[d], x_ref.at[d])]
+    for d in range(3):
+        pairs += [(b_hbm.at[d], b_ref.at[d])]
+    pairs += [(m_hbm, m_ref), (e_hbm, e_ref)]
     copies = [pltpu.make_async_copy(src, dst, sem.at[i]) for i, (src, dst) in enumerate(pairs)]
     for copy in copies:
         copy.start()
-    for copy in copies:
-        copy.wait()
-    for out, up in ((q0_ref, even), (q1_ref, 1 - even)):
-        for d in range(3):
+    outs = ((q0_ref, even), (q1_ref, 1 - even))
+    for d in range(3):
+        copies[d].wait()
+        for out, up in outs:
             out[4 * d : 4 * d + 4] = x_ref[d, pl.ds(4 * up, 4)].astype(BF16)
+    for d in range(3):
+        copies[3 + d].wait()
+        for out, up in outs:
             out[12 + 3 * d : 15 + 3 * d] = b_ref[d, pl.ds(5 * up, 3)].astype(BF16)
+    copies[6].wait()
+    for out, up in outs:
         out[21:25] = m_ref[pl.ds(4 * up, 4)].astype(F32).astype(BF16)
+    copies[7].wait()
 
 
 def own_planes(x_ref, b_ref, m_ref):

time: 42.9 us -> 42.9 us (level)
  no operation moved by 1% of the time
where the time goes in v6:
time: 42.9 us; the launch traced here: 42.6 us
  starting transfers between devices  23.7 us (55%)
  Pallas kernels  13.3 us (31%)
  waiting for transfers between devices  5.43 us (13%)
    ppermute x10, starting transfers between devices, swap(): return lax.ppermute(array, axis, pairs)  23.7 us
    ppermute x10, waiting for transfers between devices, swap(): return lax.ppermute(array, axis, pairs)  5.43 us
    pallas_call x1, Pallas kernels, body(): call(fine_rest_kernel, [shape(start_field.shape, F32), shape((15, 8, half...  4.49 us
    pallas_call x1, Pallas kernels, body(): call(fine_own_kernel, [shape(*field(8, *kind)) for kind in kinds] + [shap...  3.13 us
    pallas_call x1, Pallas kernels, body(): call(coarse_kernel, shape(start_field.shape, F32), 9, [pltpu.VMEM((11, 2...  2.93 us
    pallas_call x1, Pallas kernels, body(): call(pack_z_kernel, [packet, packet] + [shape(a.shape, a.dtype) for a in...  1.32 us
    pallas_call x1, Pallas kernels, body(): call(matrices_kernel, [shape((4 * BAND, 8 * BAND), BF16), shape((4 * BAND...  1.08 us
  transfers between devices with their start and end apart: 10, of which 4 were waited for; matrix products, arithmetic and copies ran while one was open for 0% of the time, Pallas kernels for 11%

profile of v6, /device:TPU:7, one launch (start us, length us, event | category | flops | bytes accessed | tf_op | source)
XLA Modules:
  0.0 42.6 jit_solution(1997270239499926551)
XLA Ops:
  0.0 1.3 %pack_z.1 = (bf16[25,8,512]{2,1,0:T(8,128)(2,1)S(1)}, bf16[25,8,512]{2,1,0:T(8,128)(2,1)S(1)}, f32[3,8,8,512]{3,2,1,0:T(8,128)S(1)}, f32[3,8,8,512]{3,2,1,0:T(8,...) custom-call(f32[3,8,8,512]{3,2,1,0:T(8,128)} %refs_0_.1, f32[3,8,8,512]{3,2,1,0:T(8,128)} %refs_1_.1, ...), custom_call_target="tpu_custom_call" | custom-call | tf_op jit(solution)/shard_map/pack_z/pallas_call | solution.py:616
  1.3 4.9 %collective-permute-start.2 = (bf16[25,8,512]{2,1,0:T(8,128)(2,1)S(1)}, bf16[25,8,512]{2,1,0:T(8,128)(2,1)S(1)}, u32[]{:S(2)}, u32[]{:S(2)}) collective-permute-start(bf16[25,8,512]{2,1,0:T(8,128)(2,1)S(1)} %get-tuple-element.74), channel_id=1, source_target_pairs={{8,16},{16,8},{24,32},{32,24},{40,48},{48,40},{56,64},{64,56},{72,... | collective-permute-start | bytes 614408 | tf_op jit(solution)/shard_map/ppermute | solution.py:581
  6.2 0.1 collective-permute-start.3
  6.3 0.1 pack_own.1
  6.5 1.0 %collective-permute-start = (bf16[28,8,512]{2,1,0:T(8,128)(2,1)S(1)}, bf16[28,8,512]{2,1,0:T(8,128)(2,1)S(1)}, u32[]{:S(2)}, u32[]{:S(2)}) collective-permute-start(bf16[28,8,512]{2,1,0:T(8,128)(2,1)S(1)} %get-tuple-element.60), channel_id=1, source_target_pairs={{0,1},{1,0},{2,3},{3,2},{4,5},{5,4},{6,7},{7,6},{8,9},{9,8},{10,11... | collective-permute-start | bytes 688136 | tf_op jit(solution)/shard_map/ppermute | solution.py:581
  7.5 3.4 %collective-permute-start.1 = (bf16[28,8,512]{2,1,0:T(8,128)(2,1)S(1)}, bf16[28,8,512]{2,1,0:T(8,128)(2,1)S(1)}, u32[]{:S(2)}, u32[]{:S(2)}) collective-permute-start(bf16[28,8,512]{2,1,0:T(8,128)(2,1)S(1)} %get-tuple-element.61), channel_id=1, source_target_pairs={{1,2},{2,1},{3,4},{4,3},{5,6},{6,5},{9,10},{10,9},{11,12},{12,11},... | collective-permute-start | bytes 688136 | tf_op jit(solution)/shard_map/ppermute | solution.py:581
  10.9 1.1 %matrices.1 = (bf16[192,384]{1,0:T(8,128)(2,1)S(1)}, bf16[192,32]{1,0:T(8,128)(2,1)S(1)}, f32[8,128]{1,0:T(8,128)S(1)}, bf16[96,384]{1,0:T(8,128)(2,1)S(1)}, bf1...) custom-call(bf16[24,24]{1,0:T(8,128)(2,1)S(1)} %get-tuple-element.45, ...), custom_call_target="tpu_custom_call" | custom-call | tf_op jit(solution)/shard_map/matrices/pallas_call | solution.py:632
  12.0 0.0 collective-permute-done.2.refs_1_.refs_19_
  12.0 0.0 collective-permute-done.3.refs_2_.refs_20_
  12.0 0.2 pack_far.1
  12.2 5.2 %collective-permute-start.4 = (bf16[25,8,512]{2,1,0:T(8,128)(2,1)S(1)}, bf16[25,8,512]{2,1,0:T(8,128)(2,1)S(1)}, u32[]{:S(2)}, u32[]{:S(2)}) collective-permute-start(bf16[25,8,512]{2,1,0:T(8,128)(2,1)S(1)} %get-tuple-element.76), channel_id=1, source_target_pairs={{1,2},{2,1},{3,4},{4,3},{5,6},{6,5},{9,10},{10,9},{11,12},{12,11},... | collective-permute-start | bytes 614408 | tf_op jit(solution)/shard_map/ppermute | solution.py:581
  17.4 0.1 collective-permute-start.5
  17.5 0.0 collective-permute-done.refs_8_
  17.5 0.0 collective-permute-done.1.refs_9_
  17.6 3.1 %fine_own.1 = (bf16[8,96,512]{2,1,0:T(8,128)(2,1)S(1)}, bf16[8,96,512]{2,1,0:T(8,128)(2,1)S(1)}, bf16[8,96,512]{2,1,0:T(8,128)(2,1)S(1)}, bf16[8,96,512]{2,1,0:T...) custom-call(bf16[192,384]{1,0:T(8,128)(2,1)S(1)} %get-tuple-element., ...), custom_call_target="tpu_custom_call" | custom-call | tf_op jit(solution)/shard_map/fine_own/pallas_call | solution.py:659
  20.7 0.2 collective-permute-done.4.refs_21_
  20.9 0.0 collective-permute-done.5.refs_22_
  20.9 4.5 %fine_rest.1 = (f32[3,8,8,512]{3,2,1,0:T(8,128)S(1)}, f32[15,8,256]{2,1,0:T(8,128)S(1)}, bf16[12,8,256]{2,1,0:T(8,128)(2,1)S(1)}, bf16[12,8,256]{2,1,0:T(8,128)(2,1)S(1)}) custom-call(bf16[192,384]{1,0:T(8,128)(2,1)S(1)} %get-tuple-element.50.refs_0_, bf16[192,32]{1,0:T(8,128)(2,1)S(1)} %get-tuple-element.51.refs_1_, ...), custom_call_target="tpu_custom_call" | custom-call | tf_op jit(solution)/shard_map/fine_rest/pallas_call | solution.py:667
  25.4 3.9 %collective-permute-start.6 = (bf16[12,8,256]{2,1,0:T(8,128)(2,1)S(1)}, bf16[12,8,256]{2,1,0:T(8,128)(2,1)S(1)}, u32[]{:S(2)}, u32[]{:S(2)}) collective-permute-start(bf16[12,8,256]{2,1,0:T(8,128)(2,1)S(1)} %get-tuple-element.79), channel_id=1, source_target_pairs={{8,16},{16,8},{24,32},{32,24},{40,48},{48,40},{56,64},{64,56},{72,... | collective-permute-start | bytes 147464 | tf_op jit(solution)/shard_map/ppermute | solution.py:581
  29.3 0.1 collective-permute-start.7
  29.4 2.9 %collective-permute-done.6.refs_2_ = bf16[12,8,256]{2,1,0:T(8,128)(2,1)S(1)} collective-permute-done((bf16[12,8,256]{2,1,0:T(8,128)(2,1)S(1)}, bf16[12,8,256]{2,1,0:T(8,128)(2,1)S(1)}, u32[]{:S(2)}, u32[]{:S(2)}) %collective-permute-start.6) | collective-permute-done | bytes 49184 | tf_op jit(solution)/shard_map/ppermute | solution.py:581
  32.3 0.3 collective-permute-done.7.refs_3_
  32.6 0.1 pack_coarse.1
  32.7 4.9 %collective-permute-start.8 = (bf16[20,8,256]{2,1,0:T(8,128)(2,1)S(1)}, bf16[20,8,256]{2,1,0:T(8,128)(2,1)S(1)}, u32[]{:S(2)}, u32[]{:S(2)}) collective-permute-start(bf16[20,8,256]{2,1,0:T(8,128)(2,1)S(1)} %get-tuple-element.82), channel_id=1, source_target_pairs={{1,2},{2,1},{3,4},{4,3},{5,6},{6,5},{9,10},{10,9},{11,12},{12,11},... | collective-permute-start | bytes 245768 | tf_op jit(solution)/shard_map/ppermute | solution.py:581
  37.6 0.1 collective-permute-start.9
  37.7 2.0 %collective-permute-done.8.refs_6_ = bf16[20,8,256]{2,1,0:T(8,128)(2,1)S(1)} collective-permute-done((bf16[20,8,256]{2,1,0:T(8,128)(2,1)S(1)}, bf16[20,8,256]{2,1,0:T(8,128)(2,1)S(1)}, u32[]{:S(2)}, u32[]{:S(2)}) %collective-permute-start.8) | collective-permute-done | bytes 81952 | tf_op jit(solution)/shard_map/ppermute | solution.py:581
  39.7 0.0 collective-permute-done.9.refs_7_
  39.7 2.9 %coarse.1 = f32[3,8,8,512]{3,2,1,0:T(8,128)} custom-call(bf16[192,384]{1,0:T(8,128)(2,1)S(1)} %get-tuple-element.50.refs_0_, bf16[192,32]{1,0:T(8,128)(2,1)S(1)} %get-tuple-element.51.refs_1_, f32[8,128]{1,0:T(8,128)S(1)} %get-tuple-element.52.refs_2_.refs_0_, bf16[120,240]{1,0:T(8,128)(2,1)S(1)} %get-tuple-element.53.refs_3_, ...), custom_call_target="tpu_custom_call" | custom-call | tf_op jit(solution)/shard_map/coarse/pallas_call | solution.py:686
Async XLA Ops:
  1.3 10.7 %collective-permute-start.2 = (bf16[25,8,512]{2,1,0:T(8,128)(2,1)S(1)}, bf16[25,8,512]{2,1,0:T(8,128)(2,1)S(1)}, u32[]{:S(2)}, u32[]{:S(2)}) collective-permute-start(bf16[25,8,512]{2,1,0:T(8,128)(2,1)S(1)} %get-tuple-element.74), channel_id=1, source_target_pairs={{8,16},{16,8},{24,32},{32,24},{40,48},{48,40},{56,64},{64,56},{72,... | collective-permute-start | bytes 614408 | tf_op jit(solution)/shard_map/ppermute | solution.py:581
  6.2 5.8 %collective-permute-start.3 = (bf16[25,8,512]{2,1,0:T(8,128)(2,1)S(1)}, bf16[25,8,512]{2,1,0:T(8,128)(2,1)S(1)}, u32[]{:S(2)}, u32[]{:S(2)}) collective-permute-start(bf16[25,8,512]{2,1,0:T(8,128)(2,1)S(1)} %get-tuple-element.75), channel_id=1, source_target_pairs={{0,8},{8,0},{16,24},{24,16},{32,40},{40,32},{48,56},{56,48},{64,72... | collective-permute-start | bytes 614408 | tf_op jit(solution)/shard_map/ppermute | solution.py:581
  6.5 11.1 %collective-permute-start = (bf16[28,8,512]{2,1,0:T(8,128)(2,1)S(1)}, bf16[28,8,512]{2,1,0:T(8,128)(2,1)S(1)}, u32[]{:S(2)}, u32[]{:S(2)}) collective-permute-start(bf16[28,8,512]{2,1,0:T(8,128)(2,1)S(1)} %get-tuple-element.60), channel_id=1, source_target_pairs={{0,1},{1,0},{2,3},{3,2},{4,5},{5,4},{6,7},{7,6},{8,9},{9,8},{10,11... | collective-permute-start | bytes 688136 | tf_op jit(solution)/shard_map/ppermute | solution.py:581
  7.5 10.0 %collective-permute-start.1 = (bf16[28,8,512]{2,1,0:T(8,128)(2,1)S(1)}, bf16[28,8,512]{2,1,0:T(8,128)(2,1)S(1)}, u32[]{:S(2)}, u32[]{:S(2)}) collective-permute-start(bf16[28,8,512]{2,1,0:T(8,128)(2,1)S(1)} %get-tuple-element.61), channel_id=1, source_target_pairs={{1,2},{2,1},{3,4},{4,3},{5,6},{6,5},{9,10},{10,9},{11,12},{12,11},... | collective-permute-start | bytes 688136 | tf_op jit(solution)/shard_map/ppermute | solution.py:581
  12.2 8.6 %collective-permute-start.4 = (bf16[25,8,512]{2,1,0:T(8,128)(2,1)S(1)}, bf16[25,8,512]{2,1,0:T(8,128)(2,1)S(1)}, u32[]{:S(2)}, u32[]{:S(2)}) collective-permute-start(bf16[25,8,512]{2,1,0:T(8,128)(2,1)S(1)} %get-tuple-element.76), channel_id=1, source_target_pairs={{1,2},{2,1},{3,4},{4,3},{5,6},{6,5},{9,10},{10,9},{11,12},{12,11},... | collective-permute-start | bytes 614408 | tf_op jit(solution)/shard_map/ppermute | solution.py:581
  17.4 3.4 %collective-permute-start.5 = (bf16[25,8,512]{2,1,0:T(8,128)(2,1)S(1)}, bf16[25,8,512]{2,1,0:T(8,128)(2,1)S(1)}, u32[]{:S(2)}, u32[]{:S(2)}) collective-permute-start(bf16[25,8,512]{2,1,0:T(8,128)(2,1)S(1)} %get-tuple-element.77), channel_id=1, source_target_pairs={{0,1},{1,0},{2,3},{3,2},{4,5},{5,4},{6,7},{7,6},{8,9},{9,8},{10,11... | collective-permute-start | bytes 614408 | tf_op jit(solution)/shard_map/ppermute | solution.py:581
  25.4 6.9 %collective-permute-start.6 = (bf16[12,8,256]{2,1,0:T(8,128)(2,1)S(1)}, bf16[12,8,256]{2,1,0:T(8,128)(2,1)S(1)}, u32[]{:S(2)}, u32[]{:S(2)}) collective-permute-start(bf16[12,8,256]{2,1,0:T(8,128)(2,1)S(1)} %get-tuple-element.79), channel_id=1, source_target_pairs={{8,16},{16,8},{24,32},{32,24},{40,48},{48,40},{56,64},{64,56},{72,... | collective-permute-start | bytes 147464 | tf_op jit(solution)/shard_map/ppermute | solution.py:581
  29.3 3.3 %collective-permute-start.7 = (bf16[12,8,256]{2,1,0:T(8,128)(2,1)S(1)}, bf16[12,8,256]{2,1,0:T(8,128)(2,1)S(1)}, u32[]{:S(2)}, u32[]{:S(2)}) collective-permute-start(bf16[12,8,256]{2,1,0:T(8,128)(2,1)S(1)} %get-tuple-element.80), channel_id=1, source_target_pairs={{0,8},{8,0},{16,24},{24,16},{32,40},{40,32},{48,56},{56,48},{64,72... | collective-permute-start | bytes 147464 | tf_op jit(solution)/shard_map/ppermute | solution.py:581
  32.7 7.0 %collective-permute-start.8 = (bf16[20,8,256]{2,1,0:T(8,128)(2,1)S(1)}, bf16[20,8,256]{2,1,0:T(8,128)(2,1)S(1)}, u32[]{:S(2)}, u32[]{:S(2)}) collective-permute-start(bf16[20,8,256]{2,1,0:T(8,128)(2,1)S(1)} %get-tuple-element.82), channel_id=1, source_target_pairs={{1,2},{2,1},{3,4},{4,3},{5,6},{6,5},{9,10},{10,9},{11,12},{12,11},... | collective-permute-start | bytes 245768 | tf_op jit(solution)/shard_map/ppermute | solution.py:581
  37.6 2.1 %collective-permute-start.9 = (bf16[20,8,256]{2,1,0:T(8,128)(2,1)S(1)}, bf16[20,8,256]{2,1,0:T(8,128)(2,1)S(1)}, u32[]{:S(2)}, u32[]{:S(2)}) collective-permute-start(bf16[20,8,256]{2,1,0:T(8,128)(2,1)S(1)} %get-tuple-element.83), channel_id=1, source_target_pairs={{0,1},{1,0},{2,3},{3,2},{4,5},{5,4},{6,7},{7,6},{8,9},{9,8},{10,11... | collective-permute-start | bytes 245768 | tf_op jit(solution)/shard_map/ppermute | solution.py:581

commit v7 on v6

--- a/solution.py
+++ b/solution.py
@@ -325,7 +325,7 @@
 
 
 def fine_own_kernel(
-    place, w_ref, wd_ref, bound_ref, hzy_ref, pair_ref, x_in, b_in, m_in, y0_ref, y1_ref,
+    place, w_ref, wd_ref, bound_ref, hzy_ref, pair_ref, x_in, b_in, m_in, y1_ref, y0_ref,
     v0_ref, v1_ref, v2_ref, v3_ref, s_ref, b_ref, x_ref, u_ref, inv_ref, idle_ref, seam_ref, sc_ref,
 ):
     width = x_in.shape[-1]
@@ -662,7 +662,7 @@
         + [shape(*field(6, 2 * BAND, F32)), shape((4, 8, half), F32)],
         10,
         name="fine_own",
-    )(w, wd, bound, hzy, pair, start_field, applied_load, bone_mask, yn0, yn1)
+    )(w, wd, bound, hzy, pair, start_field, applied_load, bone_mask, yn1, yn0)
     packet = shape((12, 8, half), BF16)
     smoothed, rhs, q0, q1 = call(
         fine_rest_kernel,

time: 42.9 us -> 42.9 us (level)
  no operation moved by 1% of the time
where the time goes in v7:
time: 42.9 us; the launch traced here: 42.6 us
  starting transfers between devices  23.7 us (55%)
  Pallas kernels  13.3 us (31%)
  waiting for transfers between devices  5.44 us (13%)
    ppermute x10, starting transfers between devices, swap(): return lax.ppermute(array, axis, pairs)  23.7 us
    ppermute x10, waiting for transfers between devices, swap(): return lax.ppermute(array, axis, pairs)  5.44 us
    pallas_call x1, Pallas kernels, body(): call(fine_rest_kernel, [shape(start_field.shape, F32), shape((15, 8, half...  4.49 us
    pallas_call x1, Pallas kernels, body(): call(fine_own_kernel, [shape(*field(8, *kind)) for kind in kinds] + [shap...  3.12 us
    pallas_call x1, Pallas kernels, body(): call(coarse_kernel, shape(start_field.shape, F32), 9, [pltpu.VMEM((11, 2...  2.93 us
    pallas_call x1, Pallas kernels, body(): call(pack_z_kernel, [packet, packet] + [shape(a.shape, a.dtype) for a in...  1.32 us
    pallas_call x1, Pallas kernels, body(): call(matrices_kernel, [shape((4 * BAND, 8 * BAND), BF16), shape((4 * BAND...  1.08 us
  transfers between devices with their start and end apart: 10, of which 4 were waited for; matrix products, arithmetic and copies ran while one was open for 0% of the time, Pallas kernels for 11%

profile of v7, /device:TPU:7, one launch (start us, length us, event | category | flops | bytes accessed | tf_op | source)
XLA Modules:
  0.0 42.6 jit_solution(9197076591757065490)
XLA Ops:
  0.0 1.3 %pack_z.1 = (bf16[25,8,512]{2,1,0:T(8,128)(2,1)S(1)}, bf16[25,8,512]{2,1,0:T(8,128)(2,1)S(1)}, f32[3,8,8,512]{3,2,1,0:T(8,128)S(1)}, f32[3,8,8,512]{3,2,1,0:T(8,...) custom-call(f32[3,8,8,512]{3,2,1,0:T(8,128)} %refs_0_.1, f32[3,8,8,512]{3,2,1,0:T(8,128)} %refs_1_.1, ...), custom_call_target="tpu_custom_call" | custom-call | tf_op jit(solution)/shard_map/pack_z/pallas_call | solution.py:616
  1.3 4.9 %collective-permute-start.2 = (bf16[25,8,512]{2,1,0:T(8,128)(2,1)S(1)}, bf16[25,8,512]{2,1,0:T(8,128)(2,1)S(1)}, u32[]{:S(2)}, u32[]{:S(2)}) collective-permute-start(bf16[25,8,512]{2,1,0:T(8,128)(2,1)S(1)} %get-tuple-element.74), channel_id=1, source_target_pairs={{8,16},{16,8},{24,32},{32,24},{40,48},{48,40},{56,64},{64,56},{72,... | collective-permute-start | bytes 614408 | tf_op jit(solution)/shard_map/ppermute | solution.py:581
  6.2 0.1 collective-permute-start.3
  6.3 0.1 pack_own.1
  6.5 4.4 %collective-permute-start = (bf16[28,8,512]{2,1,0:T(8,128)(2,1)S(1)}, bf16[28,8,512]{2,1,0:T(8,128)(2,1)S(1)}, u32[]{:S(2)}, u32[]{:S(2)}) collective-permute-start(bf16[28,8,512]{2,1,0:T(8,128)(2,1)S(1)} %get-tuple-element.60), channel_id=1, source_target_pairs={{1,2},{2,1},{3,4},{4,3},{5,6},{6,5},{9,10},{10,9},{11,12},{12,11},... | collective-permute-start | bytes 688136 | tf_op jit(solution)/shard_map/ppermute | solution.py:581
  10.9 0.1 collective-permute-start.1
  10.9 1.1 %matrices.1 = (bf16[192,384]{1,0:T(8,128)(2,1)S(1)}, bf16[192,32]{1,0:T(8,128)(2,1)S(1)}, f32[8,128]{1,0:T(8,128)S(1)}, bf16[96,384]{1,0:T(8,128)(2,1)S(1)}, bf1...) custom-call(bf16[24,24]{1,0:T(8,128)(2,1)S(1)} %get-tuple-element.45, ...), custom_call_target="tpu_custom_call" | custom-call | tf_op jit(solution)/shard_map/matrices/pallas_call | solution.py:632
  12.0 0.0 collective-permute-done.2.refs_1_.refs_19_
  12.0 0.0 collective-permute-done.3.refs_2_.refs_20_
  12.0 0.2 pack_far.1
  12.2 5.2 %collective-permute-start.4 = (bf16[25,8,512]{2,1,0:T(8,128)(2,1)S(1)}, bf16[25,8,512]{2,1,0:T(8,128)(2,1)S(1)}, u32[]{:S(2)}, u32[]{:S(2)}) collective-permute-start(bf16[25,8,512]{2,1,0:T(8,128)(2,1)S(1)} %get-tuple-element.76), channel_id=1, source_target_pairs={{1,2},{2,1},{3,4},{4,3},{5,6},{6,5},{9,10},{10,9},{11,12},{12,11},... | collective-permute-start | bytes 614408 | tf_op jit(solution)/shard_map/ppermute | solution.py:581
  17.4 0.1 collective-permute-start.5
  17.5 0.0 collective-permute-done.refs_8_
  17.5 0.0 collective-permute-done.1.refs_9_
  17.6 3.1 %fine_own.1 = (bf16[8,96,512]{2,1,0:T(8,128)(2,1)S(1)}, bf16[8,96,512]{2,1,0:T(8,128)(2,1)S(1)}, bf16[8,96,512]{2,1,0:T(8,128)(2,1)S(1)}, bf16[8,96,512]{2,1,0:T...) custom-call(bf16[192,384]{1,0:T(8,128)(2,1)S(1)} %get-tuple-element., ...), custom_call_target="tpu_custom_call" | custom-call | tf_op jit(solution)/shard_map/fine_own/pallas_call | solution.py:659
  20.7 0.2 collective-permute-done.4.refs_21_
  20.9 0.0 collective-permute-done.5.refs_22_
  20.9 4.5 %fine_rest.1 = (f32[3,8,8,512]{3,2,1,0:T(8,128)S(1)}, f32[15,8,256]{2,1,0:T(8,128)S(1)}, bf16[12,8,256]{2,1,0:T(8,128)(2,1)S(1)}, bf16[12,8,256]{2,1,0:T(8,128)(2,1)S(1)}) custom-call(bf16[192,384]{1,0:T(8,128)(2,1)S(1)} %get-tuple-element.50.refs_0_, bf16[192,32]{1,0:T(8,128)(2,1)S(1)} %get-tuple-element.51.refs_1_, ...), custom_call_target="tpu_custom_call" | custom-call | tf_op jit(solution)/shard_map/fine_rest/pallas_call | solution.py:667
  25.4 3.9 %collective-permute-start.6 = (bf16[12,8,256]{2,1,0:T(8,128)(2,1)S(1)}, bf16[12,8,256]{2,1,0:T(8,128)(2,1)S(1)}, u32[]{:S(2)}, u32[]{:S(2)}) collective-permute-start(bf16[12,8,256]{2,1,0:T(8,128)(2,1)S(1)} %get-tuple-element.79), channel_id=1, source_target_pairs={{8,16},{16,8},{24,32},{32,24},{40,48},{48,40},{56,64},{64,56},{72,... | collective-permute-start | bytes 147464 | tf_op jit(solution)/shard_map/ppermute | solution.py:581
  29.3 0.1 collective-permute-start.7
  29.4 2.9 %collective-permute-done.6.refs_2_ = bf16[12,8,256]{2,1,0:T(8,128)(2,1)S(1)} collective-permute-done((bf16[12,8,256]{2,1,0:T(8,128)(2,1)S(1)}, bf16[12,8,256]{2,1,0:T(8,128)(2,1)S(1)}, u32[]{:S(2)}, u32[]{:S(2)}) %collective-permute-start.6) | collective-permute-done | bytes 49184 | tf_op jit(solution)/shard_map/ppermute | solution.py:581
  32.3 0.3 collective-permute-done.7.refs_3_
  32.6 0.1 pack_coarse.1
  32.7 4.9 %collective-permute-start.8 = (bf16[20,8,256]{2,1,0:T(8,128)(2,1)S(1)}, bf16[20,8,256]{2,1,0:T(8,128)(2,1)S(1)}, u32[]{:S(2)}, u32[]{:S(2)}) collective-permute-start(bf16[20,8,256]{2,1,0:T(8,128)(2,1)S(1)} %get-tuple-element.82), channel_id=1, source_target_pairs={{1,2},{2,1},{3,4},{4,3},{5,6},{6,5},{9,10},{10,9},{11,12},{12,11},... | collective-permute-start | bytes 245768 | tf_op jit(solution)/shard_map/ppermute | solution.py:581
  37.6 0.1 collective-permute-start.9
  37.7 2.0 %collective-permute-done.8.refs_6_ = bf16[20,8,256]{2,1,0:T(8,128)(2,1)S(1)} collective-permute-done((bf16[20,8,256]{2,1,0:T(8,128)(2,1)S(1)}, bf16[20,8,256]{2,1,0:T(8,128)(2,1)S(1)}, u32[]{:S(2)}, u32[]{:S(2)}) %collective-permute-start.8) | collective-permute-done | bytes 81952 | tf_op jit(solution)/shard_map/ppermute | solution.py:581
  39.7 0.0 collective-permute-done.9.refs_7_
  39.7 2.9 %coarse.1 = f32[3,8,8,512]{3,2,1,0:T(8,128)} custom-call(bf16[192,384]{1,0:T(8,128)(2,1)S(1)} %get-tuple-element.50.refs_0_, bf16[192,32]{1,0:T(8,128)(2,1)S(1)} %get-tuple-element.51.refs_1_, f32[8,128]{1,0:T(8,128)S(1)} %get-tuple-element.52.refs_2_.refs_0_, bf16[120,240]{1,0:T(8,128)(2,1)S(1)} %get-tuple-element.53.refs_3_, ...), custom_call_target="tpu_custom_call" | custom-call | tf_op jit(solution)/shard_map/coarse/pallas_call | solution.py:686
Async XLA Ops:
  1.3 10.7 %collective-permute-start.2 = (bf16[25,8,512]{2,1,0:T(8,128)(2,1)S(1)}, bf16[25,8,512]{2,1,0:T(8,128)(2,1)S(1)}, u32[]{:S(2)}, u32[]{:S(2)}) collective-permute-start(bf16[25,8,512]{2,1,0:T(8,128)(2,1)S(1)} %get-tuple-element.74), channel_id=1, source_target_pairs={{8,16},{16,8},{24,32},{32,24},{40,48},{48,40},{56,64},{64,56},{72,... | collective-permute-start | bytes 614408 | tf_op jit(solution)/shard_map/ppermute | solution.py:581
  6.2 5.8 %collective-permute-start.3 = (bf16[25,8,512]{2,1,0:T(8,128)(2,1)S(1)}, bf16[25,8,512]{2,1,0:T(8,128)(2,1)S(1)}, u32[]{:S(2)}, u32[]{:S(2)}) collective-permute-start(bf16[25,8,512]{2,1,0:T(8,128)(2,1)S(1)} %get-tuple-element.75), channel_id=1, source_target_pairs={{0,8},{8,0},{16,24},{24,16},{32,40},{40,32},{48,56},{56,48},{64,72... | collective-permute-start | bytes 614408 | tf_op jit(solution)/shard_map/ppermute | solution.py:581
  6.5 11.1 %collective-permute-start = (bf16[28,8,512]{2,1,0:T(8,128)(2,1)S(1)}, bf16[28,8,512]{2,1,0:T(8,128)(2,1)S(1)}, u32[]{:S(2)}, u32[]{:S(2)}) collective-permute-start(bf16[28,8,512]{2,1,0:T(8,128)(2,1)S(1)} %get-tuple-element.60), channel_id=1, source_target_pairs={{1,2},{2,1},{3,4},{4,3},{5,6},{6,5},{9,10},{10,9},{11,12},{12,11},... | collective-permute-start | bytes 688136 | tf_op jit(solution)/shard_map/ppermute | solution.py:581
  10.9 6.7 %collective-permute-start.1 = (bf16[28,8,512]{2,1,0:T(8,128)(2,1)S(1)}, bf16[28,8,512]{2,1,0:T(8,128)(2,1)S(1)}, u32[]{:S(2)}, u32[]{:S(2)}) collective-permute-start(bf16[28,8,512]{2,1,0:T(8,128)(2,1)S(1)} %get-tuple-element.61), channel_id=1, source_target_pairs={{0,1},{1,0},{2,3},{3,2},{4,5},{5,4},{6,7},{7,6},{8,9},{9,8},{10,11... | collective-permute-start | bytes 688136 | tf_op jit(solution)/shard_map/ppermute | solution.py:581
  12.2 8.6 %collective-permute-start.4 = (bf16[25,8,512]{2,1,0:T(8,128)(2,1)S(1)}, bf16[25,8,512]{2,1,0:T(8,128)(2,1)S(1)}, u32[]{:S(2)}, u32[]{:S(2)}) collective-permute-start(bf16[25,8,512]{2,1,0:T(8,128)(2,1)S(1)} %get-tuple-element.76), channel_id=1, source_target_pairs={{1,2},{2,1},{3,4},{4,3},{5,6},{6,5},{9,10},{10,9},{11,12},{12,11},... | collective-permute-start | bytes 614408 | tf_op jit(solution)/shard_map/ppermute | solution.py:581
  17.4 3.4 %collective-permute-start.5 = (bf16[25,8,512]{2,1,0:T(8,128)(2,1)S(1)}, bf16[25,8,512]{2,1,0:T(8,128)(2,1)S(1)}, u32[]{:S(2)}, u32[]{:S(2)}) collective-permute-start(bf16[25,8,512]{2,1,0:T(8,128)(2,1)S(1)} %get-tuple-element.77), channel_id=1, source_target_pairs={{0,1},{1,0},{2,3},{3,2},{4,5},{5,4},{6,7},{7,6},{8,9},{9,8},{10,11... | collective-permute-start | bytes 614408 | tf_op jit(solution)/shard_map/ppermute | solution.py:581
  25.4 6.9 %collective-permute-start.6 = (bf16[12,8,256]{2,1,0:T(8,128)(2,1)S(1)}, bf16[12,8,256]{2,1,0:T(8,128)(2,1)S(1)}, u32[]{:S(2)}, u32[]{:S(2)}) collective-permute-start(bf16[12,8,256]{2,1,0:T(8,128)(2,1)S(1)} %get-tuple-element.79), channel_id=1, source_target_pairs={{8,16},{16,8},{24,32},{32,24},{40,48},{48,40},{56,64},{64,56},{72,... | collective-permute-start | bytes 147464 | tf_op jit(solution)/shard_map/ppermute | solution.py:581
  29.3 3.3 %collective-permute-start.7 = (bf16[12,8,256]{2,1,0:T(8,128)(2,1)S(1)}, bf16[12,8,256]{2,1,0:T(8,128)(2,1)S(1)}, u32[]{:S(2)}, u32[]{:S(2)}) collective-permute-start(bf16[12,8,256]{2,1,0:T(8,128)(2,1)S(1)} %get-tuple-element.80), channel_id=1, source_target_pairs={{0,8},{8,0},{16,24},{24,16},{32,40},{40,32},{48,56},{56,48},{64,72... | collective-permute-start | bytes 147464 | tf_op jit(solution)/shard_map/ppermute | solution.py:581
  32.7 7.0 %collective-permute-start.8 = (bf16[20,8,256]{2,1,0:T(8,128)(2,1)S(1)}, bf16[20,8,256]{2,1,0:T(8,128)(2,1)S(1)}, u32[]{:S(2)}, u32[]{:S(2)}) collective-permute-start(bf16[20,8,256]{2,1,0:T(8,128)(2,1)S(1)} %get-tuple-element.82), channel_id=1, source_target_pairs={{1,2},{2,1},{3,4},{4,3},{5,6},{6,5},{9,10},{10,9},{11,12},{12,11},... | collective-permute-start | bytes 245768 | tf_op jit(solution)/shard_map/ppermute | solution.py:581
  37.6 2.1 %collective-permute-start.9 = (bf16[20,8,256]{2,1,0:T(8,128)(2,1)S(1)}, bf16[20,8,256]{2,1,0:T(8,128)(2,1)S(1)}, u32[]{:S(2)}, u32[]{:S(2)}) collective-permute-start(bf16[20,8,256]{2,1,0:T(8,128)(2,1)S(1)} %get-tuple-element.83), channel_id=1, source_target_pairs={{0,1},{1,0},{2,3},{3,2},{4,5},{5,4},{6,7},{7,6},{8,9},{9,8},{10,11... | collective-permute-start | bytes 245768 | tf_op jit(solution)/shard_map/ppermute | solution.py:581
